TPU v7x, 32 devices: a whole 2x2x4 slice. The times are simulated.
32 devices in a mesh: row: 8 (over z, core), col: 4 (over y, x).
Axes of the slice: x: 2, y: 2, z: 4, core: 2. Of those that a mesh axis runs over, the one named last changes fastest.
Arguments:
- local_gap: bfloat16 [8, 4, 112, 4, 224], P('row', 'col')
- dual_ops: bfloat16 [8, 4, 896, 896], P('row', 'col'), as said below
- geneo_modes: bfloat16 [8, 4, 128, 896], P('row', 'col'), may hold values from -0.1875 to 0.1875
- coarse_inverse: float32 [8, 512, 512], P('row', 'col'), as said below
- face_rows: int32 [8, 4, 4], P('row', 'col'), may hold values from 0 to 224, as said below
Outputs:
- solution: float32 [8, 4, 112, 4, 224], P('row', 'col')
Inputs may be any that keep to these rules, and one draw needn't show every extreme that they name: face_rows[i, j, f] counts the live dual rows of face f (north, south, west, east) of subdomain (i, j); faces on the outer edge of the grid have 0, every other face 224 // 2 or more; the two subdomains sharing a face give it the same count; some face has 224. `dual_ops`: each subdomain's dual operator is symmetric positive definite. `coarse_inverse`: each strip's coarse inverse is exactly symmetric.
All inputs are finite; a program needn't handle non-finite values.
Results may differ from a plain program's by a relative error of at most 0.003.
Values sent between devices are 32-bit elements; how exact they have to be, the bound alone decides.
No kernel may reach another device: no remote copies, remote signals or barrier semaphores. Data moves between devices by JAX's collectives and lax.ppermute only.
A program may use at most 64 MiB of HBM per device.

v0:
```python
import jax
import jax.numpy as jnp
from jax import lax
from jax.sharding import PartitionSpec as P

ITERS = 2


face_sign_values = (-1.0, 1.0, -1.0, 1.0)


def padded(cells, sides, width):
    for axis, dim in sides:
        count = lax.axis_size(axis)
        ends = count - 1
        head = lax.slice_in_dim(cells, 0, width, axis=dim)
        tail = lax.slice_in_dim(cells, cells.shape[dim] - width, cells.shape[dim], axis=dim)
        cells = jnp.concatenate(
            [
                lax.ppermute(tail, axis, [(i, (i + 1) % count) for i in range(ends)]),
                cells,
                lax.ppermute(head, axis, [((i + 1) % count, i) for i in range(ends)]),
            ],
            axis=dim,
        )
    return cells


def sign_array():
    return jnp.array(face_sign_values, jnp.float32).reshape(1, 4, 1)


def glue_faces(local_part, live_mask):
    vertical = padded(local_part[:, 0:2], (("row", 1),), 1)
    across = padded(local_part[:, 2:4], (("col", 1),), 1)
    north_face = local_part[:, 0] + vertical[:, 0]
    south_face = local_part[:, 1] + vertical[:, 3]
    west_face = local_part[:, 2] + across[:, 0]
    east_face = local_part[:, 3] + across[:, 3]
    return jnp.stack([north_face, south_face, west_face, east_face], axis=1) * live_mask


def signed_dual(vector, operator):
    signed = (vector * sign_array()).astype(jnp.bfloat16).reshape(vector.shape[0], -1)
    image = jnp.dot(signed, operator, preferred_element_type=jnp.float32)
    return image.reshape(vector.shape) * sign_array()


def total_over(partial_value):
    return lax.psum(partial_value, ("row", "col"))


def project(vector, modes, coarse_block, live_mask):
    rounded = vector.astype(jnp.bfloat16).reshape(vector.shape[0], -1)
    mode_coeffs = lax.dot_general(
        modes, rounded, (((1,), (1,)), ((), ())), preferred_element_type=jnp.float32
    )
    coarse_values = jnp.dot(
        coarse_block,
        lax.all_gather(mode_coeffs, "col", axis=0, tiled=True),
        precision=lax.Precision.HIGHEST,
        preferred_element_type=jnp.float32,
    )
    spread = lax.dot_general(
        coarse_values.astype(jnp.bfloat16),
        modes,
        (((0,), (0,)), ((), ())),
        preferred_element_type=jnp.float32,
    )
    return vector - glue_faces(spread.reshape(vector.shape), live_mask)


def on_device(local_gap, dual_ops, geneo_modes, coarse_inverse, face_rows):
    operator = dual_ops[0, 0]
    modes = geneo_modes[0, 0]
    coarse_block = coarse_inverse[0]
    rows_iota = lax.broadcasted_iota(jnp.int32, (1, 4, local_gap.shape[4]), 2)
    live_mask = (rows_iota < face_rows[0, 0][None, :, None]).astype(jnp.float32)
    residual = glue_faces(local_gap[0, 0].astype(jnp.float32) * sign_array(), live_mask)
    projected = project(residual, modes, coarse_block, live_mask)
    norm_now = total_over(0.5 * jnp.sum(projected * projected, axis=(1, 2)))
    direction = projected
    solution = jnp.zeros_like(residual)
    for iteration in range(ITERS):
        signed_image = signed_dual(direction, operator)
        curvature = total_over(jnp.sum(direction * signed_image, axis=(1, 2)))
        image = glue_faces(signed_image, live_mask)
        step_size = (norm_now / curvature).reshape(-1, 1, 1)
        solution = solution + step_size * direction
        if iteration + 1 < ITERS:
            residual = residual - step_size * image
            projected = project(residual, modes, coarse_block, live_mask)
            norm_next = total_over(0.5 * jnp.sum(projected * projected, axis=(1, 2)))
            direction = projected + (norm_next / norm_now).reshape(-1, 1, 1) * direction
            norm_now = norm_next
    return solution[None, None]


def solution(mesh):
    return jax.shard_map(
        on_device,
        mesh=mesh,
        in_specs=(
            P("row", "col", None, None, None),
            P("row", "col", None, None),
            P("row", "col", None, None),
            P("row", "col", None),
            P("row", "col", None),
        ),
        out_specs=P("row", "col", None, None, None),
        check_vma=False,
    )
```

profile of v0, /device:TPU:0, one launch (start us, length us, event | category | flops | bytes accessed | tf_op | source)
XLA Modules:
  0.0 217.1 jit_solution(14358309013559164214)
XLA Ops:
  0.0 1.1 convert_multiply_fusion
  1.2 2.4 %collective-permute-start = (f32[112,1,224]{2,0,1:T(8,128)S(1)}, f32[112,1,224]{2,0,1:T(8,128)S(1)}, u32[]{:S(2)}, u32[]{:S(2)}) collective-permute-start(f32[112,1,224]{2,0,1:T(8,128)S(1)} %get-tuple-element.43), channel_id=1, source_target_pairs={{0,4},{4,8},{8,12},{12,16},{16,20},{20,24},{24,28},{1,5},{5,9},{9,... | collective-permute-start | bytes 301064 | tf_op jit(solution)/shard_map/ppermute | solution.py:20
  3.6 4.2 %collective-permute-start.2 = (f32[112,1,224]{2,0,1:T(8,128)S(1)}, f32[112,1,224]{2,0,1:T(8,128)S(1)}, u32[]{:S(2)}, u32[]{:S(2)}) collective-permute-start(f32[112,1,224]{2,0,1:T(8,128)S(1)} %get-tuple-element.44), channel_id=1, source_target_pairs={{0,1},{1,2},{2,3},{4,5},{5,6},{6,7},{8,9},{9,10},{10,11},{12,13},{... | collective-permute-start | bytes 301064 | tf_op jit(solution)/shard_map/ppermute | solution.py:20
  7.8 1.3 collective-permute-start.3
  9.1 1.3 collective-permute-start.1
  10.7 4.4 %collective-permute-done.3 = f32[112,1,224]{2,0,1:T(8,128)S(1)} collective-permute-done((f32[112,1,224]{2,0,1:T(8,128)S(1)}, f32[112,1,224]{2,0,1:T(8,128)S(1)}, u32[]{:S(2)}, u32[]{:S(2)}) %collective-permute-start.3) | collective-permute-done | bytes 100384 | tf_op jit(solution)/shard_map/ppermute | solution.py:22
  15.6 0.2 convolution_bitcast_fusion.1
  15.8 10.8 %all_gather.6 = f32[512,112]{0,1:T(8,128)S(1)} all-gather(f32[128,112]{0,1:T(8,128)S(1)} %convolution_bitcast_fusion.1), channel_id=1, replica_groups=mesh['row'=8,'col'=4] {'col'}, dimensions={0}, use_global_device_ids=true | all-gather | bytes 286720 | tf_op jit(solution)/shard_map/all_gather | solution.py:60
  26.6 0.4 fusion.2
  27.0 0.3 fusion.29
  27.3 3.4 %collective-permute-start.4 = (f32[112,1,224]{2,0,1:T(8,128)S(1)}, f32[112,1,224]{2,0,1:T(8,128)}, u32[]{:S(2)}, u32[]{:S(2)}) collective-permute-start(f32[112,1,224]{2,0,1:T(8,128)S(1)} %get-tuple-element.35), channel_id=1, source_target_pairs={{0,4},{4,8},{8,12},{12,16},{16,20},{20,24},{24,28},{1,5},{5,9},{9,... | collective-permute-start | bytes 301064 | tf_op jit(solution)/shard_map/ppermute | solution.py:20
  30.7 2.7 %collective-permute-start.6 = (f32[112,1,224]{2,0,1:T(8,128)S(1)}, f32[112,1,224]{2,0,1:T(8,128)}, u32[]{:S(2)}, u32[]{:S(2)}) collective-permute-start(f32[112,1,224]{2,0,1:T(8,128)S(1)} %get-tuple-element.36), channel_id=1, source_target_pairs={{0,1},{1,2},{2,3},{4,5},{5,6},{6,7},{8,9},{9,10},{10,11},{12,13},{... | collective-permute-start | bytes 301064 | tf_op jit(solution)/shard_map/ppermute | solution.py:20
  33.4 1.3 collective-permute-start.7
  34.7 1.3 collective-permute-start.5
  36.0 2.9 %copy.21 = bf16[1,1,896,896]{2,3,1,0:T(8,128)(2,1)S(1)} copy(bf16[1,1,896,896]{3,2,1,0:T(8,128)(2,1)} %param.11) | data formatting | bytes 3211264 | tf_op args[1]
  38.9 1.2 collective-permute-done.7
  40.2 1.1 slice_add_fusion.11
  41.3 0.6 copy-done.5
  42.2 0.9 reshape.675
  43.1 1.8 multiply_reduce_fusion.1
  44.9 0.8 fusion.26
  45.7 5.5 %collective-permute-start.8 = (f32[112,1,224]{2,0,1:T(8,128)}, f32[112,1,224]{2,0,1:T(8,128)}, u32[]{:S(2)}, u32[]{:S(2)}) collective-permute-start(f32[112,1,224]{2,0,1:T(8,128)} %get-tuple-element.27), channel_id=1, source_target_pairs={{0,4},{4,8},{8,12},{12,16},{16,20},{20,24},{24,28},{1,5},{5,9},{9,... | collective-permute-start | bytes 301064 | tf_op jit(solution)/shard_map/ppermute | solution.py:20
  51.1 4.9 %collective-permute-start.10 = (f32[112,1,224]{2,0,1:T(8,128)}, f32[112,1,224]{2,0,1:T(8,128)}, u32[]{:S(2)}, u32[]{:S(2)}) collective-permute-start(f32[112,1,224]{2,0,1:T(8,128)} %get-tuple-element.28), channel_id=1, source_target_pairs={{0,1},{1,2},{2,3},{4,5},{5,6},{6,7},{8,9},{9,10},{10,11},{12,13},{... | collective-permute-start | bytes 301064 | tf_op jit(solution)/shard_map/ppermute | solution.py:20
  56.0 1.3 collective-permute-start.11
  57.3 1.3 collective-permute-start.9
  58.6 41.5 %all-reduce = (f32[112]{0:T(128)S(1)}, f32[112]{0:T(128)S(1)}) all-reduce(f32[112]{0:T(128)S(1)} %broadcast_multiply_fusion.1, f32[112]{0:T(128)S(1)} %get-tuple-element.5), channel_id=1, replica_groups=mesh['row'=8,'col'=4] {'row','col'}, use_global_device_ids=true, to_apply=%region_1.0 | all-reduce | flops 224 | bytes 1792 | tf_op jit(solution)/shard_map/psum | solution.py:50
  100.2 1.1 slice_add_fusion.7
  101.3 0.6 copy-done.11
  101.9 0.9 fusion.22
  103.0 0.9 convert_element_type.83
  103.9 1.1 convolution_bitcast_fusion
  105.0 10.5 %all_gather.7 = f32[512,112]{0,1:T(8,128)S(1)} all-gather(f32[128,112]{0,1:T(8,128)S(1)} %convolution_bitcast_fusion), channel_id=1, replica_groups=mesh['row'=8,'col'=4] {'col'}, dimensions={0}, use_global_device_ids=true | all-gather | bytes 286720 | tf_op jit(solution)/shard_map/all_gather | solution.py:60
  115.5 0.4 fusion.3
  115.9 0.3 fusion.30
  116.3 1.3 collective-permute-start.12
  117.6 2.9 %collective-permute-start.14 = (f32[112,1,224]{2,0,1:T(8,128)S(1)}, f32[112,1,224]{2,0,1:T(8,128)S(1)}, u32[]{:S(2)}, u32[]{:S(2)}) collective-permute-start(f32[112,1,224]{2,0,1:T(8,128)S(1)} %get-tuple-element.20), channel_id=1, source_target_pairs={{0,1},{1,2},{2,3},{4,5},{5,6},{6,7},{8,9},{9,10},{10,11},{12,13},{... | collective-permute-start | bytes 301064 | tf_op jit(solution)/shard_map/ppermute | solution.py:20
  120.5 1.3 collective-permute-start.15
  121.8 1.3 collective-permute-start.13
  123.1 0.7 collective-permute-done.14
  123.8 4.6 %collective-permute-done.15 = f32[112,1,224]{2,0,1:T(8,128)S(1)} collective-permute-done((f32[112,1,224]{2,0,1:T(8,128)S(1)}, f32[112,1,224]{2,0,1:T(8,128)S(1)}, u32[]{:S(2)}, u32[]{:S(2)}) %collective-permute-start.15) | collective-permute-done | bytes 100384 | tf_op jit(solution)/shard_map/ppermute | solution.py:22
  128.7 0.4 copy-done.15
  129.2 40.8 %psum.30 = f32[112]{0:T(128)S(1)} all-reduce(f32[112]{0:T(128)S(1)} %broadcast_multiply_fusion), channel_id=1, replica_groups=mesh['row'=8,'col'=4] {'row','col'}, use_global_device_ids=true, to_apply=%region_5.0 | all-reduce | flops 112 | bytes 896 | tf_op jit(solution)/shard_map/psum | solution.py:50
  170.2 0.8 copy.23
  171.0 1.9 reshape.677
  172.9 1.8 fusion.1
  174.7 39.8 %psum.31 = f32[112]{0:T(128)S(1)} all-reduce(f32[112]{0:T(128)S(1)} %fusion.1), channel_id=1, replica_groups=mesh['row'=8,'col'=4] {'row','col'}, use_global_device_ids=true, to_apply=%region_7.0 | all-reduce | flops 112 | bytes 896 | tf_op jit(solution)/shard_map/psum | solution.py:50
  214.4 1.6 fusion.14
  216.1 1.1 copy.24
  (71 shorter events, 1.7 us)
Async XLA Ops:
  0.0 26.6 %copy-start = (f32[1,128,512]{2,1,0:T(8,128)S(1)}, f32[1,128,512]{2,1,0:T(8,128)}, u32[]{:S(2)}) copy-start(f32[1,128,512]{2,1,0:T(8,128)} %param.13) | copy-start | bytes 786436
  0.0 10.4 %copy-start.20 = (s32[1,1,4]{2,1,0:T(1,128)S(1)}, s32[1,1,4]{2,1,0:T(1,128)}, u32[]{:S(2)}) copy-start(s32[1,1,4]{2,1,0:T(1,128)} %param.14) | copy-start | bytes 52
  0.0 10.5 %copy-start.1 = (bf16[1,1,128,896]{3,2,1,0:T(8,128)(2,1)S(1)}, bf16[1,1,128,896]{3,2,1,0:T(8,128)(2,1)}, u32[]{:S(2)}) copy-start(bf16[1,1,128,896]{3,2,1,0:T(8,128)(2,1)} %param.12) | copy-start | bytes 688132
  1.2 9.5 %collective-permute-start = (f32[112,1,224]{2,0,1:T(8,128)S(1)}, f32[112,1,224]{2,0,1:T(8,128)S(1)}, u32[]{:S(2)}, u32[]{:S(2)}) collective-permute-start(f32[112,1,224]{2,0,1:T(8,128)S(1)} %get-tuple-element.43), channel_id=1, source_target_pairs={{0,4},{4,8},{8,12},{12,16},{16,20},{20,24},{24,28},{1,5},{5,9},{9,... | collective-permute-start | bytes 301064 | tf_op jit(solution)/shard_map/ppermute | solution.py:20
  3.6 7.1 %collective-permute-start.2 = (f32[112,1,224]{2,0,1:T(8,128)S(1)}, f32[112,1,224]{2,0,1:T(8,128)S(1)}, u32[]{:S(2)}, u32[]{:S(2)}) collective-permute-start(f32[112,1,224]{2,0,1:T(8,128)S(1)} %get-tuple-element.44), channel_id=1, source_target_pairs={{0,1},{1,2},{2,3},{4,5},{5,6},{6,7},{8,9},{9,10},{10,11},{12,13},{... | collective-permute-start | bytes 301064 | tf_op jit(solution)/shard_map/ppermute | solution.py:20
  7.8 7.3 %collective-permute-start.3 = (f32[112,1,224]{2,0,1:T(8,128)S(1)}, f32[112,1,224]{2,0,1:T(8,128)S(1)}, u32[]{:S(2)}, u32[]{:S(2)}) collective-permute-start(f32[112,1,224]{2,0,1:T(8,128)S(1)} %get-tuple-element.45), channel_id=1, source_target_pairs={{1,0},{2,1},{3,2},{5,4},{6,5},{7,6},{9,8},{10,9},{11,10},{13,12},{... | collective-permute-start | bytes 301064 | tf_op jit(solution)/shard_map/ppermute | solution.py:22
  9.1 6.0 %collective-permute-start.1 = (f32[112,1,224]{2,0,1:T(8,128)S(1)}, f32[112,1,224]{2,0,1:T(8,128)S(1)}, u32[]{:S(2)}, u32[]{:S(2)}) collective-permute-start(f32[112,1,224]{2,0,1:T(8,128)S(1)} %get-tuple-element.46), channel_id=1, source_target_pairs={{4,0},{8,4},{12,8},{16,12},{20,16},{24,20},{28,24},{5,1},{9,5},{13... | collective-permute-start | bytes 301064 | tf_op jit(solution)/shard_map/ppermute | solution.py:22
  10.7 16.3 %copy-start.2 = (bf16[1,1,128,896]{2,3,1,0:T(8,128)(2,1)}, bf16[1,1,128,896]{2,3,1,0:T(8,128)(2,1)S(1)}, u32[]{:S(2)}) copy-start(bf16[1,1,128,896]{2,3,1,0:T(8,128)(2,1)S(1)} %copy.19) | copy-start | bytes 688132
  27.3 11.6 %collective-permute-start.4 = (f32[112,1,224]{2,0,1:T(8,128)S(1)}, f32[112,1,224]{2,0,1:T(8,128)}, u32[]{:S(2)}, u32[]{:S(2)}) collective-permute-start(f32[112,1,224]{2,0,1:T(8,128)S(1)} %get-tuple-element.35), channel_id=1, source_target_pairs={{0,4},{4,8},{8,12},{12,16},{16,20},{20,24},{24,28},{1,5},{5,9},{9,... | collective-permute-start | bytes 301064 | tf_op jit(solution)/shard_map/ppermute | solution.py:20
  30.7 8.2 %collective-permute-start.6 = (f32[112,1,224]{2,0,1:T(8,128)S(1)}, f32[112,1,224]{2,0,1:T(8,128)}, u32[]{:S(2)}, u32[]{:S(2)}) collective-permute-start(f32[112,1,224]{2,0,1:T(8,128)S(1)} %get-tuple-element.36), channel_id=1, source_target_pairs={{0,1},{1,2},{2,3},{4,5},{5,6},{6,7},{8,9},{9,10},{10,11},{12,13},{... | collective-permute-start | bytes 301064 | tf_op jit(solution)/shard_map/ppermute | solution.py:20
  33.4 6.8 %collective-permute-start.7 = (f32[112,1,224]{2,0,1:T(8,128)S(1)}, f32[112,1,224]{2,0,1:T(8,128)}, u32[]{:S(2)}, u32[]{:S(2)}) collective-permute-start(f32[112,1,224]{2,0,1:T(8,128)S(1)} %get-tuple-element.37), channel_id=1, source_target_pairs={{1,0},{2,1},{3,2},{5,4},{6,5},{7,6},{9,8},{10,9},{11,10},{13,12},{... | collective-permute-start | bytes 301064 | tf_op jit(solution)/shard_map/ppermute | solution.py:22
  34.7 7.3 %copy-start.19 = (f32[4]{0:T(128)S(1)}, f32[4]{0:T(128)}, u32[]{:S(2)}) copy-start(f32[4]{0:T(128)} %constant.6.clone) | copy-start | bytes 52
  34.7 5.5 %collective-permute-start.5 = (f32[112,1,224]{2,0,1:T(8,128)S(1)}, f32[112,1,224]{2,0,1:T(8,128)}, u32[]{:S(2)}, u32[]{:S(2)}) collective-permute-start(f32[112,1,224]{2,0,1:T(8,128)S(1)} %get-tuple-element.38), channel_id=1, source_target_pairs={{4,0},{8,4},{12,8},{16,12},{20,16},{24,20},{28,24},{5,1},{9,5},{13... | collective-permute-start | bytes 301064 | tf_op jit(solution)/shard_map/ppermute | solution.py:22
  41.3 0.6 copy-start.5
  41.3 0.8 copy-start.7
  41.3 0.8 copy-start.9
  41.3 0.8 copy-start.10
  45.7 54.5 %collective-permute-start.8 = (f32[112,1,224]{2,0,1:T(8,128)}, f32[112,1,224]{2,0,1:T(8,128)}, u32[]{:S(2)}, u32[]{:S(2)}) collective-permute-start(f32[112,1,224]{2,0,1:T(8,128)} %get-tuple-element.27), channel_id=1, source_target_pairs={{0,4},{4,8},{8,12},{12,16},{16,20},{20,24},{24,28},{1,5},{5,9},{9,... | collective-permute-start | bytes 301064 | tf_op jit(solution)/shard_map/ppermute | solution.py:20
  51.1 49.0 %collective-permute-start.10 = (f32[112,1,224]{2,0,1:T(8,128)}, f32[112,1,224]{2,0,1:T(8,128)}, u32[]{:S(2)}, u32[]{:S(2)}) collective-permute-start(f32[112,1,224]{2,0,1:T(8,128)} %get-tuple-element.28), channel_id=1, source_target_pairs={{0,1},{1,2},{2,3},{4,5},{5,6},{6,7},{8,9},{9,10},{10,11},{12,13},{... | collective-permute-start | bytes 301064 | tf_op jit(solution)/shard_map/ppermute | solution.py:20
  56.0 44.1 %collective-permute-start.11 = (f32[112,1,224]{2,0,1:T(8,128)}, f32[112,1,224]{2,0,1:T(8,128)}, u32[]{:S(2)}, u32[]{:S(2)}) collective-permute-start(f32[112,1,224]{2,0,1:T(8,128)} %get-tuple-element.29), channel_id=1, source_target_pairs={{1,0},{2,1},{3,2},{5,4},{6,5},{7,6},{9,8},{10,9},{11,10},{13,12},{... | collective-permute-start | bytes 301064 | tf_op jit(solution)/shard_map/ppermute | solution.py:22
  57.3 42.9 %collective-permute-start.9 = (f32[112,1,224]{2,0,1:T(8,128)}, f32[112,1,224]{2,0,1:T(8,128)}, u32[]{:S(2)}, u32[]{:S(2)}) collective-permute-start(f32[112,1,224]{2,0,1:T(8,128)} %get-tuple-element.30), channel_id=1, source_target_pairs={{4,0},{8,4},{12,8},{16,12},{20,16},{24,20},{28,24},{5,1},{9,5},{13... | collective-permute-start | bytes 301064 | tf_op jit(solution)/shard_map/ppermute | solution.py:22
  101.3 0.6 copy-start.11
  101.3 1.5 copy-start.12
  101.3 1.5 copy-start.13
  101.3 1.5 copy-start.14
  101.9 14.0 %copy-start.3 = (bf16[1,1,128,896]{2,3,1,0:T(8,128)(2,1)S(1)}, bf16[1,1,128,896]{2,3,1,0:T(8,128)(2,1)}, u32[]{:S(2)}) copy-start(bf16[1,1,128,896]{2,3,1,0:T(8,128)(2,1)} %copy-done.2) | copy-start | bytes 688132
  115.9 12.6 %copy-start.4 = (f32[112,4,224]{2,0,1:T(8,128)S(1)}, f32[112,4,224]{2,0,1:T(8,128)}, u32[]{:S(2)}) copy-start(f32[112,4,224]{2,0,1:T(8,128)} %get-tuple-element.12) | copy-start | bytes 1204228
  116.3 6.9 %collective-permute-start.12 = (f32[112,1,224]{2,0,1:T(8,128)S(1)}, f32[112,1,224]{2,0,1:T(8,128)S(1)}, u32[]{:S(2)}, u32[]{:S(2)}) collective-permute-start(f32[112,1,224]{2,0,1:T(8,128)S(1)} %get-tuple-element.19), channel_id=1, source_target_pairs={{0,4},{4,8},{8,12},{12,16},{16,20},{20,24},{24,28},{1,5},{5,9},{9,... | collective-permute-start | bytes 301064 | tf_op jit(solution)/shard_map/ppermute | solution.py:20
  117.6 6.2 %collective-permute-start.14 = (f32[112,1,224]{2,0,1:T(8,128)S(1)}, f32[112,1,224]{2,0,1:T(8,128)S(1)}, u32[]{:S(2)}, u32[]{:S(2)}) collective-permute-start(f32[112,1,224]{2,0,1:T(8,128)S(1)} %get-tuple-element.20), channel_id=1, source_target_pairs={{0,1},{1,2},{2,3},{4,5},{5,6},{6,7},{8,9},{9,10},{10,11},{12,13},{... | collective-permute-start | bytes 301064 | tf_op jit(solution)/shard_map/ppermute | solution.py:20
  120.5 7.9 %collective-permute-start.15 = (f32[112,1,224]{2,0,1:T(8,128)S(1)}, f32[112,1,224]{2,0,1:T(8,128)S(1)}, u32[]{:S(2)}, u32[]{:S(2)}) collective-permute-start(f32[112,1,224]{2,0,1:T(8,128)S(1)} %get-tuple-element.21), channel_id=1, source_target_pairs={{1,0},{2,1},{3,2},{5,4},{6,5},{7,6},{9,8},{10,9},{11,10},{13,12},{... | collective-permute-start | bytes 301064 | tf_op jit(solution)/shard_map/ppermute | solution.py:22
  121.8 6.6 %collective-permute-start.13 = (f32[112,1,224]{2,0,1:T(8,128)S(1)}, f32[112,1,224]{2,0,1:T(8,128)S(1)}, u32[]{:S(2)}, u32[]{:S(2)}) collective-permute-start(f32[112,1,224]{2,0,1:T(8,128)S(1)} %get-tuple-element.22), channel_id=1, source_target_pairs={{4,0},{8,4},{12,8},{16,12},{20,16},{24,20},{28,24},{5,1},{9,5},{13... | collective-permute-start | bytes 301064 | tf_op jit(solution)/shard_map/ppermute | solution.py:22
  128.5 0.7 copy-start.15
  128.5 0.7 copy-start.16
  128.5 0.7 copy-start.17
  128.5 0.7 copy-start.18
  171.0 43.4 %copy-start.6 = (f32[112,1,224]{2,0,1:T(8,128)S(1)}, f32[112,1,224]{2,0,1:T(8,128)}, u32[]{:S(2)}) copy-start(f32[112,1,224]{2,0,1:T(8,128)} %copy-done.5) | copy-start | bytes 301060
  171.0 43.4 %copy-start.8 = (f32[112,1,224]{2,0,1:T(8,128)S(1)}, f32[112,1,224]{2,0,1:T(8,128)}, u32[]{:S(2)}) copy-start(f32[112,1,224]{2,0,1:T(8,128)} %copy-done.7) | copy-start | bytes 301060
where the time goes:
time: 218 us; the launch traced here: 217 us
  blocking collectives  143 us (66%)
  starting transfers between devices  37.6 us (17%)
  local copies, waits for them, and re-layouts  11.9 us (5%)
  waiting for transfers between devices  11 us (5%)
  other arithmetic  6.53 us (3%)
  matrix products  6.14 us (3%)
    psum x3, blocking collectives, total_over(): return lax.psum(partial_value, ('row', 'col'))  122 us
    ppermute x8, starting transfers between devices, padded(): lax.ppermute(tail, axis, [(i, (i + 1) % count) for i in range(ends)])  27.3 us
    all_gather x2, blocking collectives, project(): lax.all_gather(mode_coeffs, 'col', axis=0, tiled=True)  21.4 us
    ppermute x8, starting transfers between devices, padded(): lax.ppermute(head, axis, [((i + 1) % count, i) for i in range(ends)])  10.3 us
    ppermute x8, waiting for transfers between devices, padded(): lax.ppermute(head, axis, [((i + 1) % count, i) for i in range(ends)])  10.3 us
    unnamed x44, local copies, waits for them, and re-layouts  4.91 us
  transfers between devices with their start and end apart: 16, of which 4 were waited for; matrix products, arithmetic and copies ran while one was open for 1% of the time, Pallas kernels for 0%

commit v1 on v0

v1 whole, which is shorter than its diff:
```python
import jax
import jax.numpy as jnp
from jax import lax
from jax.sharding import PartitionSpec as P

FACE_SIGNS = (-1.0, 1.0, -1.0, 1.0)


def swap_tables(rows, cols):
    def table(partner):
        pairs = []
        for r in range(rows):
            for c in range(cols):
                r2, c2 = partner(r, c)
                pairs.append((r * cols + c, r2 * cols + c2))
        return pairs

    def across_rows(r, c):
        other = r + 1 if r % 2 else r - 1
        return (other, c) if 0 <= other < rows else (r, c ^ 1)

    def across_cols(r, c):
        other = c + 1 if c % 2 else c - 1
        return r, other % cols

    return dict(
        mate_row=table(lambda r, c: (r ^ 1, c)),
        next_row=table(across_rows),
        mate_col=table(lambda r, c: (r, c ^ 1)),
        next_col=table(across_cols),
    )


def swap(value, pairs):
    return lax.ppermute(value, ("row", "col"), pairs)


def exchange(field, tables, odd_row, odd_col):
    north, south, west, east = field
    got_mate_row = swap(jnp.where(odd_row, north, south), tables["mate_row"])
    got_next_row = swap(jnp.where(odd_row, south, north), tables["next_row"])
    got_mate_col = swap(jnp.where(odd_col, west, east), tables["mate_col"])
    got_next_col = swap(jnp.where(odd_col, east, west), tables["next_col"])
    return jnp.stack(
        [
            north + jnp.where(odd_row, got_mate_row, got_next_row),
            south + jnp.where(odd_row, got_next_row, got_mate_row),
            west + jnp.where(odd_col, got_mate_col, got_next_col),
            east + jnp.where(odd_col, got_next_col, got_mate_col),
        ]
    )


def gather_strip(block, cols):
    mine = lax.axis_index("col")
    parts = [block]
    for step in range(1, cols):
        parts.append(lax.ppermute(block, "col", [(c, c ^ step) for c in range(cols)]))
    parts = jnp.stack(parts)
    return jnp.concatenate([parts[mine ^ c] for c in range(cols)], axis=0)


def on_device(rows, cols, local_gap, dual_ops, geneo_modes, coarse_inverse, face_rows):
    tables = swap_tables(rows, cols)
    odd_row = lax.axis_index("row") % 2 == 1
    odd_col = lax.axis_index("col") % 2 == 1
    operator = dual_ops[0, 0]
    modes = geneo_modes[0, 0]
    coarse_block = coarse_inverse[0]
    unknowns = operator.shape[0]
    columns, faces, depth = local_gap.shape[2:]
    sign = jnp.array(FACE_SIGNS, jnp.float32).reshape(faces, 1, 1)
    live = lax.broadcasted_iota(jnp.int32, (faces, depth, 1), 1) < face_rows[0, 0][:, None, None]

    def glue(field):
        return jnp.where(live, exchange(field, tables, odd_row, odd_col), 0.0)

    def flat(field):
        return field.astype(jnp.bfloat16).reshape(unknowns, columns)

    def apply_dual(vector):
        image = jnp.dot(operator, flat(vector * sign), preferred_element_type=jnp.float32)
        return image.reshape(vector.shape) * sign

    def coarse_part(vector):
        coeffs = jnp.dot(modes, flat(vector), preferred_element_type=jnp.float32)
        return coeffs

    def spread(coeffs):
        coarse = jnp.dot(
            coarse_block, coeffs, precision=lax.Precision.HIGHEST, preferred_element_type=jnp.float32
        )
        part = lax.dot_general(
            modes, coarse.astype(jnp.bfloat16), (((0,), (0,)), ((), ())), preferred_element_type=jnp.float32
        )
        return part.reshape(faces, depth, columns)

    gap = jnp.transpose(local_gap[0, 0], (1, 2, 0)).astype(jnp.float32) * sign
    residual = glue(gap)
    first = residual - glue(spread(gather_strip(coarse_part(residual), cols)))
    first_image = apply_dual(first)
    image = glue(first_image)
    second = image - glue(spread(gather_strip(coarse_part(image), cols)))
    second_image = apply_dual(second)

    def inner(left, right):
        return jnp.sum(left * right, axis=(0, 1))

    partial = jnp.stack(
        [
            0.5 * inner(first, first),
            inner(first, first_image),
            0.5 * inner(first, second),
            0.5 * inner(second, second),
            inner(first, second_image) + inner(second, first_image),
            inner(second, second_image),
        ]
    )
    devices = rows * cols
    every = lax.all_to_all(jnp.broadcast_to(partial[None], (devices,) + partial.shape), ("row", "col"), 0, 0)
    norm, curvature, mixed, square, cross, bend = jnp.sum(every, axis=0)
    step = norm / curvature
    fresh = norm - 2.0 * step * mixed + step * (step * square)
    ratio = fresh / norm
    grow = 1.0 + ratio
    next_curvature = grow * (grow * curvature) - grow * (step * cross) + step * (step * bend)
    next_step = fresh / next_curvature
    solution = (step + next_step * grow) * first - (next_step * step) * second
    return jnp.transpose(solution, (2, 0, 1))[None, None]


def solution(mesh):
    rows, cols = mesh.shape["row"], mesh.shape["col"]

    def body(*arrays):
        return on_device(rows, cols, *arrays)

    return jax.shard_map(
        body,
        mesh=mesh,
        in_specs=(
            P("row", "col", None, None, None),
            P("row", "col", None, None),
            P("row", "col", None, None),
            P("row", "col", None),
            P("row", "col", None),
        ),
        out_specs=P("row", "col", None, None, None),
        check_vma=False,
    )
```

time: 218 us -> 113 us (0.52)
  blocking collectives: 143 us -> 11.6 us
  waiting for transfers between devices: 11 us -> 38.4 us
  starting transfers between devices: 37.6 us -> 24.1 us
  local copies, waits for them, and re-layouts: 11.9 us -> 25 us
    psum x3 -> x0, blocking collectives: 122 us -> none  [total_over(): return lax.psum(partial_value, ('row', 'col'))]
    ppermute x16 -> x22, waiting for transfers between devices: 11 us -> 38.4 us  [the longest x16 31.2 us: swap(): return lax.ppermute(value, ('row', 'col'), pairs)]
    all_gather x2 -> x0, blocking collectives: 21.4 us -> none  [project(): lax.all_gather(mode_coeffs, 'col', axis=0, tiled=True)]
    another operation x0 -> x9, local copies, waits for them, and re-layouts: none -> 16.4 us  [the longest x8 15.7 us: exchange(): jnp.stack([north + jnp.where(odd_row, got_mate_row, got_next_row), south...]
    ppermute x16 -> x22, starting transfers between devices: 37.6 us -> 24.1 us  [the longest x16 17 us: swap(): return lax.ppermute(value, ('row', 'col'), pairs)]
    all_to_all x0 -> x1, blocking collectives: none -> 11.6 us  [on_device(): lax.all_to_all(jnp.broadcast_to(partial[None], (devices,) + partial.shape...]
    unnamed x44 -> x40, local copies, waits for them, and re-layouts: 4.91 us -> 0.08 us
    add x5 -> x3, other arithmetic: 3.99 us -> 0.04 us  [the longest x1 0.02 us: on_device(): grow = 1.0 + ratio]
  transfers between devices with their start and end apart: 16 -> 22, of which waited for: 4 -> 18; matrix products, arithmetic and copies ran while one was open for 1% -> 9% of each run, Pallas kernels for 0% -> 0%
where the time goes in v1:
time: 113 us
  waiting for transfers between devices  38.4 us (34%)
  local copies, waits for them, and re-layouts  25 us (22%)
  starting transfers between devices  24.1 us (21%)
  blocking collectives  11.6 us (10%)
  other arithmetic  8.14 us (7%)
  matrix products  5.11 us (5%)
    ppermute x16, waiting for transfers between devices, swap(): return lax.ppermute(value, ('row', 'col'), pairs)  31.2 us
    ppermute x16, starting transfers between devices, swap(): return lax.ppermute(value, ('row', 'col'), pairs)  17 us
    another operation x8, local copies, waits for them, and re-layouts, exchange(): jnp.stack([north + jnp.where(odd_row, got_mate_row, got_next_row), south...  15.7 us
    all_to_all x1, blocking collectives, on_device(): lax.all_to_all(jnp.broadcast_to(partial[None], (devices,) + partial.shape...  11.6 us
    ppermute x6, waiting for transfers between devices, gather_strip(): lax.ppermute(block, 'col', [(c, c ^ step) for c in range(cols)])  7.23 us
    ppermute x6, starting transfers between devices, gather_strip(): lax.ppermute(block, 'col', [(c, c ^ step) for c in range(cols)])  7.11 us
    convert_element_type x8, local copies, waits for them, and re-layouts, flat(): return field.astype(jnp.bfloat16).reshape(unknowns, columns)  4.31 us
    convert_element_type x4, other arithmetic, flat(): return field.astype(jnp.bfloat16).reshape(unknowns, columns)  3.14 us
  transfers between devices with their start and end apart: 22, of which 18 were waited for; matrix products, arithmetic and copies ran while one was open for 9% of the time, Pallas kernels for 0%

profile of v1, /device:TPU:0, one launch (start us, length us, event | category | flops | bytes accessed | tf_op | source)
XLA Modules:
  0.0 112.8 jit_solution(15327116480130310203)
XLA Ops:
  0.0 1.2 %fusion.13 = f32[4,224,112]{1,2,0:T(8,128)S(1)} fusion(bf16[1,1,112,4,224]{4,3,2,1,0:T(4,128)(2,1)} %param.6, f32[4]{0:T(128)} %constant.42.clone), kind=kLoop, calls=%fused_computation.16 | loop fusion | flops 200704 | bytes 602128 | tf_op jit(solution)/shard_map/mul | solution.py:98
  1.8 2.6 %collective-permute-start.1 = (f32[224,112]{0,1:T(8,128)S(1)}, f32[224,112]{0,1:T(8,128)S(1)}, u32[]{:S(2)}, u32[]{:S(2)}) collective-permute-start(f32[224,112]{0,1:T(8,128)S(1)} %get-tuple-element.50), channel_id=1, source_target_pairs={{0,1},{1,0},{2,3},{3,2},{4,8},{5,9},{6,10},{7,11},{8,4},{9,5},{10,... | collective-permute-start | bytes 301064 | tf_op jit(solution)/shard_map/ppermute | solution.py:35
  4.3 2.8 %collective-permute-done.1 = f32[224,112]{0,1:T(8,128)S(1)} collective-permute-done((f32[224,112]{0,1:T(8,128)S(1)}, f32[224,112]{0,1:T(8,128)S(1)}, u32[]{:S(2)}, u32[]{:S(2)}) %collective-permute-start.1) | collective-permute-done | bytes 100384 | tf_op jit(solution)/shard_map/ppermute | solution.py:35
  7.2 3.0 %collective-permute-start.3 = (f32[224,112]{0,1:T(8,128)S(1)}, f32[224,112]{0,1:T(8,128)S(1)}, u32[]{:S(2)}, u32[]{:S(2)}) collective-permute-start(f32[224,112]{0,1:T(8,128)S(1)} %get-tuple-element.47), channel_id=1, source_target_pairs={{0,3},{1,2},{2,1},{3,0},{4,7},{5,6},{6,5},{7,4},{8,11},{9,10},{10,... | collective-permute-start | bytes 301064 | tf_op jit(solution)/shard_map/ppermute | solution.py:35
  10.8 3.4 %collective-permute-done.3 = f32[224,112]{0,1:T(8,128)S(1)} collective-permute-done((f32[224,112]{0,1:T(8,128)S(1)}, f32[224,112]{0,1:T(8,128)S(1)}, u32[]{:S(2)}, u32[]{:S(2)}) %collective-permute-start.3) | collective-permute-done | bytes 100384 | tf_op jit(solution)/shard_map/ppermute | solution.py:35
  14.2 2.1 %collective-permute-done.2 = f32[224,112]{0,1:T(8,128)S(1)} collective-permute-done((f32[224,112]{0,1:T(8,128)S(1)}, f32[224,112]{0,1:T(8,128)S(1)}, u32[]{:S(2)}, u32[]{:S(2)}) %collective-permute-start.2) | collective-permute-done | bytes 100384 | tf_op jit(solution)/shard_map/ppermute | solution.py:35
  17.4 1.7 %collective-permute-start.4 = (f32[128,112]{0,1:T(8,128)S(1)}, f32[128,112]{0,1:T(8,128)S(1)}, u32[]{:S(2)}, u32[]{:S(2)}) collective-permute-start(f32[128,112]{0,1:T(8,128)S(1)} %bitcast.243), channel_id=1, source_target_pairs={{0,1},{1,0},{2,3},{3,2},{4,5},{5,4},{6,7},{7,6},{8,9},{9,8},{10,11... | collective-permute-start | bytes 172040 | tf_op jit(solution)/shard_map/ppermute | solution.py:58
  19.1 1.5 %collective-permute-start.6 = (f32[128,112]{0,1:T(8,128)S(1)}, f32[128,112]{0,1:T(8,128)S(1)}, u32[]{:S(2)}, u32[]{:S(2)}) collective-permute-start(f32[128,112]{0,1:T(8,128)S(1)} %bitcast.244), channel_id=1, source_target_pairs={{0,3},{1,2},{2,1},{3,0},{4,7},{5,6},{6,5},{7,4},{8,11},{9,10},{10,... | collective-permute-start | bytes 172040 | tf_op jit(solution)/shard_map/ppermute | solution.py:58
  20.5 0.7 collective-permute-done.5
  21.8 2.3 %collective-permute-done.6 = f32[128,112]{0,1:T(8,128)S(1)} collective-permute-done((f32[128,112]{0,1:T(8,128)S(1)}, f32[128,112]{0,1:T(8,128)S(1)}, u32[]{:S(2)}, u32[]{:S(2)}) %collective-permute-start.6) | collective-permute-done | bytes 57376 | tf_op jit(solution)/shard_map/ppermute | solution.py:58
  25.0 0.7 collective-permute-start.8
  26.3 3.5 %collective-permute-done.8 = f32[224,112]{0,1:T(8,128)S(1)} collective-permute-done((f32[224,112]{0,1:T(8,128)S(1)}, f32[224,112]{0,1:T(8,128)S(1)}, u32[]{:S(2)}, u32[]{:S(2)}) %collective-permute-start.8) | collective-permute-done | bytes 100384 | tf_op jit(solution)/shard_map/ppermute | solution.py:35
  30.0 1.6 %collective-permute-start.10 = (f32[224,112]{0,1:T(8,128)S(1)}, f32[224,112]{0,1:T(8,128)S(1)}, u32[]{:S(2)}, u32[]{:S(2)}) collective-permute-start(f32[224,112]{0,1:T(8,128)S(1)} %get-tuple-element.55), channel_id=1, source_target_pairs={{0,3},{1,2},{2,1},{3,0},{4,7},{5,6},{6,5},{7,4},{8,11},{9,10},{10,... | collective-permute-start | bytes 301064 | tf_op jit(solution)/shard_map/ppermute | solution.py:35
  31.6 1.5 %collective-permute-start.9 = (f32[224,112]{0,1:T(8,128)S(1)}, f32[224,112]{0,1:T(8,128)S(1)}, u32[]{:S(2)}, u32[]{:S(2)}) collective-permute-start(f32[224,112]{0,1:T(8,128)S(1)} %get-tuple-element.56), channel_id=1, source_target_pairs={{0,1},{1,0},{2,3},{3,2},{4,5},{5,4},{6,7},{7,6},{8,9},{9,8},{10,11... | collective-permute-start | bytes 301064 | tf_op jit(solution)/shard_map/ppermute | solution.py:35
  33.0 3.9 %collective-permute-done.10 = f32[224,112]{0,1:T(8,128)S(1)} collective-permute-done((f32[224,112]{0,1:T(8,128)S(1)}, f32[224,112]{0,1:T(8,128)S(1)}, u32[]{:S(2)}, u32[]{:S(2)}) %collective-permute-start.10) | collective-permute-done | bytes 100384 | tf_op jit(solution)/shard_map/ppermute | solution.py:35
  37.0 1.7 %collective-permute-done.9 = f32[224,112]{0,1:T(8,128)S(1)} collective-permute-done((f32[224,112]{0,1:T(8,128)S(1)}, f32[224,112]{0,1:T(8,128)S(1)}, u32[]{:S(2)}, u32[]{:S(2)}) %collective-permute-start.9) | collective-permute-done | bytes 100384 | tf_op jit(solution)/shard_map/ppermute | solution.py:35
  38.8 1.1 multiply_convert_fusion.1
  42.0 0.7 collective-permute-done.11
  42.8 3.5 %collective-permute-done.12 = f32[224,112]{0,1:T(8,128)S(1)} collective-permute-done((f32[224,112]{0,1:T(8,128)S(1)}, f32[224,112]{0,1:T(8,128)S(1)}, u32[]{:S(2)}, u32[]{:S(2)}) %collective-permute-start.12) | collective-permute-done | bytes 100384 | tf_op jit(solution)/shard_map/ppermute | solution.py:35
  47.0 1.4 %collective-permute-start.13 = (f32[224,112]{0,1:T(8,128)S(1)}, f32[224,112]{0,1:T(8,128)S(1)}, u32[]{:S(2)}, u32[]{:S(2)}) collective-permute-start(f32[224,112]{0,1:T(8,128)S(1)} %get-tuple-element.44), channel_id=1, source_target_pairs={{0,1},{1,0},{2,3},{3,2},{4,5},{5,4},{6,7},{7,6},{8,9},{9,8},{10,11... | collective-permute-start | bytes 301064 | tf_op jit(solution)/shard_map/ppermute | solution.py:35
  48.4 5.0 %collective-permute-done.14 = f32[224,112]{0,1:T(8,128)S(1)} collective-permute-done((f32[224,112]{0,1:T(8,128)S(1)}, f32[224,112]{0,1:T(8,128)S(1)}, u32[]{:S(2)}, u32[]{:S(2)}) %collective-permute-start.14) | collective-permute-done | bytes 100384 | tf_op jit(solution)/shard_map/ppermute | solution.py:35
  54.1 0.8 copy.37
  54.9 1.9 %convert_element_type.75 = bf16[896,112]{0,1:T(8,128)(2,1)} reshape(bf16[4,224,112]{1,0,2:T(4,128)(2,1)} %copy.37) | data formatting | bytes 401408 | tf_op jit(solution)/shard_map/convert_element_type | solution.py:79
  56.8 1.1 %fusion.31 = f32[112,128]{1,0:T(8,128)S(1)} fusion(bf16[896,112]{0,1:T(8,128)(2,1)} %convert_element_type.75, bf16[1,1,128,896]{3,2,1,0:T(8,128)(2,1)S(1)} %copy-done.1), kind=kOutput, calls=%fused_computation.53 | convolution fusion | flops 25690112 | bytes 487424 | tf_op jit(solution)/shard_map/dot_general | solution.py:86
  57.9 1.6 %collective-permute-start.16 = (f32[128,112]{0,1:T(8,128)S(1)}, f32[128,112]{0,1:T(8,128)S(1)}, u32[]{:S(2)}, u32[]{:S(2)}) collective-permute-start(f32[128,112]{0,1:T(8,128)S(1)} %bitcast.246), channel_id=1, source_target_pairs={{0,2},{1,3},{2,0},{3,1},{4,6},{5,7},{6,4},{7,5},{8,10},{9,11},{10,... | collective-permute-start | bytes 172040 | tf_op jit(solution)/shard_map/ppermute | solution.py:58
  60.0 1.4 %collective-permute-start.17 = (f32[128,112]{0,1:T(8,128)S(1)}, f32[128,112]{0,1:T(8,128)S(1)}, u32[]{:S(2)}, u32[]{:S(2)}) collective-permute-start(f32[128,112]{0,1:T(8,128)S(1)} %bitcast.248), channel_id=1, source_target_pairs={{0,3},{1,2},{2,1},{3,0},{4,7},{5,6},{6,5},{7,4},{8,11},{9,10},{10,... | collective-permute-start | bytes 172040 | tf_op jit(solution)/shard_map/ppermute | solution.py:58
  62.2 1.5 %collective-permute-done.15 = f32[128,112]{0,1:T(8,128)S(1)} collective-permute-done((f32[128,112]{0,1:T(8,128)S(1)}, f32[128,112]{0,1:T(8,128)S(1)}, u32[]{:S(2)}, u32[]{:S(2)}) %collective-permute-start.15) | collective-permute-done | bytes 57376 | tf_op jit(solution)/shard_map/ppermute | solution.py:58
  63.7 1.4 %collective-permute-done.17 = f32[128,112]{0,1:T(8,128)S(1)} collective-permute-done((f32[128,112]{0,1:T(8,128)S(1)}, f32[128,112]{0,1:T(8,128)S(1)}, u32[]{:S(2)}, u32[]{:S(2)}) %collective-permute-start.17) | collective-permute-done | bytes 57376 | tf_op jit(solution)/shard_map/ppermute | solution.py:58
  66.0 1.6 %collective-permute-start.19 = (f32[224,112]{0,1:T(8,128)S(1)}, f32[224,112]{0,1:T(8,128)S(1)}, u32[]{:S(2)}, u32[]{:S(2)}) collective-permute-start(f32[224,112]{0,1:T(8,128)S(1)} %get-tuple-element.54), channel_id=1, source_target_pairs={{0,1},{1,0},{2,3},{3,2},{4,8},{5,9},{6,10},{7,11},{8,4},{9,5},{10,... | collective-permute-start | bytes 301064 | tf_op jit(solution)/shard_map/ppermute | solution.py:35
  67.5 3.3 %collective-permute-done.19 = f32[224,112]{0,1:T(8,128)S(1)} collective-permute-done((f32[224,112]{0,1:T(8,128)S(1)}, f32[224,112]{0,1:T(8,128)S(1)}, u32[]{:S(2)}, u32[]{:S(2)}) %collective-permute-start.19) | collective-permute-done | bytes 100384 | tf_op jit(solution)/shard_map/ppermute | solution.py:35
  70.8 0.9 add_bitcast_fusion.3
  71.7 1.4 %collective-permute-start.21 = (f32[224,112]{0,1:T(8,128)}, f32[224,112]{0,1:T(8,128)}, u32[]{:S(2)}, u32[]{:S(2)}) collective-permute-start(f32[224,112]{0,1:T(8,128)} %get-tuple-element.51), channel_id=1, source_target_pairs={{0,3},{1,2},{2,1},{3,0},{4,7},{5,6},{6,5},{7,4},{8,11},{9,10},{10,... | collective-permute-start | bytes 301064 | tf_op jit(solution)/shard_map/ppermute | solution.py:35
  73.8 1.3 %lt.51 = pred[896]{0:T(1024)(128)(4,1)} reshape(pred[4,224]{1,0:T(4,128)(4,1)} %copy-done.16) | data formatting | bytes 1792 | tf_op jit(solution)/shard_map/lt | solution.py:73
  75.1 0.7 mul.275
  76.5 2.1 %copy.33 = f32[4,224,112]{1,0,2:T(4,128)} copy(f32[4,224,112]{1,2,0:T(8,128)} %get-tuple-element.41) | data formatting | bytes 802816 | tf_op jit(solution)/shard_map/stack | solution.py:44
  78.6 2.1 %stack.126 = f32[896,112]{0,1:T(8,128)} reshape(f32[4,224,112]{1,0,2:T(4,128)} %copy.33) | data formatting | bytes 802816 | tf_op jit(solution)/shard_map/stack | solution.py:44
  80.8 1.1 copy.34
  81.8 2.1 %stack.127 = f32[896,112]{0,1:T(8,128)} reshape(f32[4,224,112]{1,0,2:T(4,128)} %copy.34) | data formatting | bytes 802816 | tf_op jit(solution)/shard_map/stack | solution.py:44
  83.9 1.1 add_bitcast_fusion.1
  85.1 2.0 %multiply_convert_fusion = (bf16[4,224,112]{1,2,0:T(8,128)(2,1)S(1)}, f32[4,224,112]{1,2,0:T(8,128)S(1)}, f32[4,224,112]{1,2,0:T(8,128)}, f32[4,224,112]{1,2,0:T(8,128)}) fusion(f32[4]{0:T(128)} %constant.42.clone, f32[1,224,112]{1,2,0:T(8,128)S(1)} %get-tuple-element.34, f32[1,224,112]{1,2,0:T(8,128)S(1)} %get-tuple-element.33, ...), kind=kLoop, calls=%fused_computation.19 | loop fusion | flops 1103872 | bytes 2208656 | tf_op jit(solution)/shard_map/convert_element_type | solution.py:79
  87.2 0.9 convert_element_type.78
  88.1 2.1 %copy.39 = f32[4,224,112]{1,0,2:T(4,128)} copy(f32[4,224,112]{1,2,0:T(8,128)} %get-tuple-element.39) | data formatting | bytes 802816 | tf_op jit(solution)/shard_map/stack | solution.py:44
  90.2 2.1 %stack.144 = f32[896,112]{0,1:T(8,128)} reshape(f32[4,224,112]{1,0,2:T(4,128)} %copy.39) | data formatting | bytes 802816 | tf_op jit(solution)/shard_map/stack | solution.py:44
  92.3 2.1 %copy.40 = f32[4,224,112]{1,0,2:T(4,128)} copy(f32[4,224,112]{1,2,0:T(8,128)} %get-tuple-element.40) | data formatting | bytes 802816 | tf_op jit(solution)/shard_map/stack | solution.py:44
  94.4 2.1 %stack.145 = f32[896,112]{0,1:T(8,128)} reshape(f32[4,224,112]{1,0,2:T(4,128)} %copy.40) | data formatting | bytes 802816 | tf_op jit(solution)/shard_map/stack | solution.py:44
  97.2 2.0 %multiply_reduce_fusion.5 = (f32[112]{0:T(128)S(1)}, f32[112]{0:T(128)S(1)}, f32[112]{0:T(128)S(1)}, f32[112]{0:T(128)S(1)}) fusion(f32[896,112]{0,1:T(8,128)} %stack.127, f32[896,112]{0,1:T(8,128)S(1)} %copy-done.3, pred[896]{0:T(1024)(128)(4,1)S(1)} %copy-done.18, f32[896,112]{0,1:T(8,128)S(1)} %fusion.4, f32[896]{0:T(1024)S(1)} %copy-done.15, ...), kind=kOutput, calls=%fused_computation.31 | convolution fusion | flops 181435968 | bytes 3819648 | tf_op jit(solution)/shard_map/dot_general | solution.py:82
  99.9 11.6 %all_to_all.5 = f32[32,6,112]{2,1,0:T(8,128)S(1)} all-to-all(f32[32,6,112]{2,1,0:T(8,128)S(1)} %broadcast_in_dim.43), channel_id=1, replica_groups=mesh['row'=8,'col'=4] {'row','col'}, dimensions={0} | all-to-all | bytes 172032 | tf_op jit(solution)/shard_map/all_to_all | solution.py:120
  111.7 1.1 copy.42
  (99 shorter events, 13.2 us)
Async XLA Ops:
  0.0 40.2 %copy-start = (bf16[1,1,896,896]{3,2,1,0:T(8,128)(2,1)S(1)}, bf16[1,1,896,896]{3,2,1,0:T(8,128)(2,1)}, u32[]{:S(2)}) copy-start(bf16[1,1,896,896]{3,2,1,0:T(8,128)(2,1)} %param.7) | copy-start | bytes 4816900
  0.0 10.7 %copy-start.19 = (s32[1,1,4]{2,1,0:T(1,128)S(1)}, s32[1,1,4]{2,1,0:T(1,128)}, u32[]{:S(2)}) copy-start(s32[1,1,4]{2,1,0:T(1,128)} %param.10) | copy-start | bytes 52
  1.2 3.1 %collective-permute-start = (f32[224,112]{0,1:T(8,128)S(1)}, f32[224,112]{0,1:T(8,128)S(1)}, u32[]{:S(2)}, u32[]{:S(2)}) collective-permute-start(f32[224,112]{0,1:T(8,128)S(1)} %get-tuple-element.49), channel_id=1, source_target_pairs={{0,4},{1,5},{2,6},{3,7},{4,0},{5,1},{6,2},{7,3},{8,12},{9,13},{10,... | collective-permute-start | bytes 301064 | tf_op jit(solution)/shard_map/ppermute | solution.py:35
  1.8 5.3 %collective-permute-start.1 = (f32[224,112]{0,1:T(8,128)S(1)}, f32[224,112]{0,1:T(8,128)S(1)}, u32[]{:S(2)}, u32[]{:S(2)}) collective-permute-start(f32[224,112]{0,1:T(8,128)S(1)} %get-tuple-element.50), channel_id=1, source_target_pairs={{0,1},{1,0},{2,3},{3,2},{4,8},{5,9},{6,10},{7,11},{8,4},{9,5},{10,... | collective-permute-start | bytes 301064 | tf_op jit(solution)/shard_map/ppermute | solution.py:35
  4.3 12.4 %copy-start.1 = (bf16[1,1,128,896]{3,2,1,0:T(8,128)(2,1)S(1)}, bf16[1,1,128,896]{3,2,1,0:T(8,128)(2,1)}, u32[]{:S(2)}) copy-start(bf16[1,1,128,896]{3,2,1,0:T(8,128)(2,1)} %param.8) | copy-start | bytes 688132
  7.2 7.0 %collective-permute-start.3 = (f32[224,112]{0,1:T(8,128)S(1)}, f32[224,112]{0,1:T(8,128)S(1)}, u32[]{:S(2)}, u32[]{:S(2)}) collective-permute-start(f32[224,112]{0,1:T(8,128)S(1)} %get-tuple-element.47), channel_id=1, source_target_pairs={{0,3},{1,2},{2,1},{3,0},{4,7},{5,6},{6,5},{7,4},{8,11},{9,10},{10,... | collective-permute-start | bytes 301064 | tf_op jit(solution)/shard_map/ppermute | solution.py:35
  10.2 6.1 %collective-permute-start.2 = (f32[224,112]{0,1:T(8,128)S(1)}, f32[224,112]{0,1:T(8,128)S(1)}, u32[]{:S(2)}, u32[]{:S(2)}) collective-permute-start(f32[224,112]{0,1:T(8,128)S(1)} %get-tuple-element.48), channel_id=1, source_target_pairs={{0,1},{1,0},{2,3},{3,2},{4,5},{5,4},{6,7},{7,6},{8,9},{9,8},{10,11... | collective-permute-start | bytes 301064 | tf_op jit(solution)/shard_map/ppermute | solution.py:35
  10.8 43.2 %copy-start.16 = (pred[4,224]{1,0:T(4,128)(4,1)}, pred[4,224]{1,0:T(4,128)(4,1)S(1)}, u32[]{:S(2)}) copy-start(pred[4,224]{1,0:T(4,128)(4,1)S(1)} %iota_compare_fusion) | copy-start | bytes 2692
  16.4 7.8 %copy-start.4 = (f32[1,128,512]{2,1,0:T(8,128)S(1)}, f32[1,128,512]{2,1,0:T(8,128)}, u32[]{:S(2)}) copy-start(f32[1,128,512]{2,1,0:T(8,128)} %param.9) | copy-start | bytes 786436
  17.0 4.2 %collective-permute-start.5 = (f32[128,112]{0,1:T(8,128)S(1)}, f32[128,112]{0,1:T(8,128)S(1)}, u32[]{:S(2)}, u32[]{:S(2)}) collective-permute-start(f32[128,112]{0,1:T(8,128)S(1)} %bitcast.242), channel_id=1, source_target_pairs={{0,2},{1,3},{2,0},{3,1},{4,6},{5,7},{6,4},{7,5},{8,10},{9,11},{10,... | collective-permute-start | bytes 172040 | tf_op jit(solution)/shard_map/ppermute | solution.py:58
  17.4 4.4 %collective-permute-start.4 = (f32[128,112]{0,1:T(8,128)S(1)}, f32[128,112]{0,1:T(8,128)S(1)}, u32[]{:S(2)}, u32[]{:S(2)}) collective-permute-start(f32[128,112]{0,1:T(8,128)S(1)} %bitcast.243), channel_id=1, source_target_pairs={{0,1},{1,0},{2,3},{3,2},{4,5},{5,4},{6,7},{7,6},{8,9},{9,8},{10,11... | collective-permute-start | bytes 172040 | tf_op jit(solution)/shard_map/ppermute | solution.py:58
  19.1 5.1 %collective-permute-start.6 = (f32[128,112]{0,1:T(8,128)S(1)}, f32[128,112]{0,1:T(8,128)S(1)}, u32[]{:S(2)}, u32[]{:S(2)}) collective-permute-start(f32[128,112]{0,1:T(8,128)S(1)} %bitcast.244), channel_id=1, source_target_pairs={{0,3},{1,2},{2,1},{3,0},{4,7},{5,6},{6,5},{7,4},{8,11},{9,10},{10,... | collective-permute-start | bytes 172040 | tf_op jit(solution)/shard_map/ppermute | solution.py:58
  24.6 14.2 %copy-start.17 = (f32[4]{0:T(128)S(1)}, f32[4]{0:T(128)}, u32[]{:S(2)}) copy-start(f32[4]{0:T(128)} %constant.42.clone) | copy-start | bytes 52
  24.9 1.4 %collective-permute-start.7 = (f32[224,112]{0,1:T(8,128)S(1)}, f32[224,112]{0,1:T(8,128)S(1)}, u32[]{:S(2)}, u32[]{:S(2)}) collective-permute-start(f32[224,112]{0,1:T(8,128)S(1)} %get-tuple-element.57), channel_id=1, source_target_pairs={{0,4},{1,5},{2,6},{3,7},{4,0},{5,1},{6,2},{7,3},{8,12},{9,13},{10,... | collective-permute-start | bytes 301064 | tf_op jit(solution)/shard_map/ppermute | solution.py:35
  25.0 4.9 %collective-permute-start.8 = (f32[224,112]{0,1:T(8,128)S(1)}, f32[224,112]{0,1:T(8,128)S(1)}, u32[]{:S(2)}, u32[]{:S(2)}) collective-permute-start(f32[224,112]{0,1:T(8,128)S(1)} %get-tuple-element.58), channel_id=1, source_target_pairs={{0,1},{1,0},{2,3},{3,2},{4,8},{5,9},{6,10},{7,11},{8,4},{9,5},{10,... | collective-permute-start | bytes 301064 | tf_op jit(solution)/shard_map/ppermute | solution.py:35
  30.0 7.0 %collective-permute-start.10 = (f32[224,112]{0,1:T(8,128)S(1)}, f32[224,112]{0,1:T(8,128)S(1)}, u32[]{:S(2)}, u32[]{:S(2)}) collective-permute-start(f32[224,112]{0,1:T(8,128)S(1)} %get-tuple-element.55), channel_id=1, source_target_pairs={{0,3},{1,2},{2,1},{3,0},{4,7},{5,6},{6,5},{7,4},{8,11},{9,10},{10,... | collective-permute-start | bytes 301064 | tf_op jit(solution)/shard_map/ppermute | solution.py:35
  31.6 7.1 %collective-permute-start.9 = (f32[224,112]{0,1:T(8,128)S(1)}, f32[224,112]{0,1:T(8,128)S(1)}, u32[]{:S(2)}, u32[]{:S(2)}) collective-permute-start(f32[224,112]{0,1:T(8,128)S(1)} %get-tuple-element.56), channel_id=1, source_target_pairs={{0,1},{1,0},{2,3},{3,2},{4,5},{5,4},{6,7},{7,6},{8,9},{9,8},{10,11... | collective-permute-start | bytes 301064 | tf_op jit(solution)/shard_map/ppermute | solution.py:35
  41.4 1.4 %collective-permute-start.11 = (f32[224,112]{0,1:T(8,128)S(1)}, f32[224,112]{0,1:T(8,128)S(1)}, u32[]{:S(2)}, u32[]{:S(2)}) collective-permute-start(f32[224,112]{0,1:T(8,128)S(1)} %get-tuple-element.45), channel_id=1, source_target_pairs={{0,4},{1,5},{2,6},{3,7},{4,0},{5,1},{6,2},{7,3},{8,12},{9,13},{10,... | collective-permute-start | bytes 301064 | tf_op jit(solution)/shard_map/ppermute | solution.py:35
  41.4 4.9 %collective-permute-start.12 = (f32[224,112]{0,1:T(8,128)S(1)}, f32[224,112]{0,1:T(8,128)S(1)}, u32[]{:S(2)}, u32[]{:S(2)}) collective-permute-start(f32[224,112]{0,1:T(8,128)S(1)} %get-tuple-element.46), channel_id=1, source_target_pairs={{0,1},{1,0},{2,3},{3,2},{4,8},{5,9},{6,10},{7,11},{8,4},{9,5},{10,... | collective-permute-start | bytes 301064 | tf_op jit(solution)/shard_map/ppermute | solution.py:35
  46.4 18.8 %copy-start.9 = (f32[1,224,112]{1,2,0:T(8,128)}, f32[1,224,112]{1,2,0:T(8,128)S(1)}, u32[]{:S(2)}) copy-start(f32[1,224,112]{1,2,0:T(8,128)S(1)} %get-tuple-element.23) | copy-start | bytes 301060
  46.4 18.8 %copy-start.11 = (f32[1,224,112]{1,2,0:T(8,128)}, f32[1,224,112]{1,2,0:T(8,128)S(1)}, u32[]{:S(2)}) copy-start(f32[1,224,112]{1,2,0:T(8,128)S(1)} %get-tuple-element.24) | copy-start | bytes 301060
  46.4 7.0 %collective-permute-start.14 = (f32[224,112]{0,1:T(8,128)S(1)}, f32[224,112]{0,1:T(8,128)S(1)}, u32[]{:S(2)}, u32[]{:S(2)}) collective-permute-start(f32[224,112]{0,1:T(8,128)S(1)} %get-tuple-element.43), channel_id=1, source_target_pairs={{0,3},{1,2},{2,1},{3,0},{4,7},{5,6},{6,5},{7,4},{8,11},{9,10},{10,... | collective-permute-start | bytes 301064 | tf_op jit(solution)/shard_map/ppermute | solution.py:35
  47.0 7.0 %collective-permute-start.13 = (f32[224,112]{0,1:T(8,128)S(1)}, f32[224,112]{0,1:T(8,128)S(1)}, u32[]{:S(2)}, u32[]{:S(2)}) collective-permute-start(f32[224,112]{0,1:T(8,128)S(1)} %get-tuple-element.44), channel_id=1, source_target_pairs={{0,1},{1,0},{2,3},{3,2},{4,5},{5,4},{6,7},{7,6},{8,9},{9,8},{10,11... | collective-permute-start | bytes 301064 | tf_op jit(solution)/shard_map/ppermute | solution.py:35
  54.0 11.2 %copy-start.5 = (f32[1,224,112]{1,2,0:T(8,128)}, f32[1,224,112]{1,2,0:T(8,128)S(1)}, u32[]{:S(2)}) copy-start(f32[1,224,112]{1,2,0:T(8,128)S(1)} %get-tuple-element.25) | copy-start | bytes 301060
  54.0 11.2 %copy-start.7 = (f32[1,224,112]{1,2,0:T(8,128)}, f32[1,224,112]{1,2,0:T(8,128)S(1)}, u32[]{:S(2)}) copy-start(f32[1,224,112]{1,2,0:T(8,128)S(1)} %get-tuple-element.26) | copy-start | bytes 301060
  57.9 4.2 %collective-permute-start.16 = (f32[128,112]{0,1:T(8,128)S(1)}, f32[128,112]{0,1:T(8,128)S(1)}, u32[]{:S(2)}, u32[]{:S(2)}) collective-permute-start(f32[128,112]{0,1:T(8,128)S(1)} %bitcast.246), channel_id=1, source_target_pairs={{0,2},{1,3},{2,0},{3,1},{4,6},{5,7},{6,4},{7,5},{8,10},{9,11},{10,... | collective-permute-start | bytes 172040 | tf_op jit(solution)/shard_map/ppermute | solution.py:58
  59.5 4.2 %collective-permute-start.15 = (f32[128,112]{0,1:T(8,128)S(1)}, f32[128,112]{0,1:T(8,128)S(1)}, u32[]{:S(2)}, u32[]{:S(2)}) collective-permute-start(f32[128,112]{0,1:T(8,128)S(1)} %bitcast.247), channel_id=1, source_target_pairs={{0,1},{1,0},{2,3},{3,2},{4,5},{5,4},{6,7},{7,6},{8,9},{9,8},{10,11... | collective-permute-start | bytes 172040 | tf_op jit(solution)/shard_map/ppermute | solution.py:58
  60.0 5.1 %collective-permute-start.17 = (f32[128,112]{0,1:T(8,128)S(1)}, f32[128,112]{0,1:T(8,128)S(1)}, u32[]{:S(2)}, u32[]{:S(2)}) collective-permute-start(f32[128,112]{0,1:T(8,128)S(1)} %bitcast.248), channel_id=1, source_target_pairs={{0,3},{1,2},{2,1},{3,0},{4,7},{5,6},{6,5},{7,4},{8,11},{9,10},{10,... | collective-permute-start | bytes 172040 | tf_op jit(solution)/shard_map/ppermute | solution.py:58
  65.8 15.0 %copy-start.2 = (f32[4,224,112]{1,2,0:T(8,128)S(1)}, f32[4,224,112]{1,2,0:T(8,128)}, u32[]{:S(2)}) copy-start(f32[4,224,112]{1,2,0:T(8,128)} %get-tuple-element.42) | copy-start | bytes 1204228
  65.9 1.6 %collective-permute-start.18 = (f32[224,112]{0,1:T(8,128)S(1)}, f32[224,112]{0,1:T(8,128)S(1)}, u32[]{:S(2)}, u32[]{:S(2)}) collective-permute-start(f32[224,112]{0,1:T(8,128)S(1)} %get-tuple-element.53), channel_id=1, source_target_pairs={{0,4},{1,5},{2,6},{3,7},{4,0},{5,1},{6,2},{7,3},{8,12},{9,13},{10,... | collective-permute-start | bytes 301064 | tf_op jit(solution)/shard_map/ppermute | solution.py:35
  66.0 4.9 %collective-permute-start.19 = (f32[224,112]{0,1:T(8,128)S(1)}, f32[224,112]{0,1:T(8,128)S(1)}, u32[]{:S(2)}, u32[]{:S(2)}) collective-permute-start(f32[224,112]{0,1:T(8,128)S(1)} %get-tuple-element.54), channel_id=1, source_target_pairs={{0,1},{1,0},{2,3},{3,2},{4,8},{5,9},{6,10},{7,11},{8,4},{9,5},{10,... | collective-permute-start | bytes 301064 | tf_op jit(solution)/shard_map/ppermute | solution.py:35
  71.7 12.2 %collective-permute-start.21 = (f32[224,112]{0,1:T(8,128)}, f32[224,112]{0,1:T(8,128)}, u32[]{:S(2)}, u32[]{:S(2)}) collective-permute-start(f32[224,112]{0,1:T(8,128)} %get-tuple-element.51), channel_id=1, source_target_pairs={{0,3},{1,2},{2,1},{3,0},{4,7},{5,6},{6,5},{7,4},{8,11},{9,10},{10,... | collective-permute-start | bytes 301064 | tf_op jit(solution)/shard_map/ppermute | solution.py:35
  73.2 10.8 %collective-permute-start.20 = (f32[224,112]{0,1:T(8,128)}, f32[224,112]{0,1:T(8,128)}, u32[]{:S(2)}, u32[]{:S(2)}) collective-permute-start(f32[224,112]{0,1:T(8,128)} %get-tuple-element.52), channel_id=1, source_target_pairs={{0,1},{1,0},{2,3},{3,2},{4,5},{5,4},{6,7},{7,6},{8,9},{9,8},{10,11... | collective-permute-start | bytes 301064 | tf_op jit(solution)/shard_map/ppermute | solution.py:35
  78.6 6.4 %copy-start.6 = (f32[1,224,112]{1,2,0:T(8,128)S(1)}, f32[1,224,112]{1,2,0:T(8,128)}, u32[]{:S(2)}) copy-start(f32[1,224,112]{1,2,0:T(8,128)} %copy-done.5) | copy-start | bytes 301060
  78.6 6.4 %copy-start.8 = (f32[1,224,112]{1,2,0:T(8,128)S(1)}, f32[1,224,112]{1,2,0:T(8,128)}, u32[]{:S(2)}) copy-start(f32[1,224,112]{1,2,0:T(8,128)} %copy-done.7) | copy-start | bytes 301060
  81.8 3.2 %copy-start.10 = (f32[1,224,112]{1,2,0:T(8,128)S(1)}, f32[1,224,112]{1,2,0:T(8,128)}, u32[]{:S(2)}) copy-start(f32[1,224,112]{1,2,0:T(8,128)} %copy-done.9) | copy-start | bytes 301060
  81.8 3.2 %copy-start.12 = (f32[1,224,112]{1,2,0:T(8,128)S(1)}, f32[1,224,112]{1,2,0:T(8,128)}, u32[]{:S(2)}) copy-start(f32[1,224,112]{1,2,0:T(8,128)} %copy-done.11) | copy-start | bytes 301060
  81.8 3.2 %copy-start.14 = (f32[1,224,112]{1,2,0:T(8,128)S(1)}, f32[1,224,112]{1,2,0:T(8,128)}, u32[]{:S(2)}) copy-start(f32[1,224,112]{1,2,0:T(8,128)} %get-tuple-element.31) | copy-start | bytes 301060
  90.2 7.0 %copy-start.3 = (f32[896,112]{0,1:T(8,128)S(1)}, f32[896,112]{0,1:T(8,128)}, u32[]{:S(2)}) copy-start(f32[896,112]{0,1:T(8,128)} %stack.126) | copy-start | bytes 1204228
  90.2 7.0 %copy-start.13 = (bf16[896,112]{0,1:T(8,128)(2,1)S(1)}, bf16[896,112]{0,1:T(8,128)(2,1)}, u32[]{:S(2)}) copy-start(bf16[896,112]{0,1:T(8,128)(2,1)} %convert_element_type.78) | copy-start | bytes 602116
  90.2 7.0 %copy-start.15 = (f32[896]{0:T(1024)S(1)}, f32[896]{0:T(1024)}, u32[]{:S(2)}) copy-start(f32[896]{0:T(1024)} %mul.276) | copy-start | bytes 10756
  90.2 7.0 %copy-start.18 = (pred[896]{0:T(1024)(128)(4,1)S(1)}, pred[896]{0:T(1024)(128)(4,1)}, u32[]{:S(2)}) copy-start(pred[896]{0:T(1024)(128)(4,1)} %lt.51) | copy-start | bytes 2692

commit v2 on v1

v2 whole, which is shorter than its diff:
```python
import functools

import jax
import jax.numpy as jnp
from jax import lax
from jax.experimental import pallas as pl
from jax.experimental.pallas import tpu as pltpu
from jax.sharding import PartitionSpec as P

PARTNERS = 4
SCALE_ROWS = 8


def swap_tables(rows, cols):
    def table(partner):
        pairs = []
        for r in range(rows):
            for c in range(cols):
                r2, c2 = partner(r, c)
                pairs.append((r * cols + c, r2 * cols + c2))
        return pairs

    def across_rows(r, c):
        other = r + 1 if r % 2 else r - 1
        return (other, c) if 0 <= other < rows else (r, c ^ 1)

    def across_cols(r, c):
        other = c + 1 if c % 2 else c - 1
        return r, other % cols

    return [
        table(lambda r, c: (r ^ 1, c)),
        table(across_rows),
        table(lambda r, c: (r, c ^ 1)),
        table(across_cols),
    ]


def faces_of_partners():
    odd_row = lax.rem(lax.axis_index("row"), 2)
    odd_col = lax.rem(lax.axis_index("col"), 2)
    return [1 - odd_row, odd_row, 3 - odd_col, 2 + odd_col]


def face_slice(face, depth):
    return pl.ds(pl.multiple_of(face * depth, depth), depth)


def face_sign(face):
    return (2 * lax.rem(face, 2) - 1).astype(jnp.float32)


def masked(value, count):
    unknown = lax.broadcasted_iota(jnp.int32, value.shape, 0)
    return jnp.where(unknown < count, value, 0.0)


def column_sum(value):
    return jnp.sum(value, axis=0, keepdims=True)


def gap_kernel(gap_ref, *refs):
    out_refs, field = refs[:PARTNERS], refs[PARTNERS]
    depth = gap_ref.shape[2]
    for face in range(PARTNERS):
        sign = 1.0 if face % 2 else -1.0
        block = gap_ref[:, face, :].astype(jnp.float32) * sign
        field[face * depth : (face + 1) * depth, :] = block.T
    for face, out_ref in zip(faces_of_partners(), out_refs):
        out_ref[...] = field[face_slice(face, depth), :]


def turn_kernel(modes_ref, out_ref):
    out_ref[...] = modes_ref[...].astype(jnp.float32).T.astype(jnp.bfloat16)


def read_pair(mine_ref, got_ref, count, scaled):
    depth = mine_ref.shape[0] - (SCALE_ROWS if scaled else 0)
    return mine_ref[:depth, :], got_ref[:depth, :]


def scale_of(ref):
    depth = ref.shape[0] - SCALE_ROWS
    return ref[depth : depth + 1, :]


def widest(own_scale, got_refs, counts):
    top = own_scale
    for ref, count in zip(got_refs, counts):
        top = jnp.maximum(top, jnp.where(count > 0, scale_of(ref), own_scale))
    return top


def glued(mine_refs, got_refs, counts, scaled):
    fields = []
    if scaled:
        own_scale = scale_of(mine_refs[0])
        top = widest(own_scale, got_refs, counts)
        own_factor = own_scale / top
    else:
        top = None
    for mine_ref, got_ref, count in zip(mine_refs, got_refs, counts):
        mine, got = read_pair(mine_ref, got_ref, count, scaled)
        if scaled:
            mine, got = mine * own_factor, got * (scale_of(got_ref) / top)
        fields.append(masked(mine + got, count))
    return fields, top


def counts_of(rows_ref, faces):
    return [rows_ref[0, 0, face] for face in faces]


def coeffs_kernel(scaled, rows_ref, modes_ref, *refs):
    mine_refs, got_refs, out_ref, flat = refs[:4], refs[4:8], refs[8], refs[9]
    faces = faces_of_partners()
    fields, top = glued(mine_refs, got_refs, counts_of(rows_ref, faces), scaled)
    depth = fields[0].shape[0]
    for face, field in zip(faces, fields):
        flat[face_slice(face, depth), :] = field.astype(jnp.bfloat16)
    count = modes_ref.shape[0]
    out_ref[:count, :] = jnp.dot(modes_ref[...], flat[...], preferred_element_type=jnp.float32)
    if scaled:
        out_ref[count:, :] = jnp.broadcast_to(top, (SCALE_ROWS, top.shape[1]))


def coarse_kernel(cols, scaled, coarse_ref, turned_ref, *refs):
    block_refs, out_refs = refs[:cols], refs[cols:]
    mine = lax.axis_index("col")
    count = coarse_ref.shape[0]
    depth = turned_ref.shape[0] // PARTNERS
    top = None
    if scaled:
        top = functools.reduce(jnp.maximum, [scale_of(ref) for ref in block_refs])
    total = None
    for step, ref in enumerate(block_refs):
        block = ref[:count, :]
        if scaled:
            block = block * (scale_of(ref) / top)
        start = pl.multiple_of((mine ^ step) * count, count)
        term = jnp.dot(
            coarse_ref[:, pl.ds(start, count)],
            block,
            precision=lax.Precision.HIGHEST,
            preferred_element_type=jnp.float32,
        )
        total = term if total is None else total + term
    coarse = total.astype(jnp.bfloat16)
    for face, out_ref in zip(faces_of_partners(), out_refs):
        out_ref[:depth, :] = jnp.dot(turned_ref[face_slice(face, depth), :], coarse, preferred_element_type=jnp.float32)
        if scaled:
            out_ref[depth:, :] = jnp.broadcast_to(top, (SCALE_ROWS, top.shape[1]))


def apply_dual(operator_ref, fields, faces, flat, image):
    depth = fields[0].shape[0]
    for face, field in zip(faces, fields):
        flat[face_slice(face, depth), :] = (field * face_sign(face)).astype(jnp.bfloat16)
    image[...] = jnp.dot(operator_ref[...], flat[...], preferred_element_type=jnp.float32)
    return [image[face_slice(face, depth), :] * face_sign(face) for face in faces]


def first_kernel(rows_ref, operator_ref, *refs):
    mine_refs, got_refs, part_refs, got_part_refs = refs[:4], refs[4:8], refs[8:12], refs[12:16]
    vector_refs, image_refs, sums_ref, flat, image = refs[16:20], refs[20:24], refs[24], refs[25], refs[26]
    faces = faces_of_partners()
    counts = counts_of(rows_ref, faces)
    residuals, _ = glued(mine_refs, got_refs, counts, False)
    parts, _ = glued(part_refs, got_part_refs, counts, False)
    fields = [residual - part for residual, part in zip(residuals, parts)]
    for ref, field in zip(vector_refs, fields):
        ref[...] = field
    images = apply_dual(operator_ref, fields, faces, flat, image)
    largest = jnp.max(jnp.abs(image[...]), axis=0, keepdims=True)
    largest = jnp.where(largest > 0.0, largest, 1.0)
    inverse = 1.0 / largest
    depth = fields[0].shape[0]
    norm, curvature = 0.0, 0.0
    for ref, field, value in zip(image_refs, fields, images):
        norm += column_sum(field * field)
        curvature += column_sum(field * value)
        ref[:depth, :] = value * inverse
        ref[depth:, :] = jnp.broadcast_to(largest, (SCALE_ROWS, largest.shape[1]))
    sums_ref[0:1, :] = 0.5 * norm
    sums_ref[1:2, :] = curvature


def second_kernel(rows_ref, operator_ref, sums_in_ref, *refs):
    mine_refs, got_refs, part_refs, got_part_refs, first_refs = (refs[4 * i : 4 * i + 4] for i in range(5))
    vector_refs, sums_ref, flat, image = refs[20:24], refs[24], refs[25], refs[26]
    faces = faces_of_partners()
    counts = counts_of(rows_ref, faces)
    images, image_scale = glued(mine_refs, got_refs, counts, True)
    parts, part_scale = glued(part_refs, got_part_refs, counts, True)
    top = jnp.maximum(image_scale, part_scale)
    fields = [value * (image_scale / top) - part * (part_scale / top) for value, part in zip(images, parts)]
    for ref, field in zip(vector_refs, fields):
        ref[...] = field
    own_scale = scale_of(mine_refs[0])
    depth = fields[0].shape[0]
    second_images = apply_dual(operator_ref, fields, faces, flat, image)
    mixed, square, cross, bend = 0.0, 0.0, 0.0, 0.0
    reach = 0.0
    for first_ref, mine_ref, field, value in zip(first_refs, mine_refs, fields, second_images):
        first = first_ref[...]
        mixed += column_sum(first * field)
        square += column_sum(field * field)
        cross += column_sum(first * value)
        reach += column_sum(field * mine_ref[:depth, :])
        bend += column_sum(field * value)
    rows = [sums_in_ref[0:1, :], sums_in_ref[1:2, :], 0.5 * mixed, 0.5 * square, cross + own_scale * reach, bend, top, top]
    table = jnp.concatenate(rows, axis=0)
    sums_ref[...] = jnp.broadcast_to(table[None], sums_ref.shape)


def last_kernel(sums_ref, *refs):
    first_refs, second_refs, out_ref, field = refs[:4], refs[4:8], refs[8], refs[9]
    faces = faces_of_partners()
    device = lax.axis_index("row") * lax.axis_size("col") + lax.axis_index("col")
    every = sums_ref[...]
    scales = every[:, 6:7, :]
    top = jnp.max(scales, axis=0, keepdims=True)
    share = scales / top
    norm = jnp.sum(every[:, 0:1, :], axis=0)
    curvature = jnp.sum(every[:, 1:2, :], axis=0)
    mixed = jnp.sum(every[:, 2:3, :] * share, axis=0)
    square = jnp.sum(every[:, 3:4, :] * share * share, axis=0)
    cross = jnp.sum(every[:, 4:5, :] * share, axis=0)
    bend = jnp.sum(every[:, 5:6, :] * share * share, axis=0)
    step = norm / curvature
    reach = step * top[0]
    fresh = norm - 2.0 * reach * mixed + reach * (reach * square)
    ratio = fresh / norm
    grow = 1.0 + ratio
    next_curvature = grow * (grow * curvature) - grow * (reach * cross) + reach * (reach * bend)
    next_step = fresh / next_curvature
    along_first = step + next_step * grow
    along_second = next_step * (step * sums_ref[device, 6:7, :])
    depth = first_refs[0].shape[0]
    for face, first_ref, second_ref in zip(faces, first_refs, second_refs):
        field[face_slice(face, depth), :] = along_first * first_ref[...] - along_second * second_ref[...]
    for face in range(PARTNERS):
        out_ref[:, face, :] = field[face * depth : (face + 1) * depth, :].T


VMEM = pl.BlockSpec(memory_space=pltpu.VMEM)
SMEM = pl.BlockSpec(memory_space=pltpu.SMEM)


def run(kernel, name, outs, scratch, in_specs, args, flops=0):
    moved = sum(a.size * a.dtype.itemsize for a in args)
    return pl.pallas_call(
        kernel,
        name=name,
        out_shape=outs,
        in_specs=in_specs,
        out_specs=jax.tree.map(lambda _: VMEM, outs),
        scratch_shapes=scratch,
        compiler_params=pltpu.CompilerParams(vmem_limit_bytes=16 * 2**20),
        cost_estimate=pl.CostEstimate(flops=flops, bytes_accessed=moved, transcendentals=0),
    )(*args)


def on_device(rows, cols, local_gap, dual_ops, geneo_modes, coarse_inverse, face_rows):
    tables = swap_tables(rows, cols)
    gap = local_gap[0, 0]
    operator = dual_ops[0, 0]
    modes = geneo_modes[0, 0]
    coarse_block = coarse_inverse[0]
    columns, _, depth = gap.shape
    unknowns = operator.shape[0]
    count = modes.shape[0]

    def shape(*dims, dtype=jnp.float32):
        return jax.ShapeDtypeStruct(dims, dtype)

    def swap(fields):
        return [lax.ppermute(field, ("row", "col"), pairs) for field, pairs in zip(fields, tables)]

    def gather(block):
        steps = [[(c, c ^ step) for c in range(cols)] for step in range(1, cols)]
        return [block] + [lax.ppermute(block, "col", pairs) for pairs in steps]

    def four(height):
        return [shape(height, columns)] * PARTNERS

    flat = pltpu.VMEM((unknowns, columns), jnp.bfloat16)
    wide = pltpu.VMEM((unknowns, columns), jnp.float32)
    tall = depth + SCALE_ROWS

    gaps = run(gap_kernel, "gap", four(depth), [wide], [VMEM], [gap])
    got_gaps = swap(gaps)
    turned = run(turn_kernel, "turn", shape(unknowns, count, dtype=jnp.bfloat16), [], [VMEM], [modes])
    coeffs = run(
        functools.partial(coeffs_kernel, False), "coeffs", shape(count, columns), [flat],
        [SMEM] + [VMEM] * 9, [face_rows, modes, *gaps, *got_gaps],
    )
    parts = run(
        functools.partial(coarse_kernel, cols, False), "coarse", four(depth), [],
        [VMEM] * (2 + cols), [coarse_block, turned, *gather(coeffs)],
    )
    got_parts = swap(parts)
    *first, sums = run(
        first_kernel, "first", four(depth) + four(tall) + [shape(2, columns)], [flat, wide],
        [SMEM] + [VMEM] * 17, [face_rows, operator, *gaps, *got_gaps, *parts, *got_parts],
    )
    first, images = first[:PARTNERS], first[PARTNERS:]
    got_images = swap(images)
    coeffs = run(
        functools.partial(coeffs_kernel, True), "coeffs2", shape(count + SCALE_ROWS, columns), [flat],
        [SMEM] + [VMEM] * 9, [face_rows, modes, *images, *got_images],
    )
    parts = run(
        functools.partial(coarse_kernel, cols, True), "coarse2", four(tall), [],
        [VMEM] * (2 + cols), [coarse_block, turned, *gather(coeffs)],
    )
    got_parts = swap(parts)
    *second, sums = run(
        second_kernel, "second", four(depth) + [shape(rows * cols, 8, columns)], [flat, wide],
        [SMEM] + [VMEM] * 22, [face_rows, operator, sums, *images, *got_images, *parts, *got_parts, *first],
    )
    every = lax.all_to_all(sums, ("row", "col"), 0, 0)
    out = run(
        last_kernel, "last", shape(columns, PARTNERS, depth), [wide],
        [VMEM] * 9, [every, *first, *second],
    )
    return out[None, None]


def solution(mesh):
    rows, cols = mesh.shape["row"], mesh.shape["col"]

    def body(*arrays):
        return on_device(rows, cols, *arrays)

    return jax.shard_map(
        body,
        mesh=mesh,
        in_specs=(
            P("row", "col", None, None, None),
            P("row", "col", None, None),
            P("row", "col", None, None),
            P("row", "col", None),
            P("row", "col", None),
        ),
        out_specs=P("row", "col", None, None, None),
        check_vma=False,
    )
```

time: 113 us -> 78.1 us (0.69)
  local copies, waits for them, and re-layouts: 25 us -> 2.67 us
  other arithmetic: 8.14 us -> 0 us
  Pallas kernels: 0 us -> 7.89 us
  waiting for transfers between devices: 38.4 us -> 32.6 us
  matrix products: 5.11 us -> 0 us
  starting transfers between devices: 24.1 us -> 22.9 us
    another operation x9 -> x0, local copies, waits for them, and re-layouts: 16.4 us -> none  [the longest x8 15.7 us: exchange(): jnp.stack([north + jnp.where(odd_row, got_mate_row, got_next_row), south...]
    pallas_call x0 -> x9, Pallas kernels: none -> 7.89 us  [run(): pl.pallas_call(kernel, name=name, out_shape=outs, in_specs=in_specs, out_...]
    ppermute x22, waiting for transfers between devices: 38.4 us -> 32.6 us  [the longest x16 26.2 us: swap(): lax.ppermute(field, ('row', 'col'), pairs)]
    dot_general x8 -> x0, matrix products: 5.11 us -> none  [the longest x2 2.63 us: apply_dual(): jnp.dot(operator, flat(vector * sign), preferred_element_type=jnp.float32)]
    convert_element_type x8 -> x0, local copies, waits for them, and re-layouts: 4.31 us -> none  [flat(): return field.astype(jnp.bfloat16).reshape(unknowns, columns)]
    convert_element_type x4 -> x0, other arithmetic: 3.14 us -> none  [flat(): return field.astype(jnp.bfloat16).reshape(unknowns, columns)]
    unnamed x40 -> x14, local copies, waits for them, and re-layouts: 0.08 us -> 2.67 us
    another operation x10 -> x0, other arithmetic: 2.44 us -> none  [the longest x8 2.4 us: exchange(): jnp.stack([north + jnp.where(odd_row, got_mate_row, got_next_row), south...]
  transfers between devices with their start and end apart: 22 -> 22, of which waited for: 18 -> 17; matrix products, arithmetic and copies ran while one was open for 9% -> 0% of each run, Pallas kernels for 0% -> 0%
where the time goes in v2:
time: 78.1 us; the launch traced here: 78 us
  waiting for transfers between devices  32.6 us (42%)
  starting transfers between devices  22.9 us (29%)
  blocking collectives  11.8 us (15%)
  Pallas kernels  7.89 us (10%)
  local copies, waits for them, and re-layouts  2.67 us (3%)
    ppermute x16, waiting for transfers between devices, swap(): lax.ppermute(field, ('row', 'col'), pairs)  26.2 us
    ppermute x16, starting transfers between devices, swap(): lax.ppermute(field, ('row', 'col'), pairs)  15.8 us
    all_to_all x1, blocking collectives, on_device(): every = lax.all_to_all(sums, ('row', 'col'), 0, 0)  11.8 us
    pallas_call x9, Pallas kernels, run(): pl.pallas_call(kernel, name=name, out_shape=outs, in_specs=in_specs, out_...  7.89 us
    ppermute x6, starting transfers between devices, gather(): return [block] + [lax.ppermute(block, 'col', pairs) for pairs in steps]  7.11 us
    ppermute x6, waiting for transfers between devices, gather(): return [block] + [lax.ppermute(block, 'col', pairs) for pairs in steps]  6.41 us
    unnamed x14, local copies, waits for them, and re-layouts  2.67 us
  transfers between devices with their start and end apart: 22, of which 17 were waited for; matrix products, arithmetic and copies ran while one was open for 0% of the time, Pallas kernels for 0%

profile of v2, /device:TPU:0, one launch (start us, length us, event | category | flops | bytes accessed | tf_op | source)
XLA Modules:
  0.0 78.0 jit_solution(13023133954394318126)
XLA Ops:
  0.0 1.1 %copy-done.4 = bf16[1,1,112,4,224]{4,3,2,1,0:T(4,128)(2,1)S(1)} copy-done((bf16[1,1,112,4,224]{4,3,2,1,0:T(4,128)(2,1)S(1)}, bf16[1,1,112,4,224]{4,3,2,1,0:T(4,128)(2,1)}, u32[]{:S(2)}) %copy-start.4) | copy-done | bytes 200728
  1.1 0.4 gap.1
  1.5 0.6 collective-permute-start
  2.0 2.5 %collective-permute-start.1 = (f32[224,112]{1,0:T(8,128)S(1)}, f32[224,112]{1,0:T(8,128)S(1)}, u32[]{:S(2)}, u32[]{:S(2)}) collective-permute-start(f32[224,112]{1,0:T(8,128)S(1)} %get-tuple-element.32.refs_1_), channel_id=1, source_target_pairs={{0,1},{1,0},{2,3},{3,2},{4,8},{5,9},{6,10},{7,11},{8,4},{9,5},{10,... | collective-permute-start | bytes 301064 | tf_op jit(solution)/shard_map/ppermute | solution.py:278
  4.7 2.9 %collective-permute-start.3 = (f32[224,112]{1,0:T(8,128)S(1)}, f32[224,112]{1,0:T(8,128)S(1)}, u32[]{:S(2)}, u32[]{:S(2)}) collective-permute-start(f32[224,112]{1,0:T(8,128)S(1)} %get-tuple-element.34.refs_3_), channel_id=1, source_target_pairs={{0,3},{1,2},{2,1},{3,0},{4,7},{5,6},{6,5},{7,4},{8,11},{9,10},{10,... | collective-permute-start | bytes 301064 | tf_op jit(solution)/shard_map/ppermute | solution.py:278
  7.6 2.6 %collective-permute-done.2.refs_6_ = f32[224,112]{1,0:T(8,128)S(1)} collective-permute-done((f32[224,112]{1,0:T(8,128)S(1)}, f32[224,112]{1,0:T(8,128)S(1)}, u32[]{:S(2)}, u32[]{:S(2)}) %collective-permute-start.2) | collective-permute-done | bytes 100384 | tf_op jit(solution)/shard_map/ppermute | solution.py:278
  10.1 3.6 %collective-permute-done.3.refs_7_ = f32[224,112]{1,0:T(8,128)S(1)} collective-permute-done((f32[224,112]{1,0:T(8,128)S(1)}, f32[224,112]{1,0:T(8,128)S(1)}, u32[]{:S(2)}, u32[]{:S(2)}) %collective-permute-start.3) | collective-permute-done | bytes 100384 | tf_op jit(solution)/shard_map/ppermute | solution.py:278
  13.8 0.9 %copy-done.1 = bf16[1,1,128,896]{3,2,1,0:T(8,128)(2,1)S(1)} copy-done((bf16[1,1,128,896]{3,2,1,0:T(8,128)(2,1)S(1)}, bf16[1,1,128,896]{3,2,1,0:T(8,128)(2,1)}, u32[]{:S(2)}) %copy-start.1) | copy-done | bytes 229400
  14.7 0.7 copy-done.5
  15.3 0.9 %coeffs.1.refs_0_ = f32[128,112]{1,0:T(8,128)S(1)} custom-call(s32[1,1,4]{2,1,0:T(1,128)S(1)} %copy-done.5, bf16[128,896]{1,0:T(8,128)(2,1)S(1)} %bitcast.7, f32[224,112]{1,0:T(8,128)S(1)} %get-tuple-element.31.refs_0_, f32[224,112]{1,0:T(8,128)S(1)} %get-tuple-element.32.refs_1_, f32[224,112]{1,0:T(8,128)S(1)} %get-tuple-element.33.refs_2_, ...), custom_call_target="tpu_custom_call" | custom-call | bytes 1032208 | tf_op jit(solution)/shard_map/coeffs/pallas_call | solution.py:252
  16.2 1.5 %collective-permute-start.6 = (f32[128,112]{1,0:T(8,128)S(1)}, f32[128,112]{1,0:T(8,128)S(1)}, u32[]{:S(2)}, u32[]{:S(2)}) collective-permute-start(f32[128,112]{1,0:T(8,128)S(1)} %coeffs.1.refs_0_), channel_id=1, source_target_pairs={{0,3},{1,2},{2,1},{3,0},{4,7},{5,6},{6,5},{7,4},{8,11},{9,10},{10,... | collective-permute-start | bytes 172040 | tf_op jit(solution)/shard_map/ppermute | solution.py:282
  17.7 1.5 %collective-permute-start.5 = (f32[128,112]{1,0:T(8,128)S(1)}, f32[128,112]{1,0:T(8,128)S(1)}, u32[]{:S(2)}, u32[]{:S(2)}) collective-permute-start(f32[128,112]{1,0:T(8,128)S(1)} %coeffs.1.refs_0_), channel_id=1, source_target_pairs={{0,2},{1,3},{2,0},{3,1},{4,6},{5,7},{6,4},{7,5},{8,10},{9,11},{10,... | collective-permute-start | bytes 172040 | tf_op jit(solution)/shard_map/ppermute | solution.py:282
  19.2 0.5 collective-permute-start.4
  19.8 0.1 turn.1.turned_ref
  19.9 2.2 %collective-permute-done.6.refs_3_ = f32[128,112]{1,0:T(8,128)S(1)} collective-permute-done((f32[128,112]{1,0:T(8,128)S(1)}, f32[128,112]{1,0:T(8,128)S(1)}, u32[]{:S(2)}, u32[]{:S(2)}) %collective-permute-start.6) | collective-permute-done | bytes 57376 | tf_op jit(solution)/shard_map/ppermute | solution.py:282
  22.1 0.3 collective-permute-done.5.refs_2_
  22.4 1.1 %collective-permute-done.4.refs_1_ = f32[128,112]{1,0:T(8,128)S(1)} collective-permute-done((f32[128,112]{1,0:T(8,128)S(1)}, f32[128,112]{1,0:T(8,128)S(1)}, u32[]{:S(2)}, u32[]{:S(2)}) %collective-permute-start.4) | collective-permute-done | bytes 57376 | tf_op jit(solution)/shard_map/ppermute | solution.py:282
  23.5 0.7 coarse.1
  24.2 0.6 collective-permute-start.8
  24.8 1.5 %collective-permute-start.9 = (f32[224,112]{1,0:T(8,128)S(1)}, f32[224,112]{1,0:T(8,128)S(1)}, u32[]{:S(2)}, u32[]{:S(2)}) collective-permute-start(f32[224,112]{1,0:T(8,128)S(1)} %get-tuple-element.37.refs_10_), channel_id=1, source_target_pairs={{0,1},{1,0},{2,3},{3,2},{4,5},{5,4},{6,7},{7,6},{8,9},{9,8},{10,11... | collective-permute-start | bytes 301064 | tf_op jit(solution)/shard_map/ppermute | solution.py:278
  26.3 0.3 collective-permute-start.10
  26.7 3.7 %collective-permute-done.8.refs_13_ = f32[224,112]{1,0:T(8,128)S(1)} collective-permute-done((f32[224,112]{1,0:T(8,128)S(1)}, f32[224,112]{1,0:T(8,128)S(1)}, u32[]{:S(2)}, u32[]{:S(2)}) %collective-permute-start.8) | collective-permute-done | bytes 100384 | tf_op jit(solution)/shard_map/ppermute | solution.py:278
  30.3 2.2 %collective-permute-done.9.refs_14_ = f32[224,112]{1,0:T(8,128)S(1)} collective-permute-done((f32[224,112]{1,0:T(8,128)S(1)}, f32[224,112]{1,0:T(8,128)S(1)}, u32[]{:S(2)}, u32[]{:S(2)}) %collective-permute-start.9) | collective-permute-done | bytes 100384 | tf_op jit(solution)/shard_map/ppermute | solution.py:278
  32.5 1.2 %collective-permute-done.10.refs_15_ = f32[224,112]{1,0:T(8,128)S(1)} collective-permute-done((f32[224,112]{1,0:T(8,128)S(1)}, f32[224,112]{1,0:T(8,128)S(1)}, u32[]{:S(2)}, u32[]{:S(2)}) %collective-permute-start.10) | collective-permute-done | bytes 100384 | tf_op jit(solution)/shard_map/ppermute | solution.py:278
  33.7 1.4 %first.1 = (f32[224,112]{1,0:T(8,128)S(1)}, f32[224,112]{1,0:T(8,128)S(1)}, f32[224,112]{1,0:T(8,128)S(1)}, f32[224,112]{1,0:T(8,128)S(1)}, f32[232,112]{1,0:T(8...) custom-call(s32[1,1,4]{2,1,0:T(1,128)S(1)} %copy-done.5, ...), custom_call_target="tpu_custom_call" | custom-call | bytes 3211280 | tf_op jit(solution)/shard_map/first/pallas_call | solution.py:252
  35.2 0.7 collective-permute-start.12
  35.9 1.4 %collective-permute-start.13 = (f32[232,112]{1,0:T(8,128)S(1)}, f32[232,112]{1,0:T(8,128)S(1)}, u32[]{:S(2)}, u32[]{:S(2)}) collective-permute-start(f32[232,112]{1,0:T(8,128)S(1)} %get-tuple-element.42.refs_2_), channel_id=1, source_target_pairs={{0,1},{1,0},{2,3},{3,2},{4,5},{5,4},{6,7},{7,6},{8,9},{9,8},{10,11... | collective-permute-start | bytes 311816 | tf_op jit(solution)/shard_map/ppermute | solution.py:278
  37.3 1.5 %collective-permute-start.14 = (f32[232,112]{1,0:T(8,128)S(1)}, f32[232,112]{1,0:T(8,128)S(1)}, u32[]{:S(2)}, u32[]{:S(2)}) collective-permute-start(f32[232,112]{1,0:T(8,128)S(1)} %get-tuple-element.43.refs_3_), channel_id=1, source_target_pairs={{0,3},{1,2},{2,1},{3,0},{4,7},{5,6},{6,5},{7,4},{8,11},{9,10},{10,... | collective-permute-start | bytes 311816 | tf_op jit(solution)/shard_map/ppermute | solution.py:278
  38.8 2.6 %collective-permute-done.12.refs_5_ = f32[232,112]{1,0:T(8,128)S(1)} collective-permute-done((f32[232,112]{1,0:T(8,128)S(1)}, f32[232,112]{1,0:T(8,128)S(1)}, u32[]{:S(2)}, u32[]{:S(2)}) %collective-permute-start.12) | collective-permute-done | bytes 103968 | tf_op jit(solution)/shard_map/ppermute | solution.py:278
  41.4 2.0 %collective-permute-done.13.refs_6_ = f32[232,112]{1,0:T(8,128)S(1)} collective-permute-done((f32[232,112]{1,0:T(8,128)S(1)}, f32[232,112]{1,0:T(8,128)S(1)}, u32[]{:S(2)}, u32[]{:S(2)}) %collective-permute-start.13) | collective-permute-done | bytes 103968 | tf_op jit(solution)/shard_map/ppermute | solution.py:278
  43.4 2.2 %collective-permute-done.14.refs_7_ = f32[232,112]{1,0:T(8,128)S(1)} collective-permute-done((f32[232,112]{1,0:T(8,128)S(1)}, f32[232,112]{1,0:T(8,128)S(1)}, u32[]{:S(2)}, u32[]{:S(2)}) %collective-permute-start.14) | collective-permute-done | bytes 103968 | tf_op jit(solution)/shard_map/ppermute | solution.py:278
  45.7 0.9 %coeffs2.1.refs_0_ = f32[136,112]{1,0:T(8,128)S(1)} custom-call(s32[1,1,4]{2,1,0:T(1,128)S(1)} %copy-done.5, bf16[128,896]{1,0:T(8,128)(2,1)S(1)} %bitcast.9, f32[232,112]{1,0:T(8,128)S(1)} %get-tuple-element.40.refs_0_, f32[232,112]{1,0:T(8,128)S(1)} %get-tuple-element.41.refs_1_, f32[232,112]{1,0:T(8,128)S(1)} %get-tuple-element.42.refs_2_, ...), custom_call_target="tpu_custom_call" | custom-call | bytes 1060880 | tf_op jit(solution)/shard_map/coeffs2/pallas_call | solution.py:252
  46.6 0.8 collective-permute-start.17
  47.3 1.3 %collective-permute-start.16 = (f32[136,112]{1,0:T(8,128)S(1)}, f32[136,112]{1,0:T(8,128)S(1)}, u32[]{:S(2)}, u32[]{:S(2)}) collective-permute-start(f32[136,112]{1,0:T(8,128)S(1)} %coeffs2.1.refs_0_), channel_id=1, source_target_pairs={{0,2},{1,3},{2,0},{3,1},{4,6},{5,7},{6,4},{7,5},{8,10},{9,11},{10,... | collective-permute-start | bytes 182792 | tf_op jit(solution)/shard_map/ppermute | solution.py:282
  48.6 1.5 %collective-permute-start.15 = (f32[136,112]{1,0:T(8,128)S(1)}, f32[136,112]{1,0:T(8,128)S(1)}, u32[]{:S(2)}, u32[]{:S(2)}) collective-permute-start(f32[136,112]{1,0:T(8,128)S(1)} %coeffs2.1.refs_0_), channel_id=1, source_target_pairs={{0,1},{1,0},{2,3},{3,2},{4,5},{5,4},{6,7},{7,6},{8,9},{9,8},{10,11... | collective-permute-start | bytes 182792 | tf_op jit(solution)/shard_map/ppermute | solution.py:282
  50.1 1.8 %collective-permute-done.17.refs_3_ = f32[136,112]{1,0:T(8,128)S(1)} collective-permute-done((f32[136,112]{1,0:T(8,128)S(1)}, f32[136,112]{1,0:T(8,128)S(1)}, u32[]{:S(2)}, u32[]{:S(2)}) %collective-permute-start.17) | collective-permute-done | bytes 60960 | tf_op jit(solution)/shard_map/ppermute | solution.py:282
  51.9 0.4 collective-permute-done.16.refs_2_
  52.4 0.6 collective-permute-done.15.refs_1_
  52.9 0.7 coarse2.1
  53.7 1.6 %collective-permute-start.19 = (f32[232,112]{1,0:T(8,128)S(1)}, f32[232,112]{1,0:T(8,128)S(1)}, u32[]{:S(2)}, u32[]{:S(2)}) collective-permute-start(f32[232,112]{1,0:T(8,128)S(1)} %get-tuple-element.45.refs_9_), channel_id=1, source_target_pairs={{0,1},{1,0},{2,3},{3,2},{4,8},{5,9},{6,10},{7,11},{8,4},{9,5},{10,... | collective-permute-start | bytes 311816 | tf_op jit(solution)/shard_map/ppermute | solution.py:278
  55.2 0.5 collective-permute-start.20
  55.8 1.4 %collective-permute-start.21 = (f32[232,112]{1,0:T(8,128)S(1)}, f32[232,112]{1,0:T(8,128)S(1)}, u32[]{:S(2)}, u32[]{:S(2)}) collective-permute-start(f32[232,112]{1,0:T(8,128)S(1)} %get-tuple-element.47.refs_11_), channel_id=1, source_target_pairs={{0,3},{1,2},{2,1},{3,0},{4,7},{5,6},{6,5},{7,4},{8,11},{9,10},{10,... | collective-permute-start | bytes 311816 | tf_op jit(solution)/shard_map/ppermute | solution.py:278
  57.2 2.6 %collective-permute-done.19.refs_13_ = f32[232,112]{1,0:T(8,128)S(1)} collective-permute-done((f32[232,112]{1,0:T(8,128)S(1)}, f32[232,112]{1,0:T(8,128)S(1)}, u32[]{:S(2)}, u32[]{:S(2)}) %collective-permute-start.19) | collective-permute-done | bytes 103968 | tf_op jit(solution)/shard_map/ppermute | solution.py:278
  59.9 2.0 %collective-permute-done.20.refs_14_ = f32[232,112]{1,0:T(8,128)S(1)} collective-permute-done((f32[232,112]{1,0:T(8,128)S(1)}, f32[232,112]{1,0:T(8,128)S(1)}, u32[]{:S(2)}, u32[]{:S(2)}) %collective-permute-start.20) | collective-permute-done | bytes 103968 | tf_op jit(solution)/shard_map/ppermute | solution.py:278
  61.9 1.4 %collective-permute-done.21.refs_15_ = f32[232,112]{1,0:T(8,128)S(1)} collective-permute-done((f32[232,112]{1,0:T(8,128)S(1)}, f32[232,112]{1,0:T(8,128)S(1)}, u32[]{:S(2)}, u32[]{:S(2)}) %collective-permute-start.21) | collective-permute-done | bytes 103968 | tf_op jit(solution)/shard_map/ppermute | solution.py:278
  63.3 1.6 %second.1 = (f32[224,112]{1,0:T(8,128)S(1)}, f32[224,112]{1,0:T(8,128)S(1)}, f32[224,112]{1,0:T(8,128)S(1)}, f32[224,112]{1,0:T(8,128)S(1)}, f32[32,8,112]{2,1,0:T(8,128)S(1)}) custom-call(s32[1,1,4]{2,1,0:T(1,128)S(1)} %copy-done.6, bf16[896,896]{1,0:T(8,128)(2,1)S(1)} %bitcast.6, f32[2,112]{1,0:T(2,128)S(1)} %get-tuple-element.39.sums_in_ref, ...), custom_call_target="tpu_custom_call" | custom-call | bytes 3670928 | tf_op jit(solution)/shard_map/second/pallas_call | solution.py:252
  64.9 11.8 %all_to_all.5.sums_ref = f32[32,8,112]{2,1,0:T(8,128)S(1)} all-to-all(f32[32,8,112]{2,1,0:T(8,128)S(1)} %get-tuple-element.52), channel_id=1, replica_groups=mesh['row'=8,'col'=4] {'row','col'}, dimensions={0} | all-to-all | bytes 229376 | tf_op jit(solution)/shard_map/all_to_all | solution.py:322
  76.7 1.3 %last.1 = f32[112,4,224]{2,1,0:T(4,128)} custom-call(f32[32,8,112]{2,1,0:T(8,128)S(1)} %all_to_all.5.sums_ref, f32[224,112]{1,0:T(8,128)S(1)} %get-tuple-element.48.refs_16_.refs_0_, f32[224,112]{1,0:T(8,128)S(1)} %get-tuple-element.49.refs_17_.refs_1_, f32[224,112]{1,0:T(8,128)S(1)} %get-tuple-element.50.refs_18_.refs_2_, ...), custom_call_target="tpu_custom_call" | custom-call | bytes 917504 | tf_op jit(solution)/shard_map/last/pallas_call | solution.py:252
  (20 shorter events, 0.3 us)
Async XLA Ops:
  0.0 33.7 %copy-start = (bf16[1,1,896,896]{3,2,1,0:T(8,128)(2,1)S(1)}, bf16[1,1,896,896]{3,2,1,0:T(8,128)(2,1)}, u32[]{:S(2)}) copy-start(bf16[1,1,896,896]{3,2,1,0:T(8,128)(2,1)} %param.6) | copy-start | bytes 4816900
  0.0 1.1 %copy-start.4 = (bf16[1,1,112,4,224]{4,3,2,1,0:T(4,128)(2,1)S(1)}, bf16[1,1,112,4,224]{4,3,2,1,0:T(4,128)(2,1)}, u32[]{:S(2)}) copy-start(bf16[1,1,112,4,224]{4,3,2,1,0:T(4,128)(2,1)} %param.5) | copy-start | bytes 602116
  1.5 6.1 %collective-permute-start = (f32[224,112]{1,0:T(8,128)S(1)}, f32[224,112]{1,0:T(8,128)S(1)}, u32[]{:S(2)}, u32[]{:S(2)}) collective-permute-start(f32[224,112]{1,0:T(8,128)S(1)} %get-tuple-element.31.refs_0_), channel_id=1, source_target_pairs={{0,4},{1,5},{2,6},{3,7},{4,0},{5,1},{6,2},{7,3},{8,12},{9,13},{10,... | collective-permute-start | bytes 301064 | tf_op jit(solution)/shard_map/ppermute | solution.py:278
  2.0 5.5 %collective-permute-start.1 = (f32[224,112]{1,0:T(8,128)S(1)}, f32[224,112]{1,0:T(8,128)S(1)}, u32[]{:S(2)}, u32[]{:S(2)}) collective-permute-start(f32[224,112]{1,0:T(8,128)S(1)} %get-tuple-element.32.refs_1_), channel_id=1, source_target_pairs={{0,1},{1,0},{2,3},{3,2},{4,8},{5,9},{6,10},{7,11},{8,4},{9,5},{10,... | collective-permute-start | bytes 301064 | tf_op jit(solution)/shard_map/ppermute | solution.py:278
  4.6 5.5 %collective-permute-start.2 = (f32[224,112]{1,0:T(8,128)S(1)}, f32[224,112]{1,0:T(8,128)S(1)}, u32[]{:S(2)}, u32[]{:S(2)}) collective-permute-start(f32[224,112]{1,0:T(8,128)S(1)} %get-tuple-element.33.refs_2_), channel_id=1, source_target_pairs={{0,1},{1,0},{2,3},{3,2},{4,5},{5,4},{6,7},{7,6},{8,9},{9,8},{10,11... | collective-permute-start | bytes 301064 | tf_op jit(solution)/shard_map/ppermute | solution.py:278
  4.7 9.1 %collective-permute-start.3 = (f32[224,112]{1,0:T(8,128)S(1)}, f32[224,112]{1,0:T(8,128)S(1)}, u32[]{:S(2)}, u32[]{:S(2)}) collective-permute-start(f32[224,112]{1,0:T(8,128)S(1)} %get-tuple-element.34.refs_3_), channel_id=1, source_target_pairs={{0,3},{1,2},{2,1},{3,0},{4,7},{5,6},{6,5},{7,4},{8,11},{9,10},{10,... | collective-permute-start | bytes 301064 | tf_op jit(solution)/shard_map/ppermute | solution.py:278
  13.8 0.9 %copy-start.1 = (bf16[1,1,128,896]{3,2,1,0:T(8,128)(2,1)S(1)}, bf16[1,1,128,896]{3,2,1,0:T(8,128)(2,1)}, u32[]{:S(2)}) copy-start(bf16[1,1,128,896]{3,2,1,0:T(8,128)(2,1)} %param.7) | copy-start | bytes 688132
  14.7 0.7 copy-start.5
  15.3 8.1 %copy-start.3 = (f32[1,128,512]{2,1,0:T(8,128)S(1)}, f32[1,128,512]{2,1,0:T(8,128)}, u32[]{:S(2)}) copy-start(f32[1,128,512]{2,1,0:T(8,128)} %param.8) | copy-start | bytes 786436
  16.2 5.9 %collective-permute-start.6 = (f32[128,112]{1,0:T(8,128)S(1)}, f32[128,112]{1,0:T(8,128)S(1)}, u32[]{:S(2)}, u32[]{:S(2)}) collective-permute-start(f32[128,112]{1,0:T(8,128)S(1)} %coeffs.1.refs_0_), channel_id=1, source_target_pairs={{0,3},{1,2},{2,1},{3,0},{4,7},{5,6},{6,5},{7,4},{8,11},{9,10},{10,... | collective-permute-start | bytes 172040 | tf_op jit(solution)/shard_map/ppermute | solution.py:282
  17.7 4.7 %collective-permute-start.5 = (f32[128,112]{1,0:T(8,128)S(1)}, f32[128,112]{1,0:T(8,128)S(1)}, u32[]{:S(2)}, u32[]{:S(2)}) collective-permute-start(f32[128,112]{1,0:T(8,128)S(1)} %coeffs.1.refs_0_), channel_id=1, source_target_pairs={{0,2},{1,3},{2,0},{3,1},{4,6},{5,7},{6,4},{7,5},{8,10},{9,11},{10,... | collective-permute-start | bytes 172040 | tf_op jit(solution)/shard_map/ppermute | solution.py:282
  19.2 4.3 %collective-permute-start.4 = (f32[128,112]{1,0:T(8,128)S(1)}, f32[128,112]{1,0:T(8,128)S(1)}, u32[]{:S(2)}, u32[]{:S(2)}) collective-permute-start(f32[128,112]{1,0:T(8,128)S(1)} %coeffs.1.refs_0_), channel_id=1, source_target_pairs={{0,1},{1,0},{2,3},{3,2},{4,5},{5,4},{6,7},{7,6},{8,9},{9,8},{10,11... | collective-permute-start | bytes 172040 | tf_op jit(solution)/shard_map/ppermute | solution.py:282
  24.2 2.5 %collective-permute-start.7 = (f32[224,112]{1,0:T(8,128)S(1)}, f32[224,112]{1,0:T(8,128)S(1)}, u32[]{:S(2)}, u32[]{:S(2)}) collective-permute-start(f32[224,112]{1,0:T(8,128)S(1)} %get-tuple-element.35.refs_8_), channel_id=1, source_target_pairs={{0,4},{1,5},{2,6},{3,7},{4,0},{5,1},{6,2},{7,3},{8,12},{9,13},{10,... | collective-permute-start | bytes 301064 | tf_op jit(solution)/shard_map/ppermute | solution.py:278
  24.2 6.1 %collective-permute-start.8 = (f32[224,112]{1,0:T(8,128)S(1)}, f32[224,112]{1,0:T(8,128)S(1)}, u32[]{:S(2)}, u32[]{:S(2)}) collective-permute-start(f32[224,112]{1,0:T(8,128)S(1)} %get-tuple-element.36.refs_9_), channel_id=1, source_target_pairs={{0,1},{1,0},{2,3},{3,2},{4,8},{5,9},{6,10},{7,11},{8,4},{9,5},{10,... | collective-permute-start | bytes 301064 | tf_op jit(solution)/shard_map/ppermute | solution.py:278
  24.8 7.7 %collective-permute-start.9 = (f32[224,112]{1,0:T(8,128)S(1)}, f32[224,112]{1,0:T(8,128)S(1)}, u32[]{:S(2)}, u32[]{:S(2)}) collective-permute-start(f32[224,112]{1,0:T(8,128)S(1)} %get-tuple-element.37.refs_10_), channel_id=1, source_target_pairs={{0,1},{1,0},{2,3},{3,2},{4,5},{5,4},{6,7},{7,6},{8,9},{9,8},{10,11... | collective-permute-start | bytes 301064 | tf_op jit(solution)/shard_map/ppermute | solution.py:278
  26.3 7.4 %collective-permute-start.10 = (f32[224,112]{1,0:T(8,128)S(1)}, f32[224,112]{1,0:T(8,128)S(1)}, u32[]{:S(2)}, u32[]{:S(2)}) collective-permute-start(f32[224,112]{1,0:T(8,128)S(1)} %get-tuple-element.38.refs_11_), channel_id=1, source_target_pairs={{0,3},{1,2},{2,1},{3,0},{4,7},{5,6},{6,5},{7,4},{8,11},{9,10},{10,... | collective-permute-start | bytes 301064 | tf_op jit(solution)/shard_map/ppermute | solution.py:278
  33.7 12.0 %copy-start.2 = (bf16[1,1,128,896]{3,2,1,0:T(8,128)(2,1)S(1)}, bf16[1,1,128,896]{3,2,1,0:T(8,128)(2,1)}, u32[]{:S(2)}) copy-start(bf16[1,1,128,896]{3,2,1,0:T(8,128)(2,1)} %param.7) | copy-start | bytes 688132
  35.1 28.2 %copy-start.6 = (s32[1,1,4]{2,1,0:T(1,128)S(1)}, s32[1,1,4]{2,1,0:T(1,128)}, u32[]{:S(2)}) copy-start(s32[1,1,4]{2,1,0:T(1,128)} %rows_ref.7) | copy-start | bytes 52
  35.1 3.7 %collective-permute-start.11 = (f32[232,112]{1,0:T(8,128)S(1)}, f32[232,112]{1,0:T(8,128)S(1)}, u32[]{:S(2)}, u32[]{:S(2)}) collective-permute-start(f32[232,112]{1,0:T(8,128)S(1)} %get-tuple-element.40.refs_0_), channel_id=1, source_target_pairs={{0,4},{1,5},{2,6},{3,7},{4,0},{5,1},{6,2},{7,3},{8,12},{9,13},{10,... | collective-permute-start | bytes 311816 | tf_op jit(solution)/shard_map/ppermute | solution.py:278
  35.2 6.2 %collective-permute-start.12 = (f32[232,112]{1,0:T(8,128)S(1)}, f32[232,112]{1,0:T(8,128)S(1)}, u32[]{:S(2)}, u32[]{:S(2)}) collective-permute-start(f32[232,112]{1,0:T(8,128)S(1)} %get-tuple-element.41.refs_1_), channel_id=1, source_target_pairs={{0,1},{1,0},{2,3},{3,2},{4,8},{5,9},{6,10},{7,11},{8,4},{9,5},{10,... | collective-permute-start | bytes 311816 | tf_op jit(solution)/shard_map/ppermute | solution.py:278
  35.9 7.5 %collective-permute-start.13 = (f32[232,112]{1,0:T(8,128)S(1)}, f32[232,112]{1,0:T(8,128)S(1)}, u32[]{:S(2)}, u32[]{:S(2)}) collective-permute-start(f32[232,112]{1,0:T(8,128)S(1)} %get-tuple-element.42.refs_2_), channel_id=1, source_target_pairs={{0,1},{1,0},{2,3},{3,2},{4,5},{5,4},{6,7},{7,6},{8,9},{9,8},{10,11... | collective-permute-start | bytes 311816 | tf_op jit(solution)/shard_map/ppermute | solution.py:278
  37.3 8.3 %collective-permute-start.14 = (f32[232,112]{1,0:T(8,128)S(1)}, f32[232,112]{1,0:T(8,128)S(1)}, u32[]{:S(2)}, u32[]{:S(2)}) collective-permute-start(f32[232,112]{1,0:T(8,128)S(1)} %get-tuple-element.43.refs_3_), channel_id=1, source_target_pairs={{0,3},{1,2},{2,1},{3,0},{4,7},{5,6},{6,5},{7,4},{8,11},{9,10},{10,... | collective-permute-start | bytes 311816 | tf_op jit(solution)/shard_map/ppermute | solution.py:278
  46.6 5.4 %collective-permute-start.17 = (f32[136,112]{1,0:T(8,128)S(1)}, f32[136,112]{1,0:T(8,128)S(1)}, u32[]{:S(2)}, u32[]{:S(2)}) collective-permute-start(f32[136,112]{1,0:T(8,128)S(1)} %coeffs2.1.refs_0_), channel_id=1, source_target_pairs={{0,3},{1,2},{2,1},{3,0},{4,7},{5,6},{6,5},{7,4},{8,11},{9,10},{10,... | collective-permute-start | bytes 182792 | tf_op jit(solution)/shard_map/ppermute | solution.py:282
  47.3 5.1 %collective-permute-start.16 = (f32[136,112]{1,0:T(8,128)S(1)}, f32[136,112]{1,0:T(8,128)S(1)}, u32[]{:S(2)}, u32[]{:S(2)}) collective-permute-start(f32[136,112]{1,0:T(8,128)S(1)} %coeffs2.1.refs_0_), channel_id=1, source_target_pairs={{0,2},{1,3},{2,0},{3,1},{4,6},{5,7},{6,4},{7,5},{8,10},{9,11},{10,... | collective-permute-start | bytes 182792 | tf_op jit(solution)/shard_map/ppermute | solution.py:282
  48.6 4.3 %collective-permute-start.15 = (f32[136,112]{1,0:T(8,128)S(1)}, f32[136,112]{1,0:T(8,128)S(1)}, u32[]{:S(2)}, u32[]{:S(2)}) collective-permute-start(f32[136,112]{1,0:T(8,128)S(1)} %coeffs2.1.refs_0_), channel_id=1, source_target_pairs={{0,1},{1,0},{2,3},{3,2},{4,5},{5,4},{6,7},{7,6},{8,9},{9,8},{10,11... | collective-permute-start | bytes 182792 | tf_op jit(solution)/shard_map/ppermute | solution.py:282
  53.6 3.6 %collective-permute-start.18 = (f32[232,112]{1,0:T(8,128)S(1)}, f32[232,112]{1,0:T(8,128)S(1)}, u32[]{:S(2)}, u32[]{:S(2)}) collective-permute-start(f32[232,112]{1,0:T(8,128)S(1)} %get-tuple-element.44.refs_8_), channel_id=1, source_target_pairs={{0,4},{1,5},{2,6},{3,7},{4,0},{5,1},{6,2},{7,3},{8,12},{9,13},{10,... | collective-permute-start | bytes 311816 | tf_op jit(solution)/shard_map/ppermute | solution.py:278
  53.7 6.2 %collective-permute-start.19 = (f32[232,112]{1,0:T(8,128)S(1)}, f32[232,112]{1,0:T(8,128)S(1)}, u32[]{:S(2)}, u32[]{:S(2)}) collective-permute-start(f32[232,112]{1,0:T(8,128)S(1)} %get-tuple-element.45.refs_9_), channel_id=1, source_target_pairs={{0,1},{1,0},{2,3},{3,2},{4,8},{5,9},{6,10},{7,11},{8,4},{9,5},{10,... | collective-permute-start | bytes 311816 | tf_op jit(solution)/shard_map/ppermute | solution.py:278
  55.2 6.6 %collective-permute-start.20 = (f32[232,112]{1,0:T(8,128)S(1)}, f32[232,112]{1,0:T(8,128)S(1)}, u32[]{:S(2)}, u32[]{:S(2)}) collective-permute-start(f32[232,112]{1,0:T(8,128)S(1)} %get-tuple-element.46.refs_10_), channel_id=1, source_target_pairs={{0,1},{1,0},{2,3},{3,2},{4,5},{5,4},{6,7},{7,6},{8,9},{9,8},{10,11... | collective-permute-start | bytes 311816 | tf_op jit(solution)/shard_map/ppermute | solution.py:278
  55.8 7.5 %collective-permute-start.21 = (f32[232,112]{1,0:T(8,128)S(1)}, f32[232,112]{1,0:T(8,128)S(1)}, u32[]{:S(2)}, u32[]{:S(2)}) collective-permute-start(f32[232,112]{1,0:T(8,128)S(1)} %get-tuple-element.47.refs_11_), channel_id=1, source_target_pairs={{0,3},{1,2},{2,1},{3,0},{4,7},{5,6},{6,5},{7,4},{8,11},{9,10},{10,... | collective-permute-start | bytes 311816 | tf_op jit(solution)/shard_map/ppermute | solution.py:278

commit v3 on v2

--- a/solution.py
+++ b/solution.py
@@ -20,26 +20,28 @@
                 pairs.append((r * cols + c, r2 * cols + c2))
         return pairs
 
+    idle = 2 if cols % 4 == 0 else 1
+
     def across_rows(r, c):
         other = r + 1 if r % 2 else r - 1
-        return (other, c) if 0 <= other < rows else (r, c ^ 1)
+        return (other, c) if 0 <= other < rows else (r, c ^ idle)
 
     def across_cols(r, c):
         other = c + 1 if c % 2 else c - 1
-        return r, other % cols
+        return (r, other) if 0 <= other < cols else (r ^ 1, c)
 
     return [
+        table(across_cols),
+        table(lambda r, c: (r, c ^ 1)),
+        table(across_rows),
         table(lambda r, c: (r ^ 1, c)),
-        table(across_rows),
-        table(lambda r, c: (r, c ^ 1)),
-        table(across_cols),
     ]
 
 
 def faces_of_partners():
     odd_row = lax.rem(lax.axis_index("row"), 2)
     odd_col = lax.rem(lax.axis_index("col"), 2)
-    return [1 - odd_row, odd_row, 3 - odd_col, 2 + odd_col]
+    return [2 + odd_col, 3 - odd_col, odd_row, 1 - odd_row]
 
 
 def face_slice(face, depth):
@@ -70,8 +72,21 @@
         out_ref[...] = field[face_slice(face, depth), :]
 
 
-def turn_kernel(modes_ref, out_ref):
-    out_ref[...] = modes_ref[...].astype(jnp.float32).T.astype(jnp.bfloat16)
+def prepare_kernel(rows_hbm, modes_hbm, coarse_hbm, after_ref, counts_ref, modes_ref, coarse_ref, turned_ref, rows, sems):
+    del after_ref
+    copies = [
+        pltpu.make_async_copy(rows_hbm, rows, sems.at[0]),
+        pltpu.make_async_copy(modes_hbm, modes_ref, sems.at[1]),
+        pltpu.make_async_copy(coarse_hbm, coarse_ref, sems.at[2]),
+    ]
+    for copy in copies:
+        copy.start()
+    copies[0].wait()
+    for partner, face in enumerate(faces_of_partners()):
+        counts_ref[partner : partner + 1, :] = jnp.full((1, counts_ref.shape[1]), rows[0, 0, face], jnp.int32)
+    copies[1].wait()
+    turned_ref[...] = modes_ref[...].astype(jnp.float32).T.astype(jnp.bfloat16)
+    copies[2].wait()
 
 
 def read_pair(mine_ref, got_ref, count, scaled):
@@ -107,14 +122,14 @@
     return fields, top
 
 
-def counts_of(rows_ref, faces):
-    return [rows_ref[0, 0, face] for face in faces]
-
-
-def coeffs_kernel(scaled, rows_ref, modes_ref, *refs):
+def counts_of(counts_ref):
+    return [counts_ref[partner : partner + 1, :] for partner in range(PARTNERS)]
+
+
+def coeffs_kernel(scaled, counts_ref, modes_ref, *refs):
     mine_refs, got_refs, out_ref, flat = refs[:4], refs[4:8], refs[8], refs[9]
     faces = faces_of_partners()
-    fields, top = glued(mine_refs, got_refs, counts_of(rows_ref, faces), scaled)
+    fields, top = glued(mine_refs, got_refs, counts_of(counts_ref), scaled)
     depth = fields[0].shape[0]
     for face, field in zip(faces, fields):
         flat[face_slice(face, depth), :] = field.astype(jnp.bfloat16)
@@ -160,11 +175,11 @@
     return [image[face_slice(face, depth), :] * face_sign(face) for face in faces]
 
 
-def first_kernel(rows_ref, operator_ref, *refs):
+def first_kernel(counts_ref, operator_ref, *refs):
     mine_refs, got_refs, part_refs, got_part_refs = refs[:4], refs[4:8], refs[8:12], refs[12:16]
     vector_refs, image_refs, sums_ref, flat, image = refs[16:20], refs[20:24], refs[24], refs[25], refs[26]
     faces = faces_of_partners()
-    counts = counts_of(rows_ref, faces)
+    counts = counts_of(counts_ref)
     residuals, _ = glued(mine_refs, got_refs, counts, False)
     parts, _ = glued(part_refs, got_part_refs, counts, False)
     fields = [residual - part for residual, part in zip(residuals, parts)]
@@ -185,11 +200,11 @@
     sums_ref[1:2, :] = curvature
 
 
-def second_kernel(rows_ref, operator_ref, sums_in_ref, *refs):
+def second_kernel(counts_ref, operator_ref, sums_in_ref, *refs):
     mine_refs, got_refs, part_refs, got_part_refs, first_refs = (refs[4 * i : 4 * i + 4] for i in range(5))
     vector_refs, sums_ref, flat, image = refs[20:24], refs[24], refs[25], refs[26]
     faces = faces_of_partners()
-    counts = counts_of(rows_ref, faces)
+    counts = counts_of(counts_ref)
     images, image_scale = glued(mine_refs, got_refs, counts, True)
     parts, part_scale = glued(part_refs, got_part_refs, counts, True)
     top = jnp.maximum(image_scale, part_scale)
@@ -244,7 +259,7 @@
 
 
 VMEM = pl.BlockSpec(memory_space=pltpu.VMEM)
-SMEM = pl.BlockSpec(memory_space=pltpu.SMEM)
+HBM = pl.BlockSpec(memory_space=pltpu.HBM)
 
 
 def run(kernel, name, outs, scratch, in_specs, args, flops=0):
@@ -290,10 +305,20 @@
 
     gaps = run(gap_kernel, "gap", four(depth), [wide], [VMEM], [gap])
     got_gaps = swap(gaps)
-    turned = run(turn_kernel, "turn", shape(unknowns, count, dtype=jnp.bfloat16), [], [VMEM], [modes])
+    counts, modes, coarse_block, turned = run(
+        prepare_kernel, "prepare",
+        [
+            shape(PARTNERS, columns, dtype=jnp.int32),
+            shape(*modes.shape, dtype=modes.dtype),
+            shape(*coarse_block.shape),
+            shape(unknowns, count, dtype=modes.dtype),
+        ],
+        [pltpu.SMEM(face_rows.shape, jnp.int32), pltpu.SemaphoreType.DMA((3,))],
+        [HBM] * 3 + [VMEM], [face_rows, modes, coarse_block, gaps[PARTNERS - 1]],
+    )
     coeffs = run(
         functools.partial(coeffs_kernel, False), "coeffs", shape(count, columns), [flat],
-        [SMEM] + [VMEM] * 9, [face_rows, modes, *gaps, *got_gaps],
+        [VMEM] * 10, [counts, modes, *gaps, *got_gaps],
     )
     parts = run(
         functools.partial(coarse_kernel, cols, False), "coarse", four(depth), [],
@@ -302,13 +327,13 @@
     got_parts = swap(parts)
     *first, sums = run(
         first_kernel, "first", four(depth) + four(tall) + [shape(2, columns)], [flat, wide],
-        [SMEM] + [VMEM] * 17, [face_rows, operator, *gaps, *got_gaps, *parts, *got_parts],
+        [VMEM] * 18, [counts, operator, *gaps, *got_gaps, *parts, *got_parts],
     )
     first, images = first[:PARTNERS], first[PARTNERS:]
     got_images = swap(images)
     coeffs = run(
         functools.partial(coeffs_kernel, True), "coeffs2", shape(count + SCALE_ROWS, columns), [flat],
-        [SMEM] + [VMEM] * 9, [face_rows, modes, *images, *got_images],
+        [VMEM] * 10, [counts, modes, *images, *got_images],
     )
     parts = run(
         functools.partial(coarse_kernel, cols, True), "coarse2", four(tall), [],
@@ -317,7 +342,7 @@
     got_parts = swap(parts)
     *second, sums = run(
         second_kernel, "second", four(depth) + [shape(rows * cols, 8, columns)], [flat, wide],
-        [SMEM] + [VMEM] * 22, [face_rows, operator, sums, *images, *got_images, *parts, *got_parts, *first],
+        [VMEM] * 23, [counts, operator, sums, *images, *got_images, *parts, *got_parts, *first],
     )
     every = lax.all_to_all(sums, ("row", "col"), 0, 0)
     out = run(

time: 78.1 us -> 64.3 us (0.82)
  waiting for transfers between devices: 32.6 us -> 17.1 us
  starting transfers between devices: 22.9 us -> 25.1 us
  Pallas kernels: 7.89 us -> 6.31 us
  local copies, waits for them, and re-layouts: 2.67 us -> 3.6 us
    ppermute x16, waiting for transfers between devices: 26.2 us -> 11.1 us  [swap(): lax.ppermute(field, ('row', 'col'), pairs)]
    ppermute x16, starting transfers between devices: 15.8 us -> 18 us  [swap(): lax.ppermute(field, ('row', 'col'), pairs)]
    pallas_call x9, Pallas kernels: 7.89 us -> 6.31 us  [run(): pl.pallas_call(kernel, name=name, out_shape=outs, in_specs=in_specs, out_...]
    unnamed x14 -> x10, local copies, waits for them, and re-layouts: 2.67 us -> 3.6 us
  transfers between devices with their start and end apart: 22 -> 22, of which waited for: 17 -> 13; matrix products, arithmetic and copies ran while one was open for 0% -> 0% of each run, Pallas kernels for 0% -> 1%
where the time goes in v3:
time: 64.3 us; the launch traced here: 64.1 us
  starting transfers between devices  25.1 us (39%)
  waiting for transfers between devices  17.1 us (27%)
  blocking collectives  11.8 us (18%)
  Pallas kernels  6.31 us (10%)
  local copies, waits for them, and re-layouts  3.6 us (6%)
    ppermute x16, starting transfers between devices, swap(): lax.ppermute(field, ('row', 'col'), pairs)  18 us
    all_to_all x1, blocking collectives, on_device(): every = lax.all_to_all(sums, ('row', 'col'), 0, 0)  11.8 us
    ppermute x16, waiting for transfers between devices, swap(): lax.ppermute(field, ('row', 'col'), pairs)  11.1 us
    ppermute x6, starting transfers between devices, gather(): return [block] + [lax.ppermute(block, 'col', pairs) for pairs in steps]  7.11 us
    pallas_call x9, Pallas kernels, run(): pl.pallas_call(kernel, name=name, out_shape=outs, in_specs=in_specs, out_...  6.31 us
    ppermute x6, waiting for transfers between devices, gather(): return [block] + [lax.ppermute(block, 'col', pairs) for pairs in steps]  5.92 us
    unnamed x10, local copies, waits for them, and re-layouts  3.6 us
  transfers between devices with their start and end apart: 22, of which 13 were waited for; matrix products, arithmetic and copies ran while one was open for 0% of the time, Pallas kernels for 1%

profile of v3, /device:TPU:0, one launch (start us, length us, event | category | flops | bytes accessed | tf_op | source)
XLA Modules:
  0.0 64.1 jit_solution(7933569042853952404)
XLA Ops:
  0.0 1.1 %copy-done.2 = bf16[1,1,112,4,224]{4,3,2,1,0:T(4,128)(2,1)S(1)} copy-done((bf16[1,1,112,4,224]{4,3,2,1,0:T(4,128)(2,1)S(1)}, bf16[1,1,112,4,224]{4,3,2,1,0:T(4,128)(2,1)}, u32[]{:S(2)}) %copy-start.2) | copy-done | bytes 200728
  1.1 0.4 gap.1
  1.5 0.6 collective-permute-start
  2.0 4.0 %collective-permute-start.1 = (f32[224,112]{1,0:T(8,128)S(1)}, f32[224,112]{1,0:T(8,128)S(1)}, u32[]{:S(2)}, u32[]{:S(2)}) collective-permute-start(f32[224,112]{1,0:T(8,128)S(1)} %get-tuple-element.38.refs_1_), channel_id=1, source_target_pairs={{0,1},{1,0},{2,3},{3,2},{4,5},{5,4},{6,7},{7,6},{8,9},{9,8},{10,11... | collective-permute-start | bytes 301064 | tf_op jit(solution)/shard_map/ppermute | solution.py:293
  6.0 0.1 collective-permute-start.2
  6.1 1.6 %collective-permute-start.3 = (f32[224,112]{1,0:T(8,128)S(1)}, f32[224,112]{1,0:T(8,128)S(1)}, u32[]{:S(2)}, u32[]{:S(2)}) collective-permute-start(f32[224,112]{1,0:T(8,128)S(1)} %get-tuple-element.35.after_ref.refs_3_), channel_id=1, source_target_pairs={{0,4},{1,5},{2,6},{3,7},{4,0},{5,1},{6,2},{7,3},{8,12},{9,13},{10,... | collective-permute-start | bytes 301064 | tf_op jit(solution)/shard_map/ppermute | solution.py:293
  7.7 0.9 %copy-done.1 = f32[1,128,512]{2,1,0:T(8,128)S(1)} copy-done((f32[1,128,512]{2,1,0:T(8,128)S(1)}, f32[1,128,512]{2,1,0:T(8,128)}, u32[]{:S(2)}) %copy-start.1) | copy-done | bytes 262168
  8.6 0.9 %copy-done.3 = bf16[1,1,128,896]{3,2,1,0:T(8,128)(2,1)S(1)} copy-done((bf16[1,1,128,896]{3,2,1,0:T(8,128)(2,1)S(1)}, bf16[1,1,128,896]{3,2,1,0:T(8,128)(2,1)}, u32[]{:S(2)}) %copy-start.3) | copy-done | bytes 229400
  9.6 0.7 %copy-done.4 = s32[1,1,4]{2,1,0:T(1,128)S(1)} copy-done((s32[1,1,4]{2,1,0:T(1,128)S(1)}, s32[1,1,4]{2,1,0:T(1,128)}, u32[]{:S(2)}) %copy-start.4) | copy-done | bytes 40
  10.2 0.7 %prepare.1 = (s32[4,112]{1,0:T(4,128)S(1)}, bf16[128,896]{1,0:T(8,128)(2,1)S(1)}, f32[128,512]{1,0:T(8,128)S(1)}, bf16[896,128]{1,0:T(8,128)(2,1)S(1)}) custom-call(s32[1,1,4]{2,1,0:T(1,128)S(1)} %copy-done.4, bf16[128,896]{1,0:T(8,128)(2,1)S(1)} %bitcast.9, f32[128,512]{1,0:T(8,128)S(1)} %bitcast.7, f32[224,112]{1,0:T(8,128)S(1)} %get-tuple-element.35.after_ref.refs_3_), custom_call_target="tpu_custom_call" | custom-call | bytes 591888 | tf_op jit(solution)/shard_map/prepare/pallas_call | solution.py:267
  11.0 0.3 collective-permute-done.1.refs_5_
  11.3 0.3 coeffs.1.refs_0_
  11.7 1.5 %collective-permute-start.6 = (f32[128,112]{1,0:T(8,128)S(1)}, f32[128,112]{1,0:T(8,128)S(1)}, u32[]{:S(2)}, u32[]{:S(2)}) collective-permute-start(f32[128,112]{1,0:T(8,128)S(1)} %coeffs.1.refs_0_), channel_id=1, source_target_pairs={{0,3},{1,2},{2,1},{3,0},{4,7},{5,6},{6,5},{7,4},{8,11},{9,10},{10,... | collective-permute-start | bytes 172040 | tf_op jit(solution)/shard_map/ppermute | solution.py:297
  13.2 0.4 collective-permute-start.5
  13.6 1.6 %collective-permute-start.4 = (f32[128,112]{1,0:T(8,128)S(1)}, f32[128,112]{1,0:T(8,128)S(1)}, u32[]{:S(2)}, u32[]{:S(2)}) collective-permute-start(f32[128,112]{1,0:T(8,128)S(1)} %coeffs.1.refs_0_), channel_id=1, source_target_pairs={{0,1},{1,0},{2,3},{3,2},{4,5},{5,4},{6,7},{7,6},{8,9},{9,8},{10,11... | collective-permute-start | bytes 172040 | tf_op jit(solution)/shard_map/ppermute | solution.py:297
  15.2 2.2 %collective-permute-done.6.refs_3_ = f32[128,112]{1,0:T(8,128)S(1)} collective-permute-done((f32[128,112]{1,0:T(8,128)S(1)}, f32[128,112]{1,0:T(8,128)S(1)}, u32[]{:S(2)}, u32[]{:S(2)}) %collective-permute-start.6) | collective-permute-done | bytes 57376 | tf_op jit(solution)/shard_map/ppermute | solution.py:297
  17.4 0.3 collective-permute-done.5.refs_2_
  17.8 0.1 collective-permute-done.4.refs_1_
  17.9 0.7 %coarse.1 = (f32[224,112]{1,0:T(8,128)S(1)}, f32[224,112]{1,0:T(8,128)S(1)}, f32[224,112]{1,0:T(8,128)S(1)}, f32[224,112]{1,0:T(8,128)S(1)}) custom-call(f32[128,512]{1,0:T(8,128)S(1)} %get-tuple-element.40.coarse_ref, bf16[896,128]{1,0:T(8,128)(2,1)S(1)} %get-tuple-element.41.turned_ref, f32[128,112]{1,0:T(8,128)S(1)} %coeffs.1.refs_0_, ...), custom_call_target="tpu_custom_call" | custom-call | bytes 720896 | tf_op jit(solution)/shard_map/coarse/pallas_call | solution.py:267
  18.5 0.1 collective-permute-start.7
  18.6 3.0 %collective-permute-start.8 = (f32[224,112]{1,0:T(8,128)S(1)}, f32[224,112]{1,0:T(8,128)S(1)}, u32[]{:S(2)}, u32[]{:S(2)}) collective-permute-start(f32[224,112]{1,0:T(8,128)S(1)} %get-tuple-element.44.refs_9_), channel_id=1, source_target_pairs={{0,1},{1,0},{2,3},{3,2},{4,5},{5,4},{6,7},{7,6},{8,9},{9,8},{10,11... | collective-permute-start | bytes 301064 | tf_op jit(solution)/shard_map/ppermute | solution.py:293
  21.6 0.0 collective-permute-start.9
  21.7 1.7 %collective-permute-start.10 = (f32[224,112]{1,0:T(8,128)S(1)}, f32[224,112]{1,0:T(8,128)S(1)}, u32[]{:S(2)}, u32[]{:S(2)}) collective-permute-start(f32[224,112]{1,0:T(8,128)S(1)} %get-tuple-element.46.refs_11_), channel_id=1, source_target_pairs={{0,4},{1,5},{2,6},{3,7},{4,0},{5,1},{6,2},{7,3},{8,12},{9,13},{10,... | collective-permute-start | bytes 301064 | tf_op jit(solution)/shard_map/ppermute | solution.py:293
  23.3 2.8 %collective-permute-done.8.refs_13_ = f32[224,112]{1,0:T(8,128)S(1)} collective-permute-done((f32[224,112]{1,0:T(8,128)S(1)}, f32[224,112]{1,0:T(8,128)S(1)}, u32[]{:S(2)}, u32[]{:S(2)}) %collective-permute-start.8) | collective-permute-done | bytes 100384 | tf_op jit(solution)/shard_map/ppermute | solution.py:293
  26.1 0.3 collective-permute-done.9.refs_14_
  26.4 0.9 %first.1 = (f32[224,112]{1,0:T(8,128)S(1)}, f32[224,112]{1,0:T(8,128)S(1)}, f32[224,112]{1,0:T(8,128)S(1)}, f32[224,112]{1,0:T(8,128)S(1)}, f32[232,112]{1,0:T(8...) custom-call(s32[4,112]{1,0:T(4,128)S(1)} %get-tuple-element.36.count, ...), custom_call_target="tpu_custom_call" | custom-call | bytes 3213056 | tf_op jit(solution)/shard_map/first/pallas_call | solution.py:267
  27.3 0.1 collective-permute-start.11
  27.4 2.4 %collective-permute-start.12 = (f32[232,112]{1,0:T(8,128)S(1)}, f32[232,112]{1,0:T(8,128)S(1)}, u32[]{:S(2)}, u32[]{:S(2)}) collective-permute-start(f32[232,112]{1,0:T(8,128)S(1)} %get-tuple-element.49.refs_1_), channel_id=1, source_target_pairs={{0,1},{1,0},{2,3},{3,2},{4,5},{5,4},{6,7},{7,6},{8,9},{9,8},{10,11... | collective-permute-start | bytes 311816 | tf_op jit(solution)/shard_map/ppermute | solution.py:293
  29.8 0.0 collective-permute-start.13
  29.8 0.8 %collective-permute-start.14 = (f32[232,112]{1,0:T(8,128)S(1)}, f32[232,112]{1,0:T(8,128)S(1)}, u32[]{:S(2)}, u32[]{:S(2)}) collective-permute-start(f32[232,112]{1,0:T(8,128)S(1)} %get-tuple-element.51.refs_3_), channel_id=1, source_target_pairs={{0,4},{1,5},{2,6},{3,7},{4,0},{5,1},{6,2},{7,3},{8,12},{9,13},{10,... | collective-permute-start | bytes 311816 | tf_op jit(solution)/shard_map/ppermute | solution.py:293
  30.6 3.7 %collective-permute-done.12.refs_5_ = f32[232,112]{1,0:T(8,128)S(1)} collective-permute-done((f32[232,112]{1,0:T(8,128)S(1)}, f32[232,112]{1,0:T(8,128)S(1)}, u32[]{:S(2)}, u32[]{:S(2)}) %collective-permute-start.12) | collective-permute-done | bytes 103968 | tf_op jit(solution)/shard_map/ppermute | solution.py:293
  34.3 0.3 collective-permute-done.13.refs_6_
  34.7 0.3 coeffs2.1.refs_0_
  35.0 1.5 %collective-permute-start.17 = (f32[136,112]{1,0:T(8,128)S(1)}, f32[136,112]{1,0:T(8,128)S(1)}, u32[]{:S(2)}, u32[]{:S(2)}) collective-permute-start(f32[136,112]{1,0:T(8,128)S(1)} %coeffs2.1.refs_0_), channel_id=1, source_target_pairs={{0,3},{1,2},{2,1},{3,0},{4,7},{5,6},{6,5},{7,4},{8,11},{9,10},{10,... | collective-permute-start | bytes 182792 | tf_op jit(solution)/shard_map/ppermute | solution.py:297
  36.5 1.0 %collective-permute-start.16 = (f32[136,112]{1,0:T(8,128)S(1)}, f32[136,112]{1,0:T(8,128)S(1)}, u32[]{:S(2)}, u32[]{:S(2)}) collective-permute-start(f32[136,112]{1,0:T(8,128)S(1)} %coeffs2.1.refs_0_), channel_id=1, source_target_pairs={{0,2},{1,3},{2,0},{3,1},{4,6},{5,7},{6,4},{7,5},{8,10},{9,11},{10,... | collective-permute-start | bytes 182792 | tf_op jit(solution)/shard_map/ppermute | solution.py:297
  37.5 1.0 %collective-permute-start.15 = (f32[136,112]{1,0:T(8,128)S(1)}, f32[136,112]{1,0:T(8,128)S(1)}, u32[]{:S(2)}, u32[]{:S(2)}) collective-permute-start(f32[136,112]{1,0:T(8,128)S(1)} %coeffs2.1.refs_0_), channel_id=1, source_target_pairs={{0,1},{1,0},{2,3},{3,2},{4,5},{5,4},{6,7},{7,6},{8,9},{9,8},{10,11... | collective-permute-start | bytes 182792 | tf_op jit(solution)/shard_map/ppermute | solution.py:297
  38.6 1.7 %collective-permute-done.17.refs_3_ = f32[136,112]{1,0:T(8,128)S(1)} collective-permute-done((f32[136,112]{1,0:T(8,128)S(1)}, f32[136,112]{1,0:T(8,128)S(1)}, u32[]{:S(2)}, u32[]{:S(2)}) %collective-permute-start.17) | collective-permute-done | bytes 60960 | tf_op jit(solution)/shard_map/ppermute | solution.py:297
  40.3 0.7 %collective-permute-done.16.refs_2_ = f32[136,112]{1,0:T(8,128)S(1)} collective-permute-done((f32[136,112]{1,0:T(8,128)S(1)}, f32[136,112]{1,0:T(8,128)S(1)}, u32[]{:S(2)}, u32[]{:S(2)}) %collective-permute-start.16) | collective-permute-done | bytes 60960 | tf_op jit(solution)/shard_map/ppermute | solution.py:297
  41.0 0.8 %collective-permute-done.15.refs_1_ = f32[136,112]{1,0:T(8,128)S(1)} collective-permute-done((f32[136,112]{1,0:T(8,128)S(1)}, f32[136,112]{1,0:T(8,128)S(1)}, u32[]{:S(2)}, u32[]{:S(2)}) %collective-permute-start.15) | collective-permute-done | bytes 60960 | tf_op jit(solution)/shard_map/ppermute | solution.py:297
  41.8 0.7 %coarse2.1 = (f32[232,112]{1,0:T(8,128)S(1)}, f32[232,112]{1,0:T(8,128)S(1)}, f32[232,112]{1,0:T(8,128)S(1)}, f32[232,112]{1,0:T(8,128)S(1)}) custom-call(f32[128,512]{1,0:T(8,128)S(1)} %get-tuple-element.40.coarse_ref, bf16[896,128]{1,0:T(8,128)(2,1)S(1)} %get-tuple-element.41.turned_ref, f32[136,112]{1,0:T(8,128)S(1)} %coeffs2.1.refs_0_, ...), custom_call_target="tpu_custom_call" | custom-call | bytes 735232 | tf_op jit(solution)/shard_map/coarse2/pallas_call | solution.py:267
  42.5 0.1 collective-permute-start.18
  42.6 2.5 %collective-permute-start.19 = (f32[232,112]{1,0:T(8,128)S(1)}, f32[232,112]{1,0:T(8,128)S(1)}, u32[]{:S(2)}, u32[]{:S(2)}) collective-permute-start(f32[232,112]{1,0:T(8,128)S(1)} %get-tuple-element.53.refs_9_), channel_id=1, source_target_pairs={{0,1},{1,0},{2,3},{3,2},{4,5},{5,4},{6,7},{7,6},{8,9},{9,8},{10,11... | collective-permute-start | bytes 311816 | tf_op jit(solution)/shard_map/ppermute | solution.py:293
  45.1 1.2 %collective-permute-start.21 = (f32[232,112]{1,0:T(8,128)S(1)}, f32[232,112]{1,0:T(8,128)S(1)}, u32[]{:S(2)}, u32[]{:S(2)}) collective-permute-start(f32[232,112]{1,0:T(8,128)S(1)} %get-tuple-element.55.refs_11_), channel_id=1, source_target_pairs={{0,4},{1,5},{2,6},{3,7},{4,0},{5,1},{6,2},{7,3},{8,12},{9,13},{10,... | collective-permute-start | bytes 311816 | tf_op jit(solution)/shard_map/ppermute | solution.py:293
  46.3 3.2 %collective-permute-done.19.refs_13_ = f32[232,112]{1,0:T(8,128)S(1)} collective-permute-done((f32[232,112]{1,0:T(8,128)S(1)}, f32[232,112]{1,0:T(8,128)S(1)}, u32[]{:S(2)}, u32[]{:S(2)}) %collective-permute-start.19) | collective-permute-done | bytes 103968 | tf_op jit(solution)/shard_map/ppermute | solution.py:293
  49.5 0.4 collective-permute-done.20.refs_14_
  49.9 1.1 %second.1 = (f32[224,112]{1,0:T(8,128)S(1)}, f32[224,112]{1,0:T(8,128)S(1)}, f32[224,112]{1,0:T(8,128)S(1)}, f32[224,112]{1,0:T(8,128)S(1)}, f32[32,8,112]{2,1,0:T(8,128)S(1)}) custom-call(s32[4,112]{1,0:T(4,128)S(1)} %get-tuple-element.36.counts_ref, bf16[896,896]{1,0:T(8,128)(2,1)S(1)} %bitcast.6, f32[2,112]{1,0:T(2,128)S(1)} %get-tuple-element.47.sums_in_ref, ...), custom_call_target="tpu_custom_call" | custom-call | bytes 3672704 | tf_op jit(solution)/shard_map/second/pallas_call | solution.py:267
  51.0 11.8 %all_to_all.5.sums_ref = f32[32,8,112]{2,1,0:T(8,128)S(1)} all-to-all(f32[32,8,112]{2,1,0:T(8,128)S(1)} %get-tuple-element.60), channel_id=1, replica_groups=mesh['row'=8,'col'=4] {'row','col'}, dimensions={0} | all-to-all | bytes 229376 | tf_op jit(solution)/shard_map/all_to_all | solution.py:347
  62.8 1.2 %last.1 = f32[112,4,224]{2,1,0:T(4,128)} custom-call(f32[32,8,112]{2,1,0:T(8,128)S(1)} %all_to_all.5.sums_ref, f32[224,112]{1,0:T(8,128)S(1)} %get-tuple-element.56.refs_16_.refs_0_, f32[224,112]{1,0:T(8,128)S(1)} %get-tuple-element.57.refs_17_.refs_1_, f32[224,112]{1,0:T(8,128)S(1)} %get-tuple-element.58.refs_18_.refs_2_, ...), custom_call_target="tpu_custom_call" | custom-call | bytes 917504 | tf_op jit(solution)/shard_map/last/pallas_call | solution.py:267
  (16 shorter events, 0.0 us)
Async XLA Ops:
  0.0 26.4 %copy-start = (bf16[1,1,896,896]{3,2,1,0:T(8,128)(2,1)S(1)}, bf16[1,1,896,896]{3,2,1,0:T(8,128)(2,1)}, u32[]{:S(2)}) copy-start(bf16[1,1,896,896]{3,2,1,0:T(8,128)(2,1)} %param.6) | copy-start | bytes 4816900
  0.0 1.1 %copy-start.2 = (bf16[1,1,112,4,224]{4,3,2,1,0:T(4,128)(2,1)S(1)}, bf16[1,1,112,4,224]{4,3,2,1,0:T(4,128)(2,1)}, u32[]{:S(2)}) copy-start(bf16[1,1,112,4,224]{4,3,2,1,0:T(4,128)(2,1)} %param.5) | copy-start | bytes 602116
  1.5 9.5 %collective-permute-start = (f32[224,112]{1,0:T(8,128)S(1)}, f32[224,112]{1,0:T(8,128)S(1)}, u32[]{:S(2)}, u32[]{:S(2)}) collective-permute-start(f32[224,112]{1,0:T(8,128)S(1)} %get-tuple-element.37.refs_0_), channel_id=1, source_target_pairs={{0,4},{1,2},{2,1},{3,7},{4,0},{5,6},{6,5},{7,3},{8,12},{9,10},{10,... | collective-permute-start | bytes 301064 | tf_op jit(solution)/shard_map/ppermute | solution.py:293
  2.0 9.3 %collective-permute-start.1 = (f32[224,112]{1,0:T(8,128)S(1)}, f32[224,112]{1,0:T(8,128)S(1)}, u32[]{:S(2)}, u32[]{:S(2)}) collective-permute-start(f32[224,112]{1,0:T(8,128)S(1)} %get-tuple-element.38.refs_1_), channel_id=1, source_target_pairs={{0,1},{1,0},{2,3},{3,2},{4,5},{5,4},{6,7},{7,6},{8,9},{9,8},{10,11... | collective-permute-start | bytes 301064 | tf_op jit(solution)/shard_map/ppermute | solution.py:293
  6.0 5.3 %collective-permute-start.2 = (f32[224,112]{1,0:T(8,128)S(1)}, f32[224,112]{1,0:T(8,128)S(1)}, u32[]{:S(2)}, u32[]{:S(2)}) collective-permute-start(f32[224,112]{1,0:T(8,128)S(1)} %get-tuple-element.39.refs_2_), channel_id=1, source_target_pairs={{0,2},{1,3},{2,0},{3,1},{4,8},{5,9},{6,10},{7,11},{8,4},{9,5},{10,... | collective-permute-start | bytes 301064 | tf_op jit(solution)/shard_map/ppermute | solution.py:293
  6.1 5.2 %collective-permute-start.3 = (f32[224,112]{1,0:T(8,128)S(1)}, f32[224,112]{1,0:T(8,128)S(1)}, u32[]{:S(2)}, u32[]{:S(2)}) collective-permute-start(f32[224,112]{1,0:T(8,128)S(1)} %get-tuple-element.35.after_ref.refs_3_), channel_id=1, source_target_pairs={{0,4},{1,5},{2,6},{3,7},{4,0},{5,1},{6,2},{7,3},{8,12},{9,13},{10,... | collective-permute-start | bytes 301064 | tf_op jit(solution)/shard_map/ppermute | solution.py:293
  7.7 0.9 %copy-start.1 = (f32[1,128,512]{2,1,0:T(8,128)S(1)}, f32[1,128,512]{2,1,0:T(8,128)}, u32[]{:S(2)}) copy-start(f32[1,128,512]{2,1,0:T(8,128)} %param.8) | copy-start | bytes 786436
  8.6 0.9 %copy-start.3 = (bf16[1,1,128,896]{3,2,1,0:T(8,128)(2,1)S(1)}, bf16[1,1,128,896]{3,2,1,0:T(8,128)(2,1)}, u32[]{:S(2)}) copy-start(bf16[1,1,128,896]{3,2,1,0:T(8,128)(2,1)} %param.7) | copy-start | bytes 688132
  9.6 0.7 %copy-start.4 = (s32[1,1,4]{2,1,0:T(1,128)S(1)}, s32[1,1,4]{2,1,0:T(1,128)}, u32[]{:S(2)}) copy-start(s32[1,1,4]{2,1,0:T(1,128)} %rows_hbm.1) | copy-start | bytes 52
  11.7 5.8 %collective-permute-start.6 = (f32[128,112]{1,0:T(8,128)S(1)}, f32[128,112]{1,0:T(8,128)S(1)}, u32[]{:S(2)}, u32[]{:S(2)}) collective-permute-start(f32[128,112]{1,0:T(8,128)S(1)} %coeffs.1.refs_0_), channel_id=1, source_target_pairs={{0,3},{1,2},{2,1},{3,0},{4,7},{5,6},{6,5},{7,4},{8,11},{9,10},{10,... | collective-permute-start | bytes 172040 | tf_op jit(solution)/shard_map/ppermute | solution.py:297
  13.2 4.6 %collective-permute-start.5 = (f32[128,112]{1,0:T(8,128)S(1)}, f32[128,112]{1,0:T(8,128)S(1)}, u32[]{:S(2)}, u32[]{:S(2)}) collective-permute-start(f32[128,112]{1,0:T(8,128)S(1)} %coeffs.1.refs_0_), channel_id=1, source_target_pairs={{0,2},{1,3},{2,0},{3,1},{4,6},{5,7},{6,4},{7,5},{8,10},{9,11},{10,... | collective-permute-start | bytes 172040 | tf_op jit(solution)/shard_map/ppermute | solution.py:297
  13.6 4.3 %collective-permute-start.4 = (f32[128,112]{1,0:T(8,128)S(1)}, f32[128,112]{1,0:T(8,128)S(1)}, u32[]{:S(2)}, u32[]{:S(2)}) collective-permute-start(f32[128,112]{1,0:T(8,128)S(1)} %coeffs.1.refs_0_), channel_id=1, source_target_pairs={{0,1},{1,0},{2,3},{3,2},{4,5},{5,4},{6,7},{7,6},{8,9},{9,8},{10,11... | collective-permute-start | bytes 172040 | tf_op jit(solution)/shard_map/ppermute | solution.py:297
  18.5 4.8 %collective-permute-start.7 = (f32[224,112]{1,0:T(8,128)S(1)}, f32[224,112]{1,0:T(8,128)S(1)}, u32[]{:S(2)}, u32[]{:S(2)}) collective-permute-start(f32[224,112]{1,0:T(8,128)S(1)} %get-tuple-element.43.refs_8_), channel_id=1, source_target_pairs={{0,4},{1,2},{2,1},{3,7},{4,0},{5,6},{6,5},{7,3},{8,12},{9,10},{10,... | collective-permute-start | bytes 301064 | tf_op jit(solution)/shard_map/ppermute | solution.py:293
  18.6 7.5 %collective-permute-start.8 = (f32[224,112]{1,0:T(8,128)S(1)}, f32[224,112]{1,0:T(8,128)S(1)}, u32[]{:S(2)}, u32[]{:S(2)}) collective-permute-start(f32[224,112]{1,0:T(8,128)S(1)} %get-tuple-element.44.refs_9_), channel_id=1, source_target_pairs={{0,1},{1,0},{2,3},{3,2},{4,5},{5,4},{6,7},{7,6},{8,9},{9,8},{10,11... | collective-permute-start | bytes 301064 | tf_op jit(solution)/shard_map/ppermute | solution.py:293
  21.6 4.8 %collective-permute-start.9 = (f32[224,112]{1,0:T(8,128)S(1)}, f32[224,112]{1,0:T(8,128)S(1)}, u32[]{:S(2)}, u32[]{:S(2)}) collective-permute-start(f32[224,112]{1,0:T(8,128)S(1)} %get-tuple-element.45.refs_10_), channel_id=1, source_target_pairs={{0,2},{1,3},{2,0},{3,1},{4,8},{5,9},{6,10},{7,11},{8,4},{9,5},{10,... | collective-permute-start | bytes 301064 | tf_op jit(solution)/shard_map/ppermute | solution.py:293
  21.7 4.8 %collective-permute-start.10 = (f32[224,112]{1,0:T(8,128)S(1)}, f32[224,112]{1,0:T(8,128)S(1)}, u32[]{:S(2)}, u32[]{:S(2)}) collective-permute-start(f32[224,112]{1,0:T(8,128)S(1)} %get-tuple-element.46.refs_11_), channel_id=1, source_target_pairs={{0,4},{1,5},{2,6},{3,7},{4,0},{5,1},{6,2},{7,3},{8,12},{9,13},{10,... | collective-permute-start | bytes 301064 | tf_op jit(solution)/shard_map/ppermute | solution.py:293
  27.3 3.3 %collective-permute-start.11 = (f32[232,112]{1,0:T(8,128)S(1)}, f32[232,112]{1,0:T(8,128)S(1)}, u32[]{:S(2)}, u32[]{:S(2)}) collective-permute-start(f32[232,112]{1,0:T(8,128)S(1)} %get-tuple-element.48.refs_0_), channel_id=1, source_target_pairs={{0,4},{1,2},{2,1},{3,7},{4,0},{5,6},{6,5},{7,3},{8,12},{9,10},{10,... | collective-permute-start | bytes 311816 | tf_op jit(solution)/shard_map/ppermute | solution.py:293
  27.4 6.9 %collective-permute-start.12 = (f32[232,112]{1,0:T(8,128)S(1)}, f32[232,112]{1,0:T(8,128)S(1)}, u32[]{:S(2)}, u32[]{:S(2)}) collective-permute-start(f32[232,112]{1,0:T(8,128)S(1)} %get-tuple-element.49.refs_1_), channel_id=1, source_target_pairs={{0,1},{1,0},{2,3},{3,2},{4,5},{5,4},{6,7},{7,6},{8,9},{9,8},{10,11... | collective-permute-start | bytes 311816 | tf_op jit(solution)/shard_map/ppermute | solution.py:293
  29.8 4.8 %collective-permute-start.13 = (f32[232,112]{1,0:T(8,128)S(1)}, f32[232,112]{1,0:T(8,128)S(1)}, u32[]{:S(2)}, u32[]{:S(2)}) collective-permute-start(f32[232,112]{1,0:T(8,128)S(1)} %get-tuple-element.50.refs_2_), channel_id=1, source_target_pairs={{0,2},{1,3},{2,0},{3,1},{4,8},{5,9},{6,10},{7,11},{8,4},{9,5},{10,... | collective-permute-start | bytes 311816 | tf_op jit(solution)/shard_map/ppermute | solution.py:293
  29.8 4.8 %collective-permute-start.14 = (f32[232,112]{1,0:T(8,128)S(1)}, f32[232,112]{1,0:T(8,128)S(1)}, u32[]{:S(2)}, u32[]{:S(2)}) collective-permute-start(f32[232,112]{1,0:T(8,128)S(1)} %get-tuple-element.51.refs_3_), channel_id=1, source_target_pairs={{0,4},{1,5},{2,6},{3,7},{4,0},{5,1},{6,2},{7,3},{8,12},{9,13},{10,... | collective-permute-start | bytes 311816 | tf_op jit(solution)/shard_map/ppermute | solution.py:293
  35.0 5.3 %collective-permute-start.17 = (f32[136,112]{1,0:T(8,128)S(1)}, f32[136,112]{1,0:T(8,128)S(1)}, u32[]{:S(2)}, u32[]{:S(2)}) collective-permute-start(f32[136,112]{1,0:T(8,128)S(1)} %coeffs2.1.refs_0_), channel_id=1, source_target_pairs={{0,3},{1,2},{2,1},{3,0},{4,7},{5,6},{6,5},{7,4},{8,11},{9,10},{10,... | collective-permute-start | bytes 182792 | tf_op jit(solution)/shard_map/ppermute | solution.py:297
  36.5 4.5 %collective-permute-start.16 = (f32[136,112]{1,0:T(8,128)S(1)}, f32[136,112]{1,0:T(8,128)S(1)}, u32[]{:S(2)}, u32[]{:S(2)}) collective-permute-start(f32[136,112]{1,0:T(8,128)S(1)} %coeffs2.1.refs_0_), channel_id=1, source_target_pairs={{0,2},{1,3},{2,0},{3,1},{4,6},{5,7},{6,4},{7,5},{8,10},{9,11},{10,... | collective-permute-start | bytes 182792 | tf_op jit(solution)/shard_map/ppermute | solution.py:297
  37.5 4.3 %collective-permute-start.15 = (f32[136,112]{1,0:T(8,128)S(1)}, f32[136,112]{1,0:T(8,128)S(1)}, u32[]{:S(2)}, u32[]{:S(2)}) collective-permute-start(f32[136,112]{1,0:T(8,128)S(1)} %coeffs2.1.refs_0_), channel_id=1, source_target_pairs={{0,1},{1,0},{2,3},{3,2},{4,5},{5,4},{6,7},{7,6},{8,9},{9,8},{10,11... | collective-permute-start | bytes 182792 | tf_op jit(solution)/shard_map/ppermute | solution.py:297
  42.5 3.8 %collective-permute-start.18 = (f32[232,112]{1,0:T(8,128)S(1)}, f32[232,112]{1,0:T(8,128)S(1)}, u32[]{:S(2)}, u32[]{:S(2)}) collective-permute-start(f32[232,112]{1,0:T(8,128)S(1)} %get-tuple-element.52.refs_8_), channel_id=1, source_target_pairs={{0,4},{1,2},{2,1},{3,7},{4,0},{5,6},{6,5},{7,3},{8,12},{9,10},{10,... | collective-permute-start | bytes 311816 | tf_op jit(solution)/shard_map/ppermute | solution.py:293
  42.6 6.9 %collective-permute-start.19 = (f32[232,112]{1,0:T(8,128)S(1)}, f32[232,112]{1,0:T(8,128)S(1)}, u32[]{:S(2)}, u32[]{:S(2)}) collective-permute-start(f32[232,112]{1,0:T(8,128)S(1)} %get-tuple-element.53.refs_9_), channel_id=1, source_target_pairs={{0,1},{1,0},{2,3},{3,2},{4,5},{5,4},{6,7},{7,6},{8,9},{9,8},{10,11... | collective-permute-start | bytes 311816 | tf_op jit(solution)/shard_map/ppermute | solution.py:293
  45.1 4.8 %collective-permute-start.20 = (f32[232,112]{1,0:T(8,128)S(1)}, f32[232,112]{1,0:T(8,128)S(1)}, u32[]{:S(2)}, u32[]{:S(2)}) collective-permute-start(f32[232,112]{1,0:T(8,128)S(1)} %get-tuple-element.54.refs_10_), channel_id=1, source_target_pairs={{0,2},{1,3},{2,0},{3,1},{4,8},{5,9},{6,10},{7,11},{8,4},{9,5},{10,... | collective-permute-start | bytes 311816 | tf_op jit(solution)/shard_map/ppermute | solution.py:293
  45.1 4.8 %collective-permute-start.21 = (f32[232,112]{1,0:T(8,128)S(1)}, f32[232,112]{1,0:T(8,128)S(1)}, u32[]{:S(2)}, u32[]{:S(2)}) collective-permute-start(f32[232,112]{1,0:T(8,128)S(1)} %get-tuple-element.55.refs_11_), channel_id=1, source_target_pairs={{0,4},{1,5},{2,6},{3,7},{4,0},{5,1},{6,2},{7,3},{8,12},{9,13},{10,... | collective-permute-start | bytes 311816 | tf_op jit(solution)/shard_map/ppermute | solution.py:293

commit v4 on v3

--- a/solution.py
+++ b/solution.py
@@ -61,32 +61,49 @@
     return jnp.sum(value, axis=0, keepdims=True)
 
 
-def gap_kernel(gap_ref, *refs):
-    out_refs, field = refs[:PARTNERS], refs[PARTNERS]
-    depth = gap_ref.shape[2]
-    for face in range(PARTNERS):
-        sign = 1.0 if face % 2 else -1.0
-        block = gap_ref[:, face, :].astype(jnp.float32) * sign
-        field[face * depth : (face + 1) * depth, :] = block.T
-    for face, out_ref in zip(faces_of_partners(), out_refs):
-        out_ref[...] = field[face_slice(face, depth), :]
-
-
-def prepare_kernel(rows_hbm, modes_hbm, coarse_hbm, after_ref, counts_ref, modes_ref, coarse_ref, turned_ref, rows, sems):
-    del after_ref
-    copies = [
-        pltpu.make_async_copy(rows_hbm, rows, sems.at[0]),
-        pltpu.make_async_copy(modes_hbm, modes_ref, sems.at[1]),
-        pltpu.make_async_copy(coarse_hbm, coarse_ref, sems.at[2]),
-    ]
+def gap_kernel(gap_hbm, rows_hbm, modes_hbm, coarse_hbm, *refs):
+    out_refs, (counts_ref, modes_ref, coarse_ref, gap, field, rows, sems) = refs[:PARTNERS], refs[PARTNERS:]
+    moves = [(gap_hbm, gap), (rows_hbm, rows), (modes_hbm, modes_ref), (coarse_hbm, coarse_ref)]
+    copies = [pltpu.make_async_copy(source, target, sems.at[at]) for at, (source, target) in enumerate(moves)]
     for copy in copies:
         copy.start()
     copies[0].wait()
-    for partner, face in enumerate(faces_of_partners()):
+    depth = gap.shape[2]
+    faces = faces_of_partners()
+    for face in range(PARTNERS):
+        sign = 1.0 if face % 2 else -1.0
+        block = gap[:, face, :].astype(jnp.float32) * sign
+        field[face * depth : (face + 1) * depth, :] = block.T
+    for face, out_ref in zip(faces, out_refs):
+        out_ref[...] = field[face_slice(face, depth), :]
+    copies[1].wait()
+    for partner, face in enumerate(faces):
         counts_ref[partner : partner + 1, :] = jnp.full((1, counts_ref.shape[1]), rows[0, 0, face], jnp.int32)
-    copies[1].wait()
+    copies[2].wait()
+    copies[3].wait()
+
+
+def high_low(value):
+    high = value.astype(jnp.bfloat16)
+    return high, (value - high.astype(jnp.float32)).astype(jnp.bfloat16)
+
+
+def turn_kernel(operator_hbm, modes_ref, coarse_ref, operator_ref, turned_ref, parts_ref, sem):
+    copy = pltpu.make_async_copy(operator_hbm, operator_ref, sem)
+    copy.start()
     turned_ref[...] = modes_ref[...].astype(jnp.float32).T.astype(jnp.bfloat16)
-    copies[2].wait()
+    unknowns = coarse_ref.shape[1]
+    high, low = high_low(coarse_ref[...])
+    parts_ref[:, :unknowns] = high
+    parts_ref[:, unknowns : 2 * unknowns] = high
+    parts_ref[:, 2 * unknowns :] = low
+    copy.wait()
+
+
+def columns_kernel(*refs):
+    field_refs, out_ref = refs[:PARTNERS], refs[PARTNERS]
+    for face, ref in zip(faces_of_partners(), field_refs):
+        out_ref[face] = ref[...].T
 
 
 def read_pair(mine_ref, got_ref, count, scaled):
@@ -139,35 +156,42 @@
         out_ref[count:, :] = jnp.broadcast_to(top, (SCALE_ROWS, top.shape[1]))
 
 
-def coarse_kernel(cols, scaled, coarse_ref, turned_ref, *refs):
-    block_refs, out_refs = refs[:cols], refs[cols:]
+def coarse_kernel(cols, scaled, parts_ref, turned_ref, *refs):
+    block_refs, out_refs, stack = refs[:cols], refs[cols:-1], refs[-1]
     mine = lax.axis_index("col")
-    count = coarse_ref.shape[0]
+    count = parts_ref.shape[0]
+    unknowns = cols * count
     depth = turned_ref.shape[0] // PARTNERS
     top = None
     if scaled:
         top = functools.reduce(jnp.maximum, [scale_of(ref) for ref in block_refs])
-    total = None
     for step, ref in enumerate(block_refs):
         block = ref[:count, :]
         if scaled:
             block = block * (scale_of(ref) / top)
-        start = pl.multiple_of((mine ^ step) * count, count)
-        term = jnp.dot(
-            coarse_ref[:, pl.ds(start, count)],
-            block,
-            precision=lax.Precision.HIGHEST,
-            preferred_element_type=jnp.float32,
-        )
-        total = term if total is None else total + term
-    coarse = total.astype(jnp.bfloat16)
+        high, low = high_low(block)
+        start = (mine ^ step) * count
+        for base, part in ((0, high), (unknowns, low), (2 * unknowns, high)):
+            stack[pl.ds(pl.multiple_of(base + start, count), count), :] = part
+    coarse = jnp.dot(parts_ref[...], stack[...], preferred_element_type=jnp.float32).astype(jnp.bfloat16)
     for face, out_ref in zip(faces_of_partners(), out_refs):
         out_ref[:depth, :] = jnp.dot(turned_ref[face_slice(face, depth), :], coarse, preferred_element_type=jnp.float32)
         if scaled:
             out_ref[depth:, :] = jnp.broadcast_to(top, (SCALE_ROWS, top.shape[1]))
 
 
-def apply_dual(operator_ref, fields, faces, flat, image):
+def apply_dual(operator_ref, fields, faces, flat):
+    depth = fields[0].shape[0]
+    for face, field in zip(faces, fields):
+        flat[face_slice(face, depth), :] = (field * face_sign(face)).astype(jnp.bfloat16)
+    signed = flat[...]
+    return [
+        jnp.dot(operator_ref[face_slice(face, depth), :], signed, preferred_element_type=jnp.float32) * face_sign(face)
+        for face in faces
+    ]
+
+
+def apply_dual_whole(operator_ref, fields, faces, flat, image):
     depth = fields[0].shape[0]
     for face, field in zip(faces, fields):
         flat[face_slice(face, depth), :] = (field * face_sign(face)).astype(jnp.bfloat16)
@@ -177,7 +201,7 @@
 
 def first_kernel(counts_ref, operator_ref, *refs):
     mine_refs, got_refs, part_refs, got_part_refs = refs[:4], refs[4:8], refs[8:12], refs[12:16]
-    vector_refs, image_refs, sums_ref, flat, image = refs[16:20], refs[20:24], refs[24], refs[25], refs[26]
+    vector_refs, image_refs, sums_ref, flat = refs[16:20], refs[20:24], refs[24], refs[25]
     faces = faces_of_partners()
     counts = counts_of(counts_ref)
     residuals, _ = glued(mine_refs, got_refs, counts, False)
@@ -185,8 +209,8 @@
     fields = [residual - part for residual, part in zip(residuals, parts)]
     for ref, field in zip(vector_refs, fields):
         ref[...] = field
-    images = apply_dual(operator_ref, fields, faces, flat, image)
-    largest = jnp.max(jnp.abs(image[...]), axis=0, keepdims=True)
+    images = apply_dual(operator_ref, fields, faces, flat)
+    largest = functools.reduce(jnp.maximum, [jnp.max(jnp.abs(value), axis=0, keepdims=True) for value in images])
     largest = jnp.where(largest > 0.0, largest, 1.0)
     inverse = 1.0 / largest
     depth = fields[0].shape[0]
@@ -202,7 +226,7 @@
 
 def second_kernel(counts_ref, operator_ref, sums_in_ref, *refs):
     mine_refs, got_refs, part_refs, got_part_refs, first_refs = (refs[4 * i : 4 * i + 4] for i in range(5))
-    vector_refs, sums_ref, flat, image = refs[20:24], refs[24], refs[25], refs[26]
+    vector_refs, sums_ref, flat, image = refs[21:25], refs[25], refs[26], refs[27]
     faces = faces_of_partners()
     counts = counts_of(counts_ref)
     images, image_scale = glued(mine_refs, got_refs, counts, True)
@@ -213,7 +237,7 @@
         ref[...] = field
     own_scale = scale_of(mine_refs[0])
     depth = fields[0].shape[0]
-    second_images = apply_dual(operator_ref, fields, faces, flat, image)
+    second_images = apply_dual_whole(operator_ref, fields, faces, flat, image)
     mixed, square, cross, bend = 0.0, 0.0, 0.0, 0.0
     reach = 0.0
     for first_ref, mine_ref, field, value in zip(first_refs, mine_refs, fields, second_images):
@@ -228,9 +252,8 @@
     sums_ref[...] = jnp.broadcast_to(table[None], sums_ref.shape)
 
 
-def last_kernel(sums_ref, *refs):
-    first_refs, second_refs, out_ref, field = refs[:4], refs[4:8], refs[8], refs[9]
-    faces = faces_of_partners()
+def last_kernel(sums_ref, first_ref, *refs):
+    second_refs, (out_hbm, turned, out, sems) = refs[:PARTNERS], refs[PARTNERS:]
     device = lax.axis_index("row") * lax.axis_size("col") + lax.axis_index("col")
     every = sums_ref[...]
     scales = every[:, 6:7, :]
@@ -251,25 +274,35 @@
     next_step = fresh / next_curvature
     along_first = step + next_step * grow
     along_second = next_step * (step * sums_ref[device, 6:7, :])
-    depth = first_refs[0].shape[0]
-    for face, first_ref, second_ref in zip(faces, first_refs, second_refs):
-        field[face_slice(face, depth), :] = along_first * first_ref[...] - along_second * second_ref[...]
-    for face in range(PARTNERS):
-        out_ref[:, face, :] = field[face * depth : (face + 1) * depth, :].T
+    columns = first_ref.shape[1]
+    rows = jnp.concatenate([along_first, along_second] + [along_first] * 6, axis=0).T
+    for face, ref in zip(faces_of_partners(), second_refs):
+        turned[face] = ref[...].T
+    copies = []
+    pieces = 2
+    for piece in range(pieces):
+        part = slice(piece * columns // pieces, (piece + 1) * columns // pieces)
+        for face in range(PARTNERS):
+            out[part, face, :] = rows[part, 0:1] * first_ref[face, part, :] - rows[part, 1:2] * turned[face, part, :]
+        copies.append(pltpu.make_async_copy(out.at[part], out_hbm.at[part], sems.at[piece]))
+        copies[-1].start()
+    for copy in copies:
+        copy.wait()
 
 
 VMEM = pl.BlockSpec(memory_space=pltpu.VMEM)
 HBM = pl.BlockSpec(memory_space=pltpu.HBM)
-
-
-def run(kernel, name, outs, scratch, in_specs, args, flops=0):
+ANY = pl.BlockSpec(memory_space=pl.ANY)
+
+
+def run(kernel, name, outs, scratch, in_specs, args, flops=0, out_spec=VMEM):
     moved = sum(a.size * a.dtype.itemsize for a in args)
     return pl.pallas_call(
         kernel,
         name=name,
         out_shape=outs,
         in_specs=in_specs,
-        out_specs=jax.tree.map(lambda _: VMEM, outs),
+        out_specs=jax.tree.map(lambda _: out_spec, outs),
         scratch_shapes=scratch,
         compiler_params=pltpu.CompilerParams(vmem_limit_bytes=16 * 2**20),
         cost_estimate=pl.CostEstimate(flops=flops, bytes_accessed=moved, transcendentals=0),
@@ -303,30 +336,43 @@
     wide = pltpu.VMEM((unknowns, columns), jnp.float32)
     tall = depth + SCALE_ROWS
 
-    gaps = run(gap_kernel, "gap", four(depth), [wide], [VMEM], [gap])
-    got_gaps = swap(gaps)
-    counts, modes, coarse_block, turned = run(
-        prepare_kernel, "prepare",
-        [
+    def in_hbm(array):
+        return pltpu.with_memory_space_constraint(array, pltpu.HBM)
+
+    *gaps, counts, modes, coarse_block = run(
+        gap_kernel, "gap",
+        four(depth)
+        + [
             shape(PARTNERS, columns, dtype=jnp.int32),
             shape(*modes.shape, dtype=modes.dtype),
             shape(*coarse_block.shape),
-            shape(unknowns, count, dtype=modes.dtype),
         ],
-        [pltpu.SMEM(face_rows.shape, jnp.int32), pltpu.SemaphoreType.DMA((3,))],
-        [HBM] * 3 + [VMEM], [face_rows, modes, coarse_block, gaps[PARTNERS - 1]],
-    )
+        [pltpu.VMEM(gap.shape, gap.dtype), wide, pltpu.SMEM(face_rows.shape, jnp.int32), pltpu.SemaphoreType.DMA((4,))],
+        [HBM] * 4, list(map(in_hbm, (gap, face_rows, modes, coarse_block))),
+    )
+    got_gaps = swap(gaps)
     coeffs = run(
         functools.partial(coeffs_kernel, False), "coeffs", shape(count, columns), [flat],
         [VMEM] * 10, [counts, modes, *gaps, *got_gaps],
     )
+    blocks = gather(coeffs)
+    operator, turned, coarse_parts = run(
+        turn_kernel, "turn",
+        [
+            shape(*operator.shape, dtype=operator.dtype),
+            shape(unknowns, count, dtype=modes.dtype),
+            shape(count, 3 * cols * count, dtype=jnp.bfloat16),
+        ],
+        [pltpu.SemaphoreType.DMA], [HBM, VMEM, VMEM], [in_hbm(operator), modes, coarse_block],
+    )
+    stack = pltpu.VMEM((3 * cols * count, columns), jnp.bfloat16)
     parts = run(
-        functools.partial(coarse_kernel, cols, False), "coarse", four(depth), [],
-        [VMEM] * (2 + cols), [coarse_block, turned, *gather(coeffs)],
+        functools.partial(coarse_kernel, cols, False), "coarse", four(depth), [stack],
+        [VMEM] * (2 + cols), [coarse_parts, turned, *blocks],
     )
     got_parts = swap(parts)
     *first, sums = run(
-        first_kernel, "first", four(depth) + four(tall) + [shape(2, columns)], [flat, wide],
+        first_kernel, "first", four(depth) + four(tall) + [shape(2, columns)], [flat],
         [VMEM] * 18, [counts, operator, *gaps, *got_gaps, *parts, *got_parts],
     )
     first, images = first[:PARTNERS], first[PARTNERS:]
@@ -336,18 +382,23 @@
         [VMEM] * 10, [counts, modes, *images, *got_images],
     )
     parts = run(
-        functools.partial(coarse_kernel, cols, True), "coarse2", four(tall), [],
-        [VMEM] * (2 + cols), [coarse_block, turned, *gather(coeffs)],
+        functools.partial(coarse_kernel, cols, True), "coarse2", four(tall), [stack],
+        [VMEM] * (2 + cols), [coarse_parts, turned, *gather(coeffs)],
     )
     got_parts = swap(parts)
+    first_turned = run(
+        columns_kernel, "columns", shape(PARTNERS, columns, depth), [], [VMEM] * 4, first,
+    )
     *second, sums = run(
         second_kernel, "second", four(depth) + [shape(rows * cols, 8, columns)], [flat, wide],
-        [VMEM] * 23, [counts, operator, sums, *images, *got_images, *parts, *got_parts, *first],
+        [VMEM] * 23 + [ANY], [counts, operator, sums, *images, *got_images, *parts, *got_parts, *first, first_turned],
     )
     every = lax.all_to_all(sums, ("row", "col"), 0, 0)
+    whole = (columns, PARTNERS, depth)
     out = run(
-        last_kernel, "last", shape(columns, PARTNERS, depth), [wide],
-        [VMEM] * 9, [every, *first, *second],
+        last_kernel, "last", shape(*whole),
+        [pltpu.VMEM((PARTNERS, columns, depth), jnp.float32), pltpu.VMEM(whole, jnp.float32), pltpu.SemaphoreType.DMA((2,))],
+        [VMEM] * 6, [every, first_turned, *second], out_spec=HBM,
     )
     return out[None, None]
 

time: 64.3 us -> 63.7 us (level)
  local copies, waits for them, and re-layouts: 3.6 us -> 0 us
  Pallas kernels: 6.31 us -> 7.79 us
  waiting for transfers between devices: 17.1 us -> 18.2 us
    unnamed x10 -> x0, local copies, waits for them, and re-layouts: 3.6 us -> none
    ppermute x16, waiting for transfers between devices: 11.1 us -> 13.6 us  [swap(): lax.ppermute(field, ('row', 'col'), pairs)]
    pallas_call x9 -> x10, Pallas kernels: 6.31 us -> 7.79 us  [run(): pl.pallas_call(kernel, name=name, out_shape=outs, in_specs=in_specs, out_...]
    ppermute x6, waiting for transfers between devices: 5.92 us -> 4.51 us  [gather(): return [block] + [lax.ppermute(block, 'col', pairs) for pairs in steps]]
  transfers between devices with their start and end apart: 22 -> 22, of which waited for: 13 -> 11; matrix products, arithmetic and copies ran while one was open for 0% -> 0% of each run, Pallas kernels for 1% -> 3%
where the time goes in v4:
time: 63.7 us; the launch traced here: 63.6 us
  starting transfers between devices  25.4 us (40%)
  waiting for transfers between devices  18.2 us (29%)
  blocking collectives  12.1 us (19%)
  Pallas kernels  7.79 us (12%)
    ppermute x16, starting transfers between devices, swap(): lax.ppermute(field, ('row', 'col'), pairs)  18.3 us
    ppermute x16, waiting for transfers between devices, swap(): lax.ppermute(field, ('row', 'col'), pairs)  13.6 us
    all_to_all x1, blocking collectives, on_device(): every = lax.all_to_all(sums, ('row', 'col'), 0, 0)  12.1 us
    pallas_call x10, Pallas kernels, run(): pl.pallas_call(kernel, name=name, out_shape=outs, in_specs=in_specs, out_...  7.79 us
    ppermute x6, starting transfers between devices, gather(): return [block] + [lax.ppermute(block, 'col', pairs) for pairs in steps]  7.11 us
    ppermute x6, waiting for transfers between devices, gather(): return [block] + [lax.ppermute(block, 'col', pairs) for pairs in steps]  4.51 us
  transfers between devices with their start and end apart: 22, of which 11 were waited for; matrix products, arithmetic and copies ran while one was open for 0% of the time, Pallas kernels for 3%

profile of v4, /device:TPU:0, one launch (start us, length us, event | category | flops | bytes accessed | tf_op | source)
XLA Modules:
  0.0 63.6 jit_solution(7239462775362497191)
XLA Ops:
  0.0 1.4 %gap.1 = (f32[224,112]{1,0:T(8,128)S(1)}, f32[224,112]{1,0:T(8,128)S(1)}, f32[224,112]{1,0:T(8,128)S(1)}, f32[224,112]{1,0:T(8,128)S(1)}, s32[4,112]{1,0:T(4,128...) custom-call(bf16[112,4,224]{2,1,0:T(4,128)(2,1)} %bitcast.7, s32[1,1,4]{2,1,0:T(1,128)} %rows_hbm.1, ...), custom_call_target="tpu_custom_call" | custom-call | bytes 692240 | tf_op jit(solution)/shard_map/gap/pallas_call | solution.py:300
  1.4 0.6 collective-permute-start
  2.0 4.0 %collective-permute-start.1 = (f32[224,112]{1,0:T(8,128)S(1)}, f32[224,112]{1,0:T(8,128)S(1)}, u32[]{:S(2)}, u32[]{:S(2)}) collective-permute-start(f32[224,112]{1,0:T(8,128)S(1)} %get-tuple-element.42.refs_1_), channel_id=1, source_target_pairs={{0,1},{1,0},{2,3},{3,2},{4,5},{5,4},{6,7},{7,6},{8,9},{9,8},{10,11... | collective-permute-start | bytes 301064 | tf_op jit(solution)/shard_map/ppermute | solution.py:326
  5.9 0.1 collective-permute-start.2
  6.0 1.6 %collective-permute-start.3 = (f32[224,112]{1,0:T(8,128)S(1)}, f32[224,112]{1,0:T(8,128)S(1)}, u32[]{:S(2)}, u32[]{:S(2)}) collective-permute-start(f32[224,112]{1,0:T(8,128)S(1)} %get-tuple-element.44.refs_3_), channel_id=1, source_target_pairs={{0,4},{1,5},{2,6},{3,7},{4,0},{5,1},{6,2},{7,3},{8,12},{9,13},{10,... | collective-permute-start | bytes 301064 | tf_op jit(solution)/shard_map/ppermute | solution.py:326
  7.6 3.6 %collective-permute-done.1.refs_5_ = f32[224,112]{1,0:T(8,128)S(1)} collective-permute-done((f32[224,112]{1,0:T(8,128)S(1)}, f32[224,112]{1,0:T(8,128)S(1)}, u32[]{:S(2)}, u32[]{:S(2)}) %collective-permute-start.1) | collective-permute-done | bytes 100384 | tf_op jit(solution)/shard_map/ppermute | solution.py:326
  11.3 0.0 collective-permute-done.3.refs_7_
  11.3 0.3 coeffs.1.refs_0_
  11.6 1.5 %collective-permute-start.6 = (f32[128,112]{1,0:T(8,128)S(1)}, f32[128,112]{1,0:T(8,128)S(1)}, u32[]{:S(2)}, u32[]{:S(2)}) collective-permute-start(f32[128,112]{1,0:T(8,128)S(1)} %coeffs.1.refs_0_), channel_id=1, source_target_pairs={{0,3},{1,2},{2,1},{3,0},{4,7},{5,6},{6,5},{7,4},{8,11},{9,10},{10,... | collective-permute-start | bytes 172040 | tf_op jit(solution)/shard_map/ppermute | solution.py:330
  13.1 0.4 collective-permute-start.5
  13.5 1.6 %collective-permute-start.4 = (f32[128,112]{1,0:T(8,128)S(1)}, f32[128,112]{1,0:T(8,128)S(1)}, u32[]{:S(2)}, u32[]{:S(2)}) collective-permute-start(f32[128,112]{1,0:T(8,128)S(1)} %coeffs.1.refs_0_), channel_id=1, source_target_pairs={{0,1},{1,0},{2,3},{3,2},{4,5},{5,4},{6,7},{7,6},{8,9},{9,8},{10,11... | collective-permute-start | bytes 172040 | tf_op jit(solution)/shard_map/ppermute | solution.py:330
  15.1 1.4 %turn.1 = (bf16[896,896]{1,0:T(8,128)(2,1)S(1)}, bf16[896,128]{1,0:T(8,128)(2,1)S(1)}, bf16[128,1536]{1,0:T(8,128)(2,1)S(1)}) custom-call(bf16[896,896]{1,0:T(8,128)(2,1)} %bitcast.5, bf16[128,896]{1,0:T(8,128)(2,1)S(1)} %get-tuple-element.38.modes_ref, f32[128,512]{1,0:T(8,128)S(1)} %get-tuple-element.39.coarse_ref), custom_call_target="tpu_custom_call" | custom-call | bytes 2097152 | tf_op jit(solution)/shard_map/turn/pallas_call | solution.py:300
  16.6 0.6 %collective-permute-done.6.refs_3_ = f32[128,112]{1,0:T(8,128)S(1)} collective-permute-done((f32[128,112]{1,0:T(8,128)S(1)}, f32[128,112]{1,0:T(8,128)S(1)}, u32[]{:S(2)}, u32[]{:S(2)}) %collective-permute-start.6) | collective-permute-done | bytes 57376 | tf_op jit(solution)/shard_map/ppermute | solution.py:330
  17.2 0.6 collective-permute-done.5.refs_2_
  17.8 0.0 collective-permute-done.4.refs_1_
  17.8 0.5 coarse.1
  18.3 0.1 collective-permute-start.7
  18.4 3.0 %collective-permute-start.8 = (f32[224,112]{1,0:T(8,128)S(1)}, f32[224,112]{1,0:T(8,128)S(1)}, u32[]{:S(2)}, u32[]{:S(2)}) collective-permute-start(f32[224,112]{1,0:T(8,128)S(1)} %get-tuple-element.48.refs_9_), channel_id=1, source_target_pairs={{0,1},{1,0},{2,3},{3,2},{4,5},{5,4},{6,7},{7,6},{8,9},{9,8},{10,11... | collective-permute-start | bytes 301064 | tf_op jit(solution)/shard_map/ppermute | solution.py:326
  21.4 0.0 collective-permute-start.9
  21.4 1.7 %collective-permute-start.10 = (f32[224,112]{1,0:T(8,128)S(1)}, f32[224,112]{1,0:T(8,128)S(1)}, u32[]{:S(2)}, u32[]{:S(2)}) collective-permute-start(f32[224,112]{1,0:T(8,128)S(1)} %get-tuple-element.50.refs_11_), channel_id=1, source_target_pairs={{0,4},{1,5},{2,6},{3,7},{4,0},{5,1},{6,2},{7,3},{8,12},{9,13},{10,... | collective-permute-start | bytes 301064 | tf_op jit(solution)/shard_map/ppermute | solution.py:326
  23.1 0.0 collective-permute-done.7.refs_12_
  23.1 2.3 %collective-permute-done.8.refs_13_ = f32[224,112]{1,0:T(8,128)S(1)} collective-permute-done((f32[224,112]{1,0:T(8,128)S(1)}, f32[224,112]{1,0:T(8,128)S(1)}, u32[]{:S(2)}, u32[]{:S(2)}) %collective-permute-start.8) | collective-permute-done | bytes 100384 | tf_op jit(solution)/shard_map/ppermute | solution.py:326
  25.4 0.8 %collective-permute-done.9.refs_14_ = f32[224,112]{1,0:T(8,128)S(1)} collective-permute-done((f32[224,112]{1,0:T(8,128)S(1)}, f32[224,112]{1,0:T(8,128)S(1)}, u32[]{:S(2)}, u32[]{:S(2)}) %collective-permute-start.9) | collective-permute-done | bytes 100384 | tf_op jit(solution)/shard_map/ppermute | solution.py:326
  26.2 0.8 %first.1 = (f32[224,112]{1,0:T(8,128)S(1)}, f32[224,112]{1,0:T(8,128)S(1)}, f32[224,112]{1,0:T(8,128)S(1)}, f32[224,112]{1,0:T(8,128)S(1)}, f32[232,112]{1,0:T(8...) custom-call(s32[4,112]{1,0:T(4,128)S(1)} %get-tuple-element.37.count, ...), custom_call_target="tpu_custom_call" | custom-call | bytes 3213056 | tf_op jit(solution)/shard_map/first/pallas_call | solution.py:300
  27.0 0.1 collective-permute-start.11
  27.1 2.1 %collective-permute-start.12 = (f32[232,112]{1,0:T(8,128)S(1)}, f32[232,112]{1,0:T(8,128)S(1)}, u32[]{:S(2)}, u32[]{:S(2)}) collective-permute-start(f32[232,112]{1,0:T(8,128)S(1)} %get-tuple-element.53.refs_1_), channel_id=1, source_target_pairs={{0,1},{1,0},{2,3},{3,2},{4,5},{5,4},{6,7},{7,6},{8,9},{9,8},{10,11... | collective-permute-start | bytes 311816 | tf_op jit(solution)/shard_map/ppermute | solution.py:326
  29.2 0.0 collective-permute-start.13
  29.2 1.0 %collective-permute-start.14 = (f32[232,112]{1,0:T(8,128)S(1)}, f32[232,112]{1,0:T(8,128)S(1)}, u32[]{:S(2)}, u32[]{:S(2)}) collective-permute-start(f32[232,112]{1,0:T(8,128)S(1)} %get-tuple-element.55.refs_3_), channel_id=1, source_target_pairs={{0,4},{1,5},{2,6},{3,7},{4,0},{5,1},{6,2},{7,3},{8,12},{9,13},{10,... | collective-permute-start | bytes 311816 | tf_op jit(solution)/shard_map/ppermute | solution.py:326
  30.3 3.7 %collective-permute-done.12.refs_5_ = f32[232,112]{1,0:T(8,128)S(1)} collective-permute-done((f32[232,112]{1,0:T(8,128)S(1)}, f32[232,112]{1,0:T(8,128)S(1)}, u32[]{:S(2)}, u32[]{:S(2)}) %collective-permute-start.12) | collective-permute-done | bytes 103968 | tf_op jit(solution)/shard_map/ppermute | solution.py:326
  34.0 0.0 collective-permute-done.13.refs_6_
  34.0 0.3 coeffs2.1.refs_0_
  34.4 1.6 %collective-permute-start.17 = (f32[136,112]{1,0:T(8,128)S(1)}, f32[136,112]{1,0:T(8,128)S(1)}, u32[]{:S(2)}, u32[]{:S(2)}) collective-permute-start(f32[136,112]{1,0:T(8,128)S(1)} %coeffs2.1.refs_0_), channel_id=1, source_target_pairs={{0,3},{1,2},{2,1},{3,0},{4,7},{5,6},{6,5},{7,4},{8,11},{9,10},{10,... | collective-permute-start | bytes 182792 | tf_op jit(solution)/shard_map/ppermute | solution.py:330
  36.0 1.0 %collective-permute-start.16 = (f32[136,112]{1,0:T(8,128)S(1)}, f32[136,112]{1,0:T(8,128)S(1)}, u32[]{:S(2)}, u32[]{:S(2)}) collective-permute-start(f32[136,112]{1,0:T(8,128)S(1)} %coeffs2.1.refs_0_), channel_id=1, source_target_pairs={{0,2},{1,3},{2,0},{3,1},{4,6},{5,7},{6,4},{7,5},{8,10},{9,11},{10,... | collective-permute-start | bytes 182792 | tf_op jit(solution)/shard_map/ppermute | solution.py:330
  36.9 1.0 %collective-permute-start.15 = (f32[136,112]{1,0:T(8,128)S(1)}, f32[136,112]{1,0:T(8,128)S(1)}, u32[]{:S(2)}, u32[]{:S(2)}) collective-permute-start(f32[136,112]{1,0:T(8,128)S(1)} %coeffs2.1.refs_0_), channel_id=1, source_target_pairs={{0,1},{1,0},{2,3},{3,2},{4,5},{5,4},{6,7},{7,6},{8,9},{9,8},{10,11... | collective-permute-start | bytes 182792 | tf_op jit(solution)/shard_map/ppermute | solution.py:330
  38.0 2.0 %collective-permute-done.17.refs_3_ = f32[136,112]{1,0:T(8,128)S(1)} collective-permute-done((f32[136,112]{1,0:T(8,128)S(1)}, f32[136,112]{1,0:T(8,128)S(1)}, u32[]{:S(2)}, u32[]{:S(2)}) %collective-permute-start.17) | collective-permute-done | bytes 60960 | tf_op jit(solution)/shard_map/ppermute | solution.py:330
  40.0 0.7 %collective-permute-done.16.refs_2_ = f32[136,112]{1,0:T(8,128)S(1)} collective-permute-done((f32[136,112]{1,0:T(8,128)S(1)}, f32[136,112]{1,0:T(8,128)S(1)}, u32[]{:S(2)}, u32[]{:S(2)}) %collective-permute-start.16) | collective-permute-done | bytes 60960 | tf_op jit(solution)/shard_map/ppermute | solution.py:330
  40.7 0.6 collective-permute-done.15.refs_1_
  41.3 0.5 coarse2.1
  41.8 0.1 collective-permute-start.18
  41.9 2.5 %collective-permute-start.19 = (f32[232,112]{1,0:T(8,128)S(1)}, f32[232,112]{1,0:T(8,128)S(1)}, u32[]{:S(2)}, u32[]{:S(2)}) collective-permute-start(f32[232,112]{1,0:T(8,128)S(1)} %get-tuple-element.57.refs_9_), channel_id=1, source_target_pairs={{0,1},{1,0},{2,3},{3,2},{4,5},{5,4},{6,7},{7,6},{8,9},{9,8},{10,11... | collective-permute-start | bytes 311816 | tf_op jit(solution)/shard_map/ppermute | solution.py:326
  44.3 0.0 collective-permute-start.20
  44.3 1.5 %collective-permute-start.21 = (f32[232,112]{1,0:T(8,128)S(1)}, f32[232,112]{1,0:T(8,128)S(1)}, u32[]{:S(2)}, u32[]{:S(2)}) collective-permute-start(f32[232,112]{1,0:T(8,128)S(1)} %get-tuple-element.59.refs_11_), channel_id=1, source_target_pairs={{0,4},{1,5},{2,6},{3,7},{4,0},{5,1},{6,2},{7,3},{8,12},{9,13},{10,... | collective-permute-start | bytes 311816 | tf_op jit(solution)/shard_map/ppermute | solution.py:326
  45.8 0.2 columns.1.refs_20_.first_ref
  46.0 2.7 %collective-permute-done.19.refs_13_ = f32[232,112]{1,0:T(8,128)S(1)} collective-permute-done((f32[232,112]{1,0:T(8,128)S(1)}, f32[232,112]{1,0:T(8,128)S(1)}, u32[]{:S(2)}, u32[]{:S(2)}) %collective-permute-start.19) | collective-permute-done | bytes 103968 | tf_op jit(solution)/shard_map/ppermute | solution.py:326
  48.8 0.4 collective-permute-done.20.refs_14_
  49.2 1.1 %second.1 = (f32[224,112]{1,0:T(8,128)S(1)}, f32[224,112]{1,0:T(8,128)S(1)}, f32[224,112]{1,0:T(8,128)S(1)}, f32[224,112]{1,0:T(8,128)S(1)}, f32[32,8,112]{2,1,0:T(8,128)S(1)}) custom-call(s32[4,112]{1,0:T(4,128)S(1)} %get-tuple-element.37.counts_ref, bf16[896,896]{1,0:T(8,128)(2,1)S(1)} %get-tuple-element.40.operator_ref, ...), custom_call_target="tpu_custom_call" | custom-call | bytes 4074112 | tf_op jit(solution)/shard_map/second/pallas_call | solution.py:300
  50.2 12.1 %all_to_all.5.sums_ref = f32[32,8,112]{2,1,0:T(8,128)S(1)} all-to-all(f32[32,8,112]{2,1,0:T(8,128)S(1)} %get-tuple-element.64), channel_id=1, replica_groups=mesh['row'=8,'col'=4] {'row','col'}, dimensions={0} | all-to-all | bytes 229376 | tf_op jit(solution)/shard_map/all_to_all | solution.py:396
  62.3 1.2 %last.1 = f32[112,4,224]{2,1,0:T(4,128)} custom-call(f32[32,8,112]{2,1,0:T(8,128)S(1)} %all_to_all.5.sums_ref, f32[4,112,224]{2,1,0:T(8,128)S(1)} %columns.1.refs_20_.first_ref, f32[224,112]{1,0:T(8,128)S(1)} %get-tuple-element.65.refs_0_, f32[224,112]{1,0:T(8,128)S(1)} %get-tuple-element.66.refs_1_, f32[224,112]{1,0:T(8,128)S(1)} %get-tuple-element.67.refs_2_, ...), custom_call_target="tpu_custom_call" | custom-call | bytes 917504 | tf_op jit(solution)/shard_map/last/pallas_call | solution.py:300
  (7 shorter events, 0.0 us)
Async XLA Ops:
  1.4 6.2 %collective-permute-start = (f32[224,112]{1,0:T(8,128)S(1)}, f32[224,112]{1,0:T(8,128)S(1)}, u32[]{:S(2)}, u32[]{:S(2)}) collective-permute-start(f32[224,112]{1,0:T(8,128)S(1)} %get-tuple-element.41.refs_0_), channel_id=1, source_target_pairs={{0,4},{1,2},{2,1},{3,7},{4,0},{5,6},{6,5},{7,3},{8,12},{9,10},{10,... | collective-permute-start | bytes 301064 | tf_op jit(solution)/shard_map/ppermute | solution.py:326
  2.0 9.3 %collective-permute-start.1 = (f32[224,112]{1,0:T(8,128)S(1)}, f32[224,112]{1,0:T(8,128)S(1)}, u32[]{:S(2)}, u32[]{:S(2)}) collective-permute-start(f32[224,112]{1,0:T(8,128)S(1)} %get-tuple-element.42.refs_1_), channel_id=1, source_target_pairs={{0,1},{1,0},{2,3},{3,2},{4,5},{5,4},{6,7},{7,6},{8,9},{9,8},{10,11... | collective-permute-start | bytes 301064 | tf_op jit(solution)/shard_map/ppermute | solution.py:326
  5.9 5.3 %collective-permute-start.2 = (f32[224,112]{1,0:T(8,128)S(1)}, f32[224,112]{1,0:T(8,128)S(1)}, u32[]{:S(2)}, u32[]{:S(2)}) collective-permute-start(f32[224,112]{1,0:T(8,128)S(1)} %get-tuple-element.43.refs_2_), channel_id=1, source_target_pairs={{0,2},{1,3},{2,0},{3,1},{4,8},{5,9},{6,10},{7,11},{8,4},{9,5},{10,... | collective-permute-start | bytes 301064 | tf_op jit(solution)/shard_map/ppermute | solution.py:326
  6.0 5.2 %collective-permute-start.3 = (f32[224,112]{1,0:T(8,128)S(1)}, f32[224,112]{1,0:T(8,128)S(1)}, u32[]{:S(2)}, u32[]{:S(2)}) collective-permute-start(f32[224,112]{1,0:T(8,128)S(1)} %get-tuple-element.44.refs_3_), channel_id=1, source_target_pairs={{0,4},{1,5},{2,6},{3,7},{4,0},{5,1},{6,2},{7,3},{8,12},{9,13},{10,... | collective-permute-start | bytes 301064 | tf_op jit(solution)/shard_map/ppermute | solution.py:326
  11.6 5.6 %collective-permute-start.6 = (f32[128,112]{1,0:T(8,128)S(1)}, f32[128,112]{1,0:T(8,128)S(1)}, u32[]{:S(2)}, u32[]{:S(2)}) collective-permute-start(f32[128,112]{1,0:T(8,128)S(1)} %coeffs.1.refs_0_), channel_id=1, source_target_pairs={{0,3},{1,2},{2,1},{3,0},{4,7},{5,6},{6,5},{7,4},{8,11},{9,10},{10,... | collective-permute-start | bytes 172040 | tf_op jit(solution)/shard_map/ppermute | solution.py:330
  13.1 4.7 %collective-permute-start.5 = (f32[128,112]{1,0:T(8,128)S(1)}, f32[128,112]{1,0:T(8,128)S(1)}, u32[]{:S(2)}, u32[]{:S(2)}) collective-permute-start(f32[128,112]{1,0:T(8,128)S(1)} %coeffs.1.refs_0_), channel_id=1, source_target_pairs={{0,2},{1,3},{2,0},{3,1},{4,6},{5,7},{6,4},{7,5},{8,10},{9,11},{10,... | collective-permute-start | bytes 172040 | tf_op jit(solution)/shard_map/ppermute | solution.py:330
  13.5 4.3 %collective-permute-start.4 = (f32[128,112]{1,0:T(8,128)S(1)}, f32[128,112]{1,0:T(8,128)S(1)}, u32[]{:S(2)}, u32[]{:S(2)}) collective-permute-start(f32[128,112]{1,0:T(8,128)S(1)} %coeffs.1.refs_0_), channel_id=1, source_target_pairs={{0,1},{1,0},{2,3},{3,2},{4,5},{5,4},{6,7},{7,6},{8,9},{9,8},{10,11... | collective-permute-start | bytes 172040 | tf_op jit(solution)/shard_map/ppermute | solution.py:330
  18.3 4.8 %collective-permute-start.7 = (f32[224,112]{1,0:T(8,128)S(1)}, f32[224,112]{1,0:T(8,128)S(1)}, u32[]{:S(2)}, u32[]{:S(2)}) collective-permute-start(f32[224,112]{1,0:T(8,128)S(1)} %get-tuple-element.47.refs_8_), channel_id=1, source_target_pairs={{0,4},{1,2},{2,1},{3,7},{4,0},{5,6},{6,5},{7,3},{8,12},{9,10},{10,... | collective-permute-start | bytes 301064 | tf_op jit(solution)/shard_map/ppermute | solution.py:326
  18.4 7.0 %collective-permute-start.8 = (f32[224,112]{1,0:T(8,128)S(1)}, f32[224,112]{1,0:T(8,128)S(1)}, u32[]{:S(2)}, u32[]{:S(2)}) collective-permute-start(f32[224,112]{1,0:T(8,128)S(1)} %get-tuple-element.48.refs_9_), channel_id=1, source_target_pairs={{0,1},{1,0},{2,3},{3,2},{4,5},{5,4},{6,7},{7,6},{8,9},{9,8},{10,11... | collective-permute-start | bytes 301064 | tf_op jit(solution)/shard_map/ppermute | solution.py:326
  21.4 4.8 %collective-permute-start.9 = (f32[224,112]{1,0:T(8,128)S(1)}, f32[224,112]{1,0:T(8,128)S(1)}, u32[]{:S(2)}, u32[]{:S(2)}) collective-permute-start(f32[224,112]{1,0:T(8,128)S(1)} %get-tuple-element.49.refs_10_), channel_id=1, source_target_pairs={{0,2},{1,3},{2,0},{3,1},{4,8},{5,9},{6,10},{7,11},{8,4},{9,5},{10,... | collective-permute-start | bytes 301064 | tf_op jit(solution)/shard_map/ppermute | solution.py:326
  21.4 4.8 %collective-permute-start.10 = (f32[224,112]{1,0:T(8,128)S(1)}, f32[224,112]{1,0:T(8,128)S(1)}, u32[]{:S(2)}, u32[]{:S(2)}) collective-permute-start(f32[224,112]{1,0:T(8,128)S(1)} %get-tuple-element.50.refs_11_), channel_id=1, source_target_pairs={{0,4},{1,5},{2,6},{3,7},{4,0},{5,1},{6,2},{7,3},{8,12},{9,13},{10,... | collective-permute-start | bytes 301064 | tf_op jit(solution)/shard_map/ppermute | solution.py:326
  27.0 3.3 %collective-permute-start.11 = (f32[232,112]{1,0:T(8,128)S(1)}, f32[232,112]{1,0:T(8,128)S(1)}, u32[]{:S(2)}, u32[]{:S(2)}) collective-permute-start(f32[232,112]{1,0:T(8,128)S(1)} %get-tuple-element.52.refs_0_), channel_id=1, source_target_pairs={{0,4},{1,2},{2,1},{3,7},{4,0},{5,6},{6,5},{7,3},{8,12},{9,10},{10,... | collective-permute-start | bytes 311816 | tf_op jit(solution)/shard_map/ppermute | solution.py:326
  27.1 6.9 %collective-permute-start.12 = (f32[232,112]{1,0:T(8,128)S(1)}, f32[232,112]{1,0:T(8,128)S(1)}, u32[]{:S(2)}, u32[]{:S(2)}) collective-permute-start(f32[232,112]{1,0:T(8,128)S(1)} %get-tuple-element.53.refs_1_), channel_id=1, source_target_pairs={{0,1},{1,0},{2,3},{3,2},{4,5},{5,4},{6,7},{7,6},{8,9},{9,8},{10,11... | collective-permute-start | bytes 311816 | tf_op jit(solution)/shard_map/ppermute | solution.py:326
  29.2 4.8 %collective-permute-start.13 = (f32[232,112]{1,0:T(8,128)S(1)}, f32[232,112]{1,0:T(8,128)S(1)}, u32[]{:S(2)}, u32[]{:S(2)}) collective-permute-start(f32[232,112]{1,0:T(8,128)S(1)} %get-tuple-element.54.refs_2_), channel_id=1, source_target_pairs={{0,2},{1,3},{2,0},{3,1},{4,8},{5,9},{6,10},{7,11},{8,4},{9,5},{10,... | collective-permute-start | bytes 311816 | tf_op jit(solution)/shard_map/ppermute | solution.py:326
  29.2 4.8 %collective-permute-start.14 = (f32[232,112]{1,0:T(8,128)S(1)}, f32[232,112]{1,0:T(8,128)S(1)}, u32[]{:S(2)}, u32[]{:S(2)}) collective-permute-start(f32[232,112]{1,0:T(8,128)S(1)} %get-tuple-element.55.refs_3_), channel_id=1, source_target_pairs={{0,4},{1,5},{2,6},{3,7},{4,0},{5,1},{6,2},{7,3},{8,12},{9,13},{10,... | collective-permute-start | bytes 311816 | tf_op jit(solution)/shard_map/ppermute | solution.py:326
  34.4 5.6 %collective-permute-start.17 = (f32[136,112]{1,0:T(8,128)S(1)}, f32[136,112]{1,0:T(8,128)S(1)}, u32[]{:S(2)}, u32[]{:S(2)}) collective-permute-start(f32[136,112]{1,0:T(8,128)S(1)} %coeffs2.1.refs_0_), channel_id=1, source_target_pairs={{0,3},{1,2},{2,1},{3,0},{4,7},{5,6},{6,5},{7,4},{8,11},{9,10},{10,... | collective-permute-start | bytes 182792 | tf_op jit(solution)/shard_map/ppermute | solution.py:330
  36.0 4.7 %collective-permute-start.16 = (f32[136,112]{1,0:T(8,128)S(1)}, f32[136,112]{1,0:T(8,128)S(1)}, u32[]{:S(2)}, u32[]{:S(2)}) collective-permute-start(f32[136,112]{1,0:T(8,128)S(1)} %coeffs2.1.refs_0_), channel_id=1, source_target_pairs={{0,2},{1,3},{2,0},{3,1},{4,6},{5,7},{6,4},{7,5},{8,10},{9,11},{10,... | collective-permute-start | bytes 182792 | tf_op jit(solution)/shard_map/ppermute | solution.py:330
  36.9 4.3 %collective-permute-start.15 = (f32[136,112]{1,0:T(8,128)S(1)}, f32[136,112]{1,0:T(8,128)S(1)}, u32[]{:S(2)}, u32[]{:S(2)}) collective-permute-start(f32[136,112]{1,0:T(8,128)S(1)} %coeffs2.1.refs_0_), channel_id=1, source_target_pairs={{0,1},{1,0},{2,3},{3,2},{4,5},{5,4},{6,7},{7,6},{8,9},{9,8},{10,11... | collective-permute-start | bytes 182792 | tf_op jit(solution)/shard_map/ppermute | solution.py:330
  41.8 4.3 %collective-permute-start.18 = (f32[232,112]{1,0:T(8,128)S(1)}, f32[232,112]{1,0:T(8,128)S(1)}, u32[]{:S(2)}, u32[]{:S(2)}) collective-permute-start(f32[232,112]{1,0:T(8,128)S(1)} %get-tuple-element.56.refs_8_), channel_id=1, source_target_pairs={{0,4},{1,2},{2,1},{3,7},{4,0},{5,6},{6,5},{7,3},{8,12},{9,10},{10,... | collective-permute-start | bytes 311816 | tf_op jit(solution)/shard_map/ppermute | solution.py:326
  41.9 6.9 %collective-permute-start.19 = (f32[232,112]{1,0:T(8,128)S(1)}, f32[232,112]{1,0:T(8,128)S(1)}, u32[]{:S(2)}, u32[]{:S(2)}) collective-permute-start(f32[232,112]{1,0:T(8,128)S(1)} %get-tuple-element.57.refs_9_), channel_id=1, source_target_pairs={{0,1},{1,0},{2,3},{3,2},{4,5},{5,4},{6,7},{7,6},{8,9},{9,8},{10,11... | collective-permute-start | bytes 311816 | tf_op jit(solution)/shard_map/ppermute | solution.py:326
  44.3 4.8 %collective-permute-start.20 = (f32[232,112]{1,0:T(8,128)S(1)}, f32[232,112]{1,0:T(8,128)S(1)}, u32[]{:S(2)}, u32[]{:S(2)}) collective-permute-start(f32[232,112]{1,0:T(8,128)S(1)} %get-tuple-element.58.refs_10_), channel_id=1, source_target_pairs={{0,2},{1,3},{2,0},{3,1},{4,8},{5,9},{6,10},{7,11},{8,4},{9,5},{10,... | collective-permute-start | bytes 311816 | tf_op jit(solution)/shard_map/ppermute | solution.py:326
  44.3 4.8 %collective-permute-start.21 = (f32[232,112]{1,0:T(8,128)S(1)}, f32[232,112]{1,0:T(8,128)S(1)}, u32[]{:S(2)}, u32[]{:S(2)}) collective-permute-start(f32[232,112]{1,0:T(8,128)S(1)} %get-tuple-element.59.refs_11_), channel_id=1, source_target_pairs={{0,4},{1,5},{2,6},{3,7},{4,0},{5,1},{6,2},{7,3},{8,12},{9,13},{10,... | collective-permute-start | bytes 311816 | tf_op jit(solution)/shard_map/ppermute | solution.py:326

commit v5 on v4

v5 whole, which is shorter than its diff:
```python
import functools

import jax
import jax.numpy as jnp
from jax import lax
from jax.experimental import pallas as pl
from jax.experimental.pallas import tpu as pltpu
from jax.sharding import PartitionSpec as P

PARTNERS = 4
SCALE_ROWS = 8


def swap_tables(rows, cols):
    def table(partner):
        pairs = []
        for r in range(rows):
            for c in range(cols):
                r2, c2 = partner(r, c)
                pairs.append((r * cols + c, r2 * cols + c2))
        return pairs

    idle = 2 if cols % 4 == 0 else 1

    def across_rows(r, c):
        other = r + 1 if r % 2 else r - 1
        return (other, c) if 0 <= other < rows else (r, c ^ idle)

    def across_cols(r, c):
        other = c + 1 if c % 2 else c - 1
        return (r, other) if 0 <= other < cols else (r ^ 1, c)

    return [
        table(across_cols),
        table(lambda r, c: (r, c ^ 1)),
        table(across_rows),
        table(lambda r, c: (r ^ 1, c)),
    ]


def faces_of_partners():
    odd_row = lax.rem(lax.axis_index("row"), 2)
    odd_col = lax.rem(lax.axis_index("col"), 2)
    return [2 + odd_col, 3 - odd_col, odd_row, 1 - odd_row]


def face_slice(face, depth):
    return pl.ds(pl.multiple_of(face * depth, depth), depth)


def face_sign(face):
    return (2 * lax.rem(face, 2) - 1).astype(jnp.float32)


def masked(value, count):
    unknown = lax.broadcasted_iota(jnp.int32, value.shape, 0)
    return jnp.where(unknown < count, value, 0.0)


def column_sum(value):
    return jnp.sum(value, axis=0, keepdims=True)


def gap_kernel(gap_hbm, *refs):
    out_refs, (gap, field, sem) = refs[:PARTNERS], refs[PARTNERS:]
    copy = pltpu.make_async_copy(gap_hbm, gap, sem)
    copy.start()
    copy.wait()
    depth = gap.shape[2]
    for face in range(PARTNERS):
        sign = 1.0 if face % 2 else -1.0
        block = gap[:, face, :].astype(jnp.float32) * sign
        field[face * depth : (face + 1) * depth, :] = block.T
    for face, out_ref in zip(faces_of_partners(), out_refs):
        out_ref[...] = field[face_slice(face, depth), :]


def high_low(value):
    high = value.astype(jnp.bfloat16)
    return high, (value - high.astype(jnp.float32)).astype(jnp.bfloat16)


def prepare_kernel(rows_hbm, modes_hbm, coarse_hbm, operator_hbm, after_ref, *refs):
    del after_ref
    counts_ref, modes_ref, operator_ref, turned_ref, parts_ref, rows, coarse, sems = refs
    moves = [(modes_hbm, modes_ref), (coarse_hbm, coarse), (rows_hbm, rows), (operator_hbm, operator_ref)]
    copies = [pltpu.make_async_copy(source, target, sems.at[at]) for at, (source, target) in enumerate(moves)]
    for copy in copies:
        copy.start()
    copies[0].wait()
    turned_ref[...] = modes_ref[...].astype(jnp.float32).T.astype(jnp.bfloat16)
    copies[1].wait()
    unknowns = coarse.shape[1]
    high, low = high_low(coarse[...])
    parts_ref[:, :unknowns] = high
    parts_ref[:, unknowns : 2 * unknowns] = high
    parts_ref[:, 2 * unknowns :] = low
    copies[2].wait()
    for partner, face in enumerate(faces_of_partners()):
        counts_ref[partner : partner + 1, :] = jnp.full((1, counts_ref.shape[1]), rows[0, 0, face], jnp.int32)
    copies[3].wait()


def columns_kernel(*refs):
    field_refs, out_ref = refs[:PARTNERS], refs[PARTNERS]
    for face, ref in zip(faces_of_partners(), field_refs):
        out_ref[face] = ref[...].T


def scale_of(ref):
    depth = ref.shape[0] - SCALE_ROWS
    return ref[depth : depth + 1, :]


def set_scale(ref, scale):
    depth = ref.shape[0] - SCALE_ROWS
    ref[depth:, :] = jnp.broadcast_to(scale, (SCALE_ROWS, scale.shape[1]))


def widest(own_scale, got_refs, counts):
    top = own_scale
    for ref, count in zip(got_refs, counts):
        top = jnp.maximum(top, jnp.where(count > 0, scale_of(ref), own_scale))
    return top


def counts_of(counts_ref):
    return [counts_ref[partner : partner + 1, :] for partner in range(PARTNERS)]


def sum_of_pair(mine_ref, got_ref, depth, top):
    mine, got = mine_ref[:depth, :], got_ref[:depth, :]
    if top is not None:
        mine, got = mine * (scale_of(mine_ref) / top), got * (scale_of(got_ref) / top)
    return mine + got


def coeffs_kernel(scaled, counts_ref, modes_ref, *refs):
    mine_refs, got_refs, out_ref, flat = refs[:4], refs[4:8], refs[8], refs[9]
    counts = counts_of(counts_ref)
    depth = flat.shape[0] // PARTNERS
    top = widest(scale_of(mine_refs[0]), got_refs, counts) if scaled else None
    for face, mine_ref, got_ref, count in zip(faces_of_partners(), mine_refs, got_refs, counts):
        field = masked(sum_of_pair(mine_ref, got_ref, depth, top), count)
        flat[face_slice(face, depth), :] = field.astype(jnp.bfloat16)
    modes = modes_ref.shape[0]
    out_ref[:modes, :] = jnp.dot(modes_ref[...], flat[...], preferred_element_type=jnp.float32)
    if scaled:
        set_scale(out_ref, top)


def base_kernel(scaled, counts_ref, *refs):
    mine_refs, got_refs, part_refs, out_refs = (refs[4 * i : 4 * i + 4] for i in range(4))
    top = scale_of(part_refs[0]) if scaled else None
    depth = mine_refs[0].shape[0] - (SCALE_ROWS if scaled else 0)
    for mine_ref, got_ref, part_ref, out_ref, count in zip(mine_refs, got_refs, part_refs, out_refs, counts_of(counts_ref)):
        out_ref[:depth, :] = masked(sum_of_pair(mine_ref, got_ref, depth, top) - part_ref[:depth, :], count)
        if scaled:
            set_scale(out_ref, top)


def coarse_kernel(cols, scaled, parts_ref, turned_ref, *refs):
    block_refs, out_refs, stack = refs[:cols], refs[cols:-1], refs[-1]
    mine = lax.axis_index("col")
    count = parts_ref.shape[0]
    unknowns = cols * count
    depth = turned_ref.shape[0] // PARTNERS
    top = None
    if scaled:
        top = functools.reduce(jnp.maximum, [scale_of(ref) for ref in block_refs])
    for step, ref in enumerate(block_refs):
        block = ref[:count, :]
        if scaled:
            block = block * (scale_of(ref) / top)
        high, low = high_low(block)
        start = (mine ^ step) * count
        for base, part in ((0, high), (unknowns, low), (2 * unknowns, high)):
            stack[pl.ds(pl.multiple_of(base + start, count), count), :] = part
    coarse = jnp.dot(parts_ref[...], stack[...], preferred_element_type=jnp.float32).astype(jnp.bfloat16)
    for face, out_ref in zip(faces_of_partners(), out_refs):
        out_ref[:depth, :] = jnp.dot(turned_ref[face_slice(face, depth), :], coarse, preferred_element_type=jnp.float32)
        if scaled:
            out_ref[depth:, :] = jnp.broadcast_to(top, (SCALE_ROWS, top.shape[1]))


def dual_rows(operator_ref, flat, face):
    depth = flat.shape[0] // PARTNERS
    return jnp.dot(operator_ref[face_slice(face, depth), :], flat[...], preferred_element_type=jnp.float32) * face_sign(face)


def first_kernel(counts_ref, operator_ref, *refs):
    base_refs, got_part_refs, vector_refs, image_refs = (refs[4 * i : 4 * i + 4] for i in range(4))
    sums_ref, flat = refs[16:]
    faces = faces_of_partners()
    depth = flat.shape[0] // PARTNERS
    norm, curvature, largest = 0.0, 0.0, 0.0
    for face, base_ref, got_ref, vector_ref, count in zip(faces, base_refs, got_part_refs, vector_refs, counts_of(counts_ref)):
        field = base_ref[...] - masked(got_ref[...], count)
        vector_ref[...] = field
        flat[face_slice(face, depth), :] = (field * face_sign(face)).astype(jnp.bfloat16)
        norm += column_sum(field * field)
    for face, vector_ref, image_ref in zip(faces, vector_refs, image_refs):
        value = dual_rows(operator_ref, flat, face)
        image_ref[:depth, :] = value
        curvature += column_sum(vector_ref[...] * value)
        largest = jnp.maximum(largest, jnp.max(jnp.abs(value), axis=0, keepdims=True))
    largest = jnp.where(largest > 0.0, largest, 1.0)
    inverse = 1.0 / largest
    for image_ref in image_refs:
        image_ref[:depth, :] = image_ref[:depth, :] * inverse
        set_scale(image_ref, largest)
    sums_ref[0:1, :] = 0.5 * norm
    sums_ref[1:2, :] = curvature


def second_kernel(counts_ref, operator_ref, sums_in_ref, *refs):
    base_refs, got_part_refs, image_refs, first_refs = (refs[4 * i : 4 * i + 4] for i in range(4))
    after_ref, turned_ref, sums_ref, flat = refs[16:20]
    vector_refs = refs[20:]
    del after_ref
    faces = faces_of_partners()
    counts = counts_of(counts_ref)
    depth = flat.shape[0] // PARTNERS
    own_scale = scale_of(base_refs[0])
    top = widest(own_scale, got_part_refs, counts)
    own_factor = own_scale / top
    mixed, square, reach, bend = 0.0, 0.0, 0.0, 0.0
    for face, base_ref, got_ref, vector_ref, count in zip(faces, base_refs, got_part_refs, vector_refs, counts):
        field = base_ref[:depth, :] * own_factor - masked(got_ref[:depth, :] * (scale_of(got_ref) / top), count)
        vector_ref[...] = field
        flat[face_slice(face, depth), :] = (field * face_sign(face)).astype(jnp.bfloat16)
    for face, vector_ref, first_ref, image_ref in zip(faces, vector_refs, first_refs, image_refs):
        value = dual_rows(operator_ref, flat, face)
        field = vector_ref[...]
        mixed += column_sum(first_ref[...] * field)
        square += column_sum(field * field)
        reach += column_sum(field * image_ref[:depth, :])
        bend += column_sum(field * value)
        turned_ref[face] = field.T
    cross = (2.0 * scale_of(image_refs[0])) * reach
    rows = [sums_in_ref[0:1, :], sums_in_ref[1:2, :], 0.5 * mixed, 0.5 * square, cross, bend, top, top]
    table = jnp.concatenate(rows, axis=0)
    sums_ref[...] = jnp.broadcast_to(table[None], sums_ref.shape)


def last_kernel(sums_ref, first_ref, second_ref, out_hbm, out, sems):
    device = lax.axis_index("col") * lax.axis_size("row") + lax.axis_index("row")
    every = sums_ref[...]
    scales = every[:, 6:7, :]
    top = jnp.max(scales, axis=0, keepdims=True)
    share = scales / top
    norm = jnp.sum(every[:, 0:1, :], axis=0)
    curvature = jnp.sum(every[:, 1:2, :], axis=0)
    mixed = jnp.sum(every[:, 2:3, :] * share, axis=0)
    square = jnp.sum(every[:, 3:4, :] * share * share, axis=0)
    cross = jnp.sum(every[:, 4:5, :] * share, axis=0)
    bend = jnp.sum(every[:, 5:6, :] * share * share, axis=0)
    step = norm / curvature
    reach = step * top[0]
    fresh = norm - 2.0 * reach * mixed + reach * (reach * square)
    ratio = fresh / norm
    grow = 1.0 + ratio
    next_curvature = grow * (grow * curvature) - grow * (reach * cross) + reach * (reach * bend)
    next_step = fresh / next_curvature
    along_first = step + next_step * grow
    along_second = next_step * (step * sums_ref[device, 6:7, :])
    columns = first_ref.shape[1]
    rows = jnp.concatenate([along_first, along_second] + [along_first] * 6, axis=0).T
    copies = []
    pieces = 2
    for piece in range(pieces):
        part = slice(piece * columns // pieces, (piece + 1) * columns // pieces)
        for face in range(PARTNERS):
            out[part, face, :] = rows[part, 0:1] * first_ref[face, part, :] - rows[part, 1:2] * second_ref[face, part, :]
        copies.append(pltpu.make_async_copy(out.at[part], out_hbm.at[part], sems.at[piece]))
        copies[-1].start()
    for copy in copies:
        copy.wait()


VMEM = pl.BlockSpec(memory_space=pltpu.VMEM)
HBM = pl.BlockSpec(memory_space=pltpu.HBM)
ANY = pl.BlockSpec(memory_space=pl.ANY)


def run(kernel, name, outs, scratch, in_specs, args, flops=0, out_spec=VMEM):
    moved = sum(a.size * a.dtype.itemsize for a in args)
    return pl.pallas_call(
        kernel,
        name=name,
        out_shape=outs,
        in_specs=in_specs,
        out_specs=jax.tree.map(lambda _: out_spec, outs),
        scratch_shapes=scratch,
        compiler_params=pltpu.CompilerParams(vmem_limit_bytes=16 * 2**20),
        cost_estimate=pl.CostEstimate(flops=flops, bytes_accessed=moved, transcendentals=0),
    )(*args)


def on_device(rows, cols, local_gap, dual_ops, geneo_modes, coarse_inverse, face_rows):
    tables = swap_tables(rows, cols)
    gap = local_gap[0, 0]
    operator = dual_ops[0, 0]
    modes = geneo_modes[0, 0]
    coarse_block = coarse_inverse[0]
    columns, _, depth = gap.shape
    unknowns = operator.shape[0]
    count = modes.shape[0]

    def shape(*dims, dtype=jnp.float32):
        return jax.ShapeDtypeStruct(dims, dtype)

    def swap(fields):
        return [lax.ppermute(field, ("row", "col"), pairs) for field, pairs in zip(fields, tables)]

    def gather(block):
        steps = [[(c, c ^ step) for c in range(cols)] for step in range(1, cols)]
        return [block] + [lax.ppermute(block, "col", pairs) for pairs in steps]

    def four(height):
        return [shape(height, columns)] * PARTNERS

    flat = pltpu.VMEM((unknowns, columns), jnp.bfloat16)
    wide = pltpu.VMEM((unknowns, columns), jnp.float32)
    tall = depth + SCALE_ROWS

    def in_hbm(array):
        return pltpu.with_memory_space_constraint(array, pltpu.HBM)

    gaps = run(
        gap_kernel, "gap", four(depth), [pltpu.VMEM(gap.shape, gap.dtype), wide, pltpu.SemaphoreType.DMA],
        [HBM], [in_hbm(gap)],
    )
    got_gaps = swap(gaps)
    counts, modes, operator, turned, coarse_parts = run(
        prepare_kernel, "prepare",
        [
            shape(PARTNERS, columns, dtype=jnp.int32),
            shape(*modes.shape, dtype=modes.dtype),
            shape(*operator.shape, dtype=operator.dtype),
            shape(unknowns, count, dtype=modes.dtype),
            shape(count, 3 * cols * count, dtype=jnp.bfloat16),
        ],
        [
            pltpu.SMEM(face_rows.shape, jnp.int32),
            pltpu.VMEM(coarse_block.shape, jnp.float32),
            pltpu.SemaphoreType.DMA((4,)),
        ],
        [HBM] * 4 + [ANY], [*map(in_hbm, (face_rows, modes, coarse_block, operator)), gaps[PARTNERS - 1]],
    )
    stack = pltpu.VMEM((3 * cols * count, columns), jnp.bfloat16)

    def correction(scaled, fields, got_fields):
        extra = SCALE_ROWS if scaled else 0
        name = "second" if scaled else "first"
        coeffs = run(
            functools.partial(coeffs_kernel, scaled), name + "_coeffs", shape(count + extra, columns), [flat],
            [VMEM] * 10, [counts, modes, *fields, *got_fields],
        )
        parts = run(
            functools.partial(coarse_kernel, cols, scaled), name + "_coarse", four(depth + extra), [stack],
            [VMEM] * (2 + cols), [coarse_parts, turned, *gather(coeffs)],
        )
        got_parts = swap(parts)
        base = run(
            functools.partial(base_kernel, scaled), name + "_base", four(depth + extra), [],
            [VMEM] * 13, [counts, *fields, *got_fields, *parts],
        )
        return base, got_parts

    base, got_parts = correction(False, gaps, got_gaps)
    *first, sums = run(
        first_kernel, "first", four(depth) + four(tall) + [shape(2, columns)], [flat],
        [VMEM] * 10, [counts, operator, *base, *got_parts],
    )
    first, images = first[:PARTNERS], first[PARTNERS:]
    got_images = swap(images)
    first_turned = run(columns_kernel, "columns", shape(PARTNERS, columns, depth), [], [VMEM] * 4, first)
    base, got_parts = correction(True, images, got_images)
    second_turned, sums = run(
        second_kernel, "second", [shape(PARTNERS, columns, depth), shape(rows * cols, 8, columns)],
        [flat] + [pltpu.VMEM((depth, columns), jnp.float32)] * PARTNERS,
        [VMEM] * 19 + [ANY], [counts, operator, sums, *base, *got_parts, *images, *first, first_turned],
    )
    every = lax.all_to_all(sums, ("col", "row"), 0, 0)
    whole = (columns, PARTNERS, depth)
    out = run(
        last_kernel, "last", shape(*whole),
        [pltpu.VMEM(whole, jnp.float32), pltpu.SemaphoreType.DMA((2,))],
        [VMEM] * 3, [every, first_turned, second_turned], out_spec=HBM,
    )
    return out[None, None]


def solution(mesh):
    rows, cols = mesh.shape["row"], mesh.shape["col"]

    def body(*arrays):
        return on_device(rows, cols, *arrays)

    return jax.shard_map(
        body,
        mesh=mesh,
        in_specs=(
            P("row", "col", None, None, None),
            P("row", "col", None, None),
            P("row", "col", None, None),
            P("row", "col", None),
            P("row", "col", None),
        ),
        out_specs=P("row", "col", None, None, None),
        check_vma=False,
    )
```

time: 63.7 us -> 63.1 us (level)
    ppermute x16, waiting for transfers between devices: 13.6 us -> 11.7 us  [swap(): lax.ppermute(field, ('row', 'col'), pairs)]
    ppermute x6, waiting for transfers between devices: 4.51 us -> 5.94 us  [gather(): return [block] + [lax.ppermute(block, 'col', pairs) for pairs in steps]]
    pallas_call x10 -> x12, Pallas kernels: 7.79 us -> 7.83 us  [run(): pl.pallas_call(kernel, name=name, out_shape=outs, in_specs=in_specs, out_...]
where the time goes in v5:
time: 63.1 us; the launch traced here: 62.9 us
  starting transfers between devices  25.4 us (40%)
  waiting for transfers between devices  17.7 us (28%)
  blocking collectives  11.9 us (19%)
  Pallas kernels  7.83 us (12%)
    ppermute x16, starting transfers between devices, swap(): lax.ppermute(field, ('row', 'col'), pairs)  18.3 us
    all_to_all x1, blocking collectives, on_device(): every = lax.all_to_all(sums, ('col', 'row'), 0, 0)  11.9 us
    ppermute x16, waiting for transfers between devices, swap(): lax.ppermute(field, ('row', 'col'), pairs)  11.7 us
    pallas_call x12, Pallas kernels, run(): pl.pallas_call(kernel, name=name, out_shape=outs, in_specs=in_specs, out_...  7.83 us
    ppermute x6, starting transfers between devices, gather(): return [block] + [lax.ppermute(block, 'col', pairs) for pairs in steps]  7.11 us
    ppermute x6, waiting for transfers between devices, gather(): return [block] + [lax.ppermute(block, 'col', pairs) for pairs in steps]  5.94 us
  transfers between devices with their start and end apart: 22, of which 11 were waited for; matrix products, arithmetic and copies ran while one was open for 0% of the time, Pallas kernels for 3%

profile of v5, /device:TPU:0, one launch (start us, length us, event | category | flops | bytes accessed | tf_op | source)
XLA Modules:
  0.0 62.9 jit_solution(14103043828622245107)
XLA Ops:
  0.0 1.4 %gap.1 = (f32[224,112]{1,0:T(8,128)S(1)}, f32[224,112]{1,0:T(8,128)S(1)}, f32[224,112]{1,0:T(8,128)S(1)}, f32[224,112]{1,0:T(8,128)S(1)}) custom-call(bf16[112,4,224]{2,1,0:T(4,128)(2,1)} %bitcast.8), custom_call_target="tpu_custom_call" | custom-call | bytes 200704 | tf_op jit(solution)/shard_map/gap/pallas_call | solution.py:288
  1.4 0.6 collective-permute-start
  1.9 4.0 %collective-permute-start.1 = (f32[224,112]{1,0:T(8,128)S(1)}, f32[224,112]{1,0:T(8,128)S(1)}, u32[]{:S(2)}, u32[]{:S(2)}) collective-permute-start(f32[224,112]{1,0:T(8,128)S(1)} %get-tuple-element.45.refs_1_), channel_id=1, source_target_pairs={{0,1},{1,0},{2,3},{3,2},{4,5},{5,4},{6,7},{7,6},{8,9},{9,8},{10,11... | collective-permute-start | bytes 301064 | tf_op jit(solution)/shard_map/ppermute | solution.py:314
  5.9 0.1 collective-permute-start.2
  6.0 1.6 %collective-permute-start.3 = (f32[224,112]{1,0:T(8,128)S(1)}, f32[224,112]{1,0:T(8,128)S(1)}, u32[]{:S(2)}, u32[]{:S(2)}) collective-permute-start(f32[224,112]{1,0:T(8,128)S(1)} %get-tuple-element.41.after_ref.refs_3_), channel_id=1, source_target_pairs={{0,4},{1,5},{2,6},{3,7},{4,0},{5,1},{6,2},{7,3},{8,12},{9,13},{10,... | collective-permute-start | bytes 301064 | tf_op jit(solution)/shard_map/ppermute | solution.py:314
  7.6 1.7 %prepare.1 = (s32[4,112]{1,0:T(4,128)S(1)}, bf16[128,896]{1,0:T(8,128)(2,1)S(1)}, bf16[896,896]{1,0:T(8,128)(2,1)S(1)}, bf16[896,128]{1,0:T(8,128)(2,1)S(1)}, bf16[128,1536]{1,0:T(8,128)(2,1)S(1)}) custom-call(s32[1,1,4]{2,1,0:T(1,128)} %rows_hbm.1, bf16[128,896]{1,0:T(8,128)(2,1)} %bitcast.7, f32[128,512]{1,0:T(8,128)} %bitcast.6, ...), custom_call_target="tpu_custom_call" | custom-call | bytes 2197520 | tf_op jit(solution)/shard_map/prepare/pallas_call | solution.py:288
  9.3 0.0 collective-permute-done.refs_4_
  9.3 1.9 %collective-permute-done.1.refs_5_ = f32[224,112]{1,0:T(8,128)S(1)} collective-permute-done((f32[224,112]{1,0:T(8,128)S(1)}, f32[224,112]{1,0:T(8,128)S(1)}, u32[]{:S(2)}, u32[]{:S(2)}) %collective-permute-start.1) | collective-permute-done | bytes 100384 | tf_op jit(solution)/shard_map/ppermute | solution.py:314
  11.2 0.0 collective-permute-done.2.refs_6_
  11.2 0.3 first_coeffs.1.refs_0_
  11.5 1.5 %collective-permute-start.6 = (f32[128,112]{1,0:T(8,128)S(1)}, f32[128,112]{1,0:T(8,128)S(1)}, u32[]{:S(2)}, u32[]{:S(2)}) collective-permute-start(f32[128,112]{1,0:T(8,128)S(1)} %first_coeffs.1.refs_0_), channel_id=1, source_target_pairs={{0,3},{1,2},{2,1},{3,0},{4,7},{5,6},{6,5},{7,4},{8,11},{9,10},{10,... | collective-permute-start | bytes 172040 | tf_op jit(solution)/shard_map/ppermute | solution.py:318
  13.0 0.4 collective-permute-start.5
  13.5 1.6 %collective-permute-start.4 = (f32[128,112]{1,0:T(8,128)S(1)}, f32[128,112]{1,0:T(8,128)S(1)}, u32[]{:S(2)}, u32[]{:S(2)}) collective-permute-start(f32[128,112]{1,0:T(8,128)S(1)} %first_coeffs.1.refs_0_), channel_id=1, source_target_pairs={{0,1},{1,0},{2,3},{3,2},{4,5},{5,4},{6,7},{7,6},{8,9},{9,8},{10,11... | collective-permute-start | bytes 172040 | tf_op jit(solution)/shard_map/ppermute | solution.py:318
  15.1 2.1 %collective-permute-done.6.refs_3_ = f32[128,112]{1,0:T(8,128)S(1)} collective-permute-done((f32[128,112]{1,0:T(8,128)S(1)}, f32[128,112]{1,0:T(8,128)S(1)}, u32[]{:S(2)}, u32[]{:S(2)}) %collective-permute-start.6) | collective-permute-done | bytes 57376 | tf_op jit(solution)/shard_map/ppermute | solution.py:318
  17.2 0.6 collective-permute-done.5.refs_2_
  17.8 0.5 first_coarse.1
  18.3 0.1 collective-permute-start.7
  18.3 3.0 %collective-permute-start.8 = (f32[224,112]{1,0:T(8,128)S(1)}, f32[224,112]{1,0:T(8,128)S(1)}, u32[]{:S(2)}, u32[]{:S(2)}) collective-permute-start(f32[224,112]{1,0:T(8,128)S(1)} %get-tuple-element.51.refs_9_), channel_id=1, source_target_pairs={{0,1},{1,0},{2,3},{3,2},{4,5},{5,4},{6,7},{7,6},{8,9},{9,8},{10,11... | collective-permute-start | bytes 301064 | tf_op jit(solution)/shard_map/ppermute | solution.py:314
  21.4 0.0 collective-permute-start.9
  21.4 1.7 %collective-permute-start.10 = (f32[224,112]{1,0:T(8,128)S(1)}, f32[224,112]{1,0:T(8,128)S(1)}, u32[]{:S(2)}, u32[]{:S(2)}) collective-permute-start(f32[224,112]{1,0:T(8,128)S(1)} %get-tuple-element.53.refs_11_), channel_id=1, source_target_pairs={{0,4},{1,5},{2,6},{3,7},{4,0},{5,1},{6,2},{7,3},{8,12},{9,13},{10,... | collective-permute-start | bytes 301064 | tf_op jit(solution)/shard_map/ppermute | solution.py:314
  23.1 0.1 first_base.1
  23.2 2.2 %collective-permute-done.8.refs_5_ = f32[224,112]{1,0:T(8,128)S(1)} collective-permute-done((f32[224,112]{1,0:T(8,128)S(1)}, f32[224,112]{1,0:T(8,128)S(1)}, u32[]{:S(2)}, u32[]{:S(2)}) %collective-permute-start.8) | collective-permute-done | bytes 100384 | tf_op jit(solution)/shard_map/ppermute | solution.py:314
  25.4 0.8 %collective-permute-done.9.refs_6_ = f32[224,112]{1,0:T(8,128)S(1)} collective-permute-done((f32[224,112]{1,0:T(8,128)S(1)}, f32[224,112]{1,0:T(8,128)S(1)}, u32[]{:S(2)}, u32[]{:S(2)}) %collective-permute-start.9) | collective-permute-done | bytes 100384 | tf_op jit(solution)/shard_map/ppermute | solution.py:314
  26.2 0.8 %first.1 = (f32[224,112]{1,0:T(8,128)S(1)}, f32[224,112]{1,0:T(8,128)S(1)}, f32[224,112]{1,0:T(8,128)S(1)}, f32[224,112]{1,0:T(8,128)S(1)}, f32[232,112]{1,0:T(8...) custom-call(s32[4,112]{1,0:T(4,128)S(1)} %get-tuple-element.42.count, ...), custom_call_target="tpu_custom_call" | custom-call | bytes 2410240 | tf_op jit(solution)/shard_map/first/pallas_call | solution.py:288
  27.0 0.1 collective-permute-start.11
  27.0 2.1 %collective-permute-start.12 = (f32[232,112]{1,0:T(8,128)S(1)}, f32[232,112]{1,0:T(8,128)S(1)}, u32[]{:S(2)}, u32[]{:S(2)}) collective-permute-start(f32[232,112]{1,0:T(8,128)S(1)} %get-tuple-element.60.refs_1_.refs_9_), channel_id=1, source_target_pairs={{0,1},{1,0},{2,3},{3,2},{4,5},{5,4},{6,7},{7,6},{8,9},{9,8},{10,11... | collective-permute-start | bytes 311816 | tf_op jit(solution)/shard_map/ppermute | solution.py:314
  29.2 0.0 collective-permute-start.13
  29.2 1.0 %collective-permute-start.14 = (f32[232,112]{1,0:T(8,128)S(1)}, f32[232,112]{1,0:T(8,128)S(1)}, u32[]{:S(2)}, u32[]{:S(2)}) collective-permute-start(f32[232,112]{1,0:T(8,128)S(1)} %get-tuple-element.62.refs_3_.refs_11_), channel_id=1, source_target_pairs={{0,4},{1,5},{2,6},{3,7},{4,0},{5,1},{6,2},{7,3},{8,12},{9,13},{10,... | collective-permute-start | bytes 311816 | tf_op jit(solution)/shard_map/ppermute | solution.py:314
  30.2 3.7 %collective-permute-done.12.refs_5_ = f32[232,112]{1,0:T(8,128)S(1)} collective-permute-done((f32[232,112]{1,0:T(8,128)S(1)}, f32[232,112]{1,0:T(8,128)S(1)}, u32[]{:S(2)}, u32[]{:S(2)}) %collective-permute-start.12) | collective-permute-done | bytes 103968 | tf_op jit(solution)/shard_map/ppermute | solution.py:314
  33.9 0.0 collective-permute-done.13.refs_6_
  34.0 0.4 second_coeffs.1.refs_0_
  34.4 1.5 %collective-permute-start.17 = (f32[136,112]{1,0:T(8,128)S(1)}, f32[136,112]{1,0:T(8,128)S(1)}, u32[]{:S(2)}, u32[]{:S(2)}) collective-permute-start(f32[136,112]{1,0:T(8,128)S(1)} %second_coeffs.1.refs_0_), channel_id=1, source_target_pairs={{0,3},{1,2},{2,1},{3,0},{4,7},{5,6},{6,5},{7,4},{8,11},{9,10},{10,... | collective-permute-start | bytes 182792 | tf_op jit(solution)/shard_map/ppermute | solution.py:318
  35.9 1.0 %collective-permute-start.16 = (f32[136,112]{1,0:T(8,128)S(1)}, f32[136,112]{1,0:T(8,128)S(1)}, u32[]{:S(2)}, u32[]{:S(2)}) collective-permute-start(f32[136,112]{1,0:T(8,128)S(1)} %second_coeffs.1.refs_0_), channel_id=1, source_target_pairs={{0,2},{1,3},{2,0},{3,1},{4,6},{5,7},{6,4},{7,5},{8,10},{9,11},{10,... | collective-permute-start | bytes 182792 | tf_op jit(solution)/shard_map/ppermute | solution.py:318
  36.9 1.0 %collective-permute-start.15 = (f32[136,112]{1,0:T(8,128)S(1)}, f32[136,112]{1,0:T(8,128)S(1)}, u32[]{:S(2)}, u32[]{:S(2)}) collective-permute-start(f32[136,112]{1,0:T(8,128)S(1)} %second_coeffs.1.refs_0_), channel_id=1, source_target_pairs={{0,1},{1,0},{2,3},{3,2},{4,5},{5,4},{6,7},{7,6},{8,9},{9,8},{10,11... | collective-permute-start | bytes 182792 | tf_op jit(solution)/shard_map/ppermute | solution.py:318
  37.9 2.0 %collective-permute-done.17.refs_3_ = f32[136,112]{1,0:T(8,128)S(1)} collective-permute-done((f32[136,112]{1,0:T(8,128)S(1)}, f32[136,112]{1,0:T(8,128)S(1)}, u32[]{:S(2)}, u32[]{:S(2)}) %collective-permute-start.17) | collective-permute-done | bytes 60960 | tf_op jit(solution)/shard_map/ppermute | solution.py:318
  39.9 0.7 %collective-permute-done.16.refs_2_ = f32[136,112]{1,0:T(8,128)S(1)} collective-permute-done((f32[136,112]{1,0:T(8,128)S(1)}, f32[136,112]{1,0:T(8,128)S(1)}, u32[]{:S(2)}, u32[]{:S(2)}) %collective-permute-start.16) | collective-permute-done | bytes 60960 | tf_op jit(solution)/shard_map/ppermute | solution.py:318
  40.6 0.6 collective-permute-done.15.refs_1_
  41.2 0.5 second_coarse.1
  41.7 0.1 collective-permute-start.18
  41.8 2.5 %collective-permute-start.19 = (f32[232,112]{1,0:T(8,128)S(1)}, f32[232,112]{1,0:T(8,128)S(1)}, u32[]{:S(2)}, u32[]{:S(2)}) collective-permute-start(f32[232,112]{1,0:T(8,128)S(1)} %get-tuple-element.64.refs_9_), channel_id=1, source_target_pairs={{0,1},{1,0},{2,3},{3,2},{4,5},{5,4},{6,7},{7,6},{8,9},{9,8},{10,11... | collective-permute-start | bytes 311816 | tf_op jit(solution)/shard_map/ppermute | solution.py:314
  44.3 1.5 %collective-permute-start.21 = (f32[232,112]{1,0:T(8,128)S(1)}, f32[232,112]{1,0:T(8,128)S(1)}, u32[]{:S(2)}, u32[]{:S(2)}) collective-permute-start(f32[232,112]{1,0:T(8,128)S(1)} %get-tuple-element.66.refs_11_), channel_id=1, source_target_pairs={{0,4},{1,5},{2,6},{3,7},{4,0},{5,1},{6,2},{7,3},{8,12},{9,13},{10,... | collective-permute-start | bytes 311816 | tf_op jit(solution)/shard_map/ppermute | solution.py:314
  45.8 0.2 columns.1.refs_16_.first_ref
  46.0 0.1 second_base.1
  46.1 2.6 %collective-permute-done.19.refs_5_ = f32[232,112]{1,0:T(8,128)S(1)} collective-permute-done((f32[232,112]{1,0:T(8,128)S(1)}, f32[232,112]{1,0:T(8,128)S(1)}, u32[]{:S(2)}, u32[]{:S(2)}) %collective-permute-start.19) | collective-permute-done | bytes 103968 | tf_op jit(solution)/shard_map/ppermute | solution.py:314
  48.7 0.4 collective-permute-done.20.refs_6_
  49.1 0.8 %second.1 = (f32[4,112,224]{2,1,0:T(8,128)S(1)}, f32[32,8,112]{2,1,0:T(8,128)S(1)}) custom-call(s32[4,112]{1,0:T(4,128)S(1)} %get-tuple-element.42.counts_ref, bf16[896,896]{1,0:T(8,128)(2,1)S(1)} %get-tuple-element.43.operator_ref, f32[2,112]{1,0:T(2,128)S(1)} %get-tuple-element.58.sums_in_ref, f32[232,112]{1,0:T(8,128)S(1)} %get-tuple-element.67.refs_0_, ...), custom_call_target="tpu_custom_call" | custom-call | bytes 3658368 | tf_op jit(solution)/shard_map/second/pallas_call | solution.py:288
  49.9 11.9 %all_to_all.5.sums_ref = f32[32,8,112]{2,1,0:T(8,128)S(1)} all-to-all(f32[32,8,112]{2,1,0:T(8,128)S(1)} %get-tuple-element.75), channel_id=1, replica_groups=mesh['row'=8,'col'=4] {'col','row'}, dimensions={0} | all-to-all | bytes 229376 | tf_op jit(solution)/shard_map/all_to_all | solution.py:385
  61.8 1.2 %last.1 = f32[112,4,224]{2,1,0:T(4,128)} custom-call(f32[32,8,112]{2,1,0:T(8,128)S(1)} %all_to_all.5.sums_ref, f32[4,112,224]{2,1,0:T(8,128)S(1)} %columns.1.refs_16_.first_ref, f32[4,112,224]{2,1,0:T(8,128)S(1)} %get-tuple-element.76.second_ref), custom_call_target="tpu_custom_call" | custom-call | bytes 917504 | tf_op jit(solution)/shard_map/last/pallas_call | solution.py:288
  (9 shorter events, 0.0 us)
Async XLA Ops:
  1.4 7.9 %collective-permute-start = (f32[224,112]{1,0:T(8,128)S(1)}, f32[224,112]{1,0:T(8,128)S(1)}, u32[]{:S(2)}, u32[]{:S(2)}) collective-permute-start(f32[224,112]{1,0:T(8,128)S(1)} %get-tuple-element.44.refs_0_), channel_id=1, source_target_pairs={{0,4},{1,2},{2,1},{3,7},{4,0},{5,6},{6,5},{7,3},{8,12},{9,10},{10,... | collective-permute-start | bytes 301064 | tf_op jit(solution)/shard_map/ppermute | solution.py:314
  1.9 9.3 %collective-permute-start.1 = (f32[224,112]{1,0:T(8,128)S(1)}, f32[224,112]{1,0:T(8,128)S(1)}, u32[]{:S(2)}, u32[]{:S(2)}) collective-permute-start(f32[224,112]{1,0:T(8,128)S(1)} %get-tuple-element.45.refs_1_), channel_id=1, source_target_pairs={{0,1},{1,0},{2,3},{3,2},{4,5},{5,4},{6,7},{7,6},{8,9},{9,8},{10,11... | collective-permute-start | bytes 301064 | tf_op jit(solution)/shard_map/ppermute | solution.py:314
  5.9 5.3 %collective-permute-start.2 = (f32[224,112]{1,0:T(8,128)S(1)}, f32[224,112]{1,0:T(8,128)S(1)}, u32[]{:S(2)}, u32[]{:S(2)}) collective-permute-start(f32[224,112]{1,0:T(8,128)S(1)} %get-tuple-element.46.refs_2_), channel_id=1, source_target_pairs={{0,2},{1,3},{2,0},{3,1},{4,8},{5,9},{6,10},{7,11},{8,4},{9,5},{10,... | collective-permute-start | bytes 301064 | tf_op jit(solution)/shard_map/ppermute | solution.py:314
  6.0 5.2 %collective-permute-start.3 = (f32[224,112]{1,0:T(8,128)S(1)}, f32[224,112]{1,0:T(8,128)S(1)}, u32[]{:S(2)}, u32[]{:S(2)}) collective-permute-start(f32[224,112]{1,0:T(8,128)S(1)} %get-tuple-element.41.after_ref.refs_3_), channel_id=1, source_target_pairs={{0,4},{1,5},{2,6},{3,7},{4,0},{5,1},{6,2},{7,3},{8,12},{9,13},{10,... | collective-permute-start | bytes 301064 | tf_op jit(solution)/shard_map/ppermute | solution.py:314
  11.5 5.6 %collective-permute-start.6 = (f32[128,112]{1,0:T(8,128)S(1)}, f32[128,112]{1,0:T(8,128)S(1)}, u32[]{:S(2)}, u32[]{:S(2)}) collective-permute-start(f32[128,112]{1,0:T(8,128)S(1)} %first_coeffs.1.refs_0_), channel_id=1, source_target_pairs={{0,3},{1,2},{2,1},{3,0},{4,7},{5,6},{6,5},{7,4},{8,11},{9,10},{10,... | collective-permute-start | bytes 172040 | tf_op jit(solution)/shard_map/ppermute | solution.py:318
  13.0 4.7 %collective-permute-start.5 = (f32[128,112]{1,0:T(8,128)S(1)}, f32[128,112]{1,0:T(8,128)S(1)}, u32[]{:S(2)}, u32[]{:S(2)}) collective-permute-start(f32[128,112]{1,0:T(8,128)S(1)} %first_coeffs.1.refs_0_), channel_id=1, source_target_pairs={{0,2},{1,3},{2,0},{3,1},{4,6},{5,7},{6,4},{7,5},{8,10},{9,11},{10,... | collective-permute-start | bytes 172040 | tf_op jit(solution)/shard_map/ppermute | solution.py:318
  13.5 4.3 %collective-permute-start.4 = (f32[128,112]{1,0:T(8,128)S(1)}, f32[128,112]{1,0:T(8,128)S(1)}, u32[]{:S(2)}, u32[]{:S(2)}) collective-permute-start(f32[128,112]{1,0:T(8,128)S(1)} %first_coeffs.1.refs_0_), channel_id=1, source_target_pairs={{0,1},{1,0},{2,3},{3,2},{4,5},{5,4},{6,7},{7,6},{8,9},{9,8},{10,11... | collective-permute-start | bytes 172040 | tf_op jit(solution)/shard_map/ppermute | solution.py:318
  18.3 4.9 %collective-permute-start.7 = (f32[224,112]{1,0:T(8,128)S(1)}, f32[224,112]{1,0:T(8,128)S(1)}, u32[]{:S(2)}, u32[]{:S(2)}) collective-permute-start(f32[224,112]{1,0:T(8,128)S(1)} %get-tuple-element.50.refs_8_), channel_id=1, source_target_pairs={{0,4},{1,2},{2,1},{3,7},{4,0},{5,6},{6,5},{7,3},{8,12},{9,10},{10,... | collective-permute-start | bytes 301064 | tf_op jit(solution)/shard_map/ppermute | solution.py:314
  18.3 7.0 %collective-permute-start.8 = (f32[224,112]{1,0:T(8,128)S(1)}, f32[224,112]{1,0:T(8,128)S(1)}, u32[]{:S(2)}, u32[]{:S(2)}) collective-permute-start(f32[224,112]{1,0:T(8,128)S(1)} %get-tuple-element.51.refs_9_), channel_id=1, source_target_pairs={{0,1},{1,0},{2,3},{3,2},{4,5},{5,4},{6,7},{7,6},{8,9},{9,8},{10,11... | collective-permute-start | bytes 301064 | tf_op jit(solution)/shard_map/ppermute | solution.py:314
  21.4 4.8 %collective-permute-start.9 = (f32[224,112]{1,0:T(8,128)S(1)}, f32[224,112]{1,0:T(8,128)S(1)}, u32[]{:S(2)}, u32[]{:S(2)}) collective-permute-start(f32[224,112]{1,0:T(8,128)S(1)} %get-tuple-element.52.refs_10_), channel_id=1, source_target_pairs={{0,2},{1,3},{2,0},{3,1},{4,8},{5,9},{6,10},{7,11},{8,4},{9,5},{10,... | collective-permute-start | bytes 301064 | tf_op jit(solution)/shard_map/ppermute | solution.py:314
  21.4 4.8 %collective-permute-start.10 = (f32[224,112]{1,0:T(8,128)S(1)}, f32[224,112]{1,0:T(8,128)S(1)}, u32[]{:S(2)}, u32[]{:S(2)}) collective-permute-start(f32[224,112]{1,0:T(8,128)S(1)} %get-tuple-element.53.refs_11_), channel_id=1, source_target_pairs={{0,4},{1,5},{2,6},{3,7},{4,0},{5,1},{6,2},{7,3},{8,12},{9,13},{10,... | collective-permute-start | bytes 301064 | tf_op jit(solution)/shard_map/ppermute | solution.py:314
  27.0 3.3 %collective-permute-start.11 = (f32[232,112]{1,0:T(8,128)S(1)}, f32[232,112]{1,0:T(8,128)S(1)}, u32[]{:S(2)}, u32[]{:S(2)}) collective-permute-start(f32[232,112]{1,0:T(8,128)S(1)} %get-tuple-element.59.refs_0_.refs_8_), channel_id=1, source_target_pairs={{0,4},{1,2},{2,1},{3,7},{4,0},{5,6},{6,5},{7,3},{8,12},{9,10},{10,... | collective-permute-start | bytes 311816 | tf_op jit(solution)/shard_map/ppermute | solution.py:314
  27.0 6.9 %collective-permute-start.12 = (f32[232,112]{1,0:T(8,128)S(1)}, f32[232,112]{1,0:T(8,128)S(1)}, u32[]{:S(2)}, u32[]{:S(2)}) collective-permute-start(f32[232,112]{1,0:T(8,128)S(1)} %get-tuple-element.60.refs_1_.refs_9_), channel_id=1, source_target_pairs={{0,1},{1,0},{2,3},{3,2},{4,5},{5,4},{6,7},{7,6},{8,9},{9,8},{10,11... | collective-permute-start | bytes 311816 | tf_op jit(solution)/shard_map/ppermute | solution.py:314
  29.2 4.8 %collective-permute-start.13 = (f32[232,112]{1,0:T(8,128)S(1)}, f32[232,112]{1,0:T(8,128)S(1)}, u32[]{:S(2)}, u32[]{:S(2)}) collective-permute-start(f32[232,112]{1,0:T(8,128)S(1)} %get-tuple-element.61.refs_2_.refs_10_), channel_id=1, source_target_pairs={{0,2},{1,3},{2,0},{3,1},{4,8},{5,9},{6,10},{7,11},{8,4},{9,5},{10,... | collective-permute-start | bytes 311816 | tf_op jit(solution)/shard_map/ppermute | solution.py:314
  29.2 4.8 %collective-permute-start.14 = (f32[232,112]{1,0:T(8,128)S(1)}, f32[232,112]{1,0:T(8,128)S(1)}, u32[]{:S(2)}, u32[]{:S(2)}) collective-permute-start(f32[232,112]{1,0:T(8,128)S(1)} %get-tuple-element.62.refs_3_.refs_11_), channel_id=1, source_target_pairs={{0,4},{1,5},{2,6},{3,7},{4,0},{5,1},{6,2},{7,3},{8,12},{9,13},{10,... | collective-permute-start | bytes 311816 | tf_op jit(solution)/shard_map/ppermute | solution.py:314
  34.4 5.6 %collective-permute-start.17 = (f32[136,112]{1,0:T(8,128)S(1)}, f32[136,112]{1,0:T(8,128)S(1)}, u32[]{:S(2)}, u32[]{:S(2)}) collective-permute-start(f32[136,112]{1,0:T(8,128)S(1)} %second_coeffs.1.refs_0_), channel_id=1, source_target_pairs={{0,3},{1,2},{2,1},{3,0},{4,7},{5,6},{6,5},{7,4},{8,11},{9,10},{10,... | collective-permute-start | bytes 182792 | tf_op jit(solution)/shard_map/ppermute | solution.py:318
  35.9 4.7 %collective-permute-start.16 = (f32[136,112]{1,0:T(8,128)S(1)}, f32[136,112]{1,0:T(8,128)S(1)}, u32[]{:S(2)}, u32[]{:S(2)}) collective-permute-start(f32[136,112]{1,0:T(8,128)S(1)} %second_coeffs.1.refs_0_), channel_id=1, source_target_pairs={{0,2},{1,3},{2,0},{3,1},{4,6},{5,7},{6,4},{7,5},{8,10},{9,11},{10,... | collective-permute-start | bytes 182792 | tf_op jit(solution)/shard_map/ppermute | solution.py:318
  36.9 4.3 %collective-permute-start.15 = (f32[136,112]{1,0:T(8,128)S(1)}, f32[136,112]{1,0:T(8,128)S(1)}, u32[]{:S(2)}, u32[]{:S(2)}) collective-permute-start(f32[136,112]{1,0:T(8,128)S(1)} %second_coeffs.1.refs_0_), channel_id=1, source_target_pairs={{0,1},{1,0},{2,3},{3,2},{4,5},{5,4},{6,7},{7,6},{8,9},{9,8},{10,11... | collective-permute-start | bytes 182792 | tf_op jit(solution)/shard_map/ppermute | solution.py:318
  41.7 4.4 %collective-permute-start.18 = (f32[232,112]{1,0:T(8,128)S(1)}, f32[232,112]{1,0:T(8,128)S(1)}, u32[]{:S(2)}, u32[]{:S(2)}) collective-permute-start(f32[232,112]{1,0:T(8,128)S(1)} %get-tuple-element.63.refs_8_), channel_id=1, source_target_pairs={{0,4},{1,2},{2,1},{3,7},{4,0},{5,6},{6,5},{7,3},{8,12},{9,10},{10,... | collective-permute-start | bytes 311816 | tf_op jit(solution)/shard_map/ppermute | solution.py:314
  41.8 6.9 %collective-permute-start.19 = (f32[232,112]{1,0:T(8,128)S(1)}, f32[232,112]{1,0:T(8,128)S(1)}, u32[]{:S(2)}, u32[]{:S(2)}) collective-permute-start(f32[232,112]{1,0:T(8,128)S(1)} %get-tuple-element.64.refs_9_), channel_id=1, source_target_pairs={{0,1},{1,0},{2,3},{3,2},{4,5},{5,4},{6,7},{7,6},{8,9},{9,8},{10,11... | collective-permute-start | bytes 311816 | tf_op jit(solution)/shard_map/ppermute | solution.py:314
  44.3 4.8 %collective-permute-start.20 = (f32[232,112]{1,0:T(8,128)S(1)}, f32[232,112]{1,0:T(8,128)S(1)}, u32[]{:S(2)}, u32[]{:S(2)}) collective-permute-start(f32[232,112]{1,0:T(8,128)S(1)} %get-tuple-element.65.refs_10_), channel_id=1, source_target_pairs={{0,2},{1,3},{2,0},{3,1},{4,8},{5,9},{6,10},{7,11},{8,4},{9,5},{10,... | collective-permute-start | bytes 311816 | tf_op jit(solution)/shard_map/ppermute | solution.py:314
  44.3 4.8 %collective-permute-start.21 = (f32[232,112]{1,0:T(8,128)S(1)}, f32[232,112]{1,0:T(8,128)S(1)}, u32[]{:S(2)}, u32[]{:S(2)}) collective-permute-start(f32[232,112]{1,0:T(8,128)S(1)} %get-tuple-element.66.refs_11_), channel_id=1, source_target_pairs={{0,4},{1,5},{2,6},{3,7},{4,0},{5,1},{6,2},{7,3},{8,12},{9,13},{10,... | collective-permute-start | bytes 311816 | tf_op jit(solution)/shard_map/ppermute | solution.py:314

commit v6 on v5

--- a/solution.py
+++ b/solution.py
@@ -20,11 +20,12 @@
                 pairs.append((r * cols + c, r2 * cols + c2))
         return pairs
 
-    idle = 2 if cols % 4 == 0 else 1
+    def idle(c):
+        return c - c % 4 + (1, 3, 0, 2)[c % 4] if cols % 4 == 0 else c ^ 1
 
     def across_rows(r, c):
         other = r + 1 if r % 2 else r - 1
-        return (other, c) if 0 <= other < rows else (r, c ^ idle)
+        return (other, c) if 0 <= other < rows else (r, idle(c))
 
     def across_cols(r, c):
         other = c + 1 if c % 2 else c - 1

time: 63.1 us -> 62.9 us (level)
  waiting for transfers between devices: 17.7 us -> 19.4 us
  starting transfers between devices: 25.4 us -> 24.3 us
  blocking collectives: 11.9 us -> 11.1 us
    ppermute x16, starting transfers between devices: 18.3 us -> 17.2 us  [swap(): lax.ppermute(field, ('row', 'col'), pairs)]
    ppermute x16, waiting for transfers between devices: 11.7 us -> 12.9 us  [swap(): lax.ppermute(field, ('row', 'col'), pairs)]
    all_to_all x1, blocking collectives: 11.9 us -> 11.1 us  [on_device(): every = lax.all_to_all(sums, ('col', 'row'), 0, 0)]
  transfers between devices with their start and end apart: 22 -> 22, of which waited for: 11 -> 13; matrix products, arithmetic and copies ran while one was open for 0% -> 0% of each run, Pallas kernels for 3% -> 3%
where the time goes in v6:
time: 62.9 us; the launch traced here: 62.7 us
  starting transfers between devices  24.3 us (39%)
  waiting for transfers between devices  19.4 us (31%)
  blocking collectives  11.1 us (18%)
  Pallas kernels  7.83 us (12%)
    ppermute x16, starting transfers between devices, swap(): lax.ppermute(field, ('row', 'col'), pairs)  17.2 us
    ppermute x16, waiting for transfers between devices, swap(): lax.ppermute(field, ('row', 'col'), pairs)  12.9 us
    all_to_all x1, blocking collectives, on_device(): every = lax.all_to_all(sums, ('col', 'row'), 0, 0)  11.1 us
    pallas_call x12, Pallas kernels, run(): pl.pallas_call(kernel, name=name, out_shape=outs, in_specs=in_specs, out_...  7.83 us
    ppermute x6, starting transfers between devices, gather(): return [block] + [lax.ppermute(block, 'col', pairs) for pairs in steps]  7.11 us
    ppermute x6, waiting for transfers between devices, gather(): return [block] + [lax.ppermute(block, 'col', pairs) for pairs in steps]  6.49 us
  transfers between devices with their start and end apart: 22, of which 13 were waited for; matrix products, arithmetic and copies ran while one was open for 0% of the time, Pallas kernels for 3%

profile of v6, /device:TPU:0, one launch (start us, length us, event | category | flops | bytes accessed | tf_op | source)
XLA Modules:
  0.0 62.7 jit_solution(2246675590249450531)
XLA Ops:
  0.0 1.4 %gap.1 = (f32[224,112]{1,0:T(8,128)S(1)}, f32[224,112]{1,0:T(8,128)S(1)}, f32[224,112]{1,0:T(8,128)S(1)}, f32[224,112]{1,0:T(8,128)S(1)}) custom-call(bf16[112,4,224]{2,1,0:T(4,128)(2,1)} %bitcast.8), custom_call_target="tpu_custom_call" | custom-call | bytes 200704 | tf_op jit(solution)/shard_map/gap/pallas_call | solution.py:289
  1.4 0.6 collective-permute-start
  1.9 4.0 %collective-permute-start.1 = (f32[224,112]{1,0:T(8,128)S(1)}, f32[224,112]{1,0:T(8,128)S(1)}, u32[]{:S(2)}, u32[]{:S(2)}) collective-permute-start(f32[224,112]{1,0:T(8,128)S(1)} %get-tuple-element.45.refs_1_), channel_id=1, source_target_pairs={{0,1},{1,0},{2,3},{3,2},{4,5},{5,4},{6,7},{7,6},{8,9},{9,8},{10,11... | collective-permute-start | bytes 301064 | tf_op jit(solution)/shard_map/ppermute | solution.py:315
  5.9 0.0 collective-permute-start.2
  5.9 1.7 %collective-permute-start.3 = (f32[224,112]{1,0:T(8,128)S(1)}, f32[224,112]{1,0:T(8,128)S(1)}, u32[]{:S(2)}, u32[]{:S(2)}) collective-permute-start(f32[224,112]{1,0:T(8,128)S(1)} %get-tuple-element.41.after_ref.refs_3_), channel_id=1, source_target_pairs={{0,4},{1,5},{2,6},{3,7},{4,0},{5,1},{6,2},{7,3},{8,12},{9,13},{10,... | collective-permute-start | bytes 301064 | tf_op jit(solution)/shard_map/ppermute | solution.py:315
  7.6 1.7 %prepare.1 = (s32[4,112]{1,0:T(4,128)S(1)}, bf16[128,896]{1,0:T(8,128)(2,1)S(1)}, bf16[896,896]{1,0:T(8,128)(2,1)S(1)}, bf16[896,128]{1,0:T(8,128)(2,1)S(1)}, bf16[128,1536]{1,0:T(8,128)(2,1)S(1)}) custom-call(s32[1,1,4]{2,1,0:T(1,128)} %rows_hbm.1, bf16[128,896]{1,0:T(8,128)(2,1)} %bitcast.7, f32[128,512]{1,0:T(8,128)} %bitcast.6, ...), custom_call_target="tpu_custom_call" | custom-call | bytes 2197520 | tf_op jit(solution)/shard_map/prepare/pallas_call | solution.py:289
  9.3 1.9 %collective-permute-done.1.refs_5_ = f32[224,112]{1,0:T(8,128)S(1)} collective-permute-done((f32[224,112]{1,0:T(8,128)S(1)}, f32[224,112]{1,0:T(8,128)S(1)}, u32[]{:S(2)}, u32[]{:S(2)}) %collective-permute-start.1) | collective-permute-done | bytes 100384 | tf_op jit(solution)/shard_map/ppermute | solution.py:315
  11.2 0.3 first_coeffs.1.refs_0_
  11.5 1.5 %collective-permute-start.6 = (f32[128,112]{1,0:T(8,128)S(1)}, f32[128,112]{1,0:T(8,128)S(1)}, u32[]{:S(2)}, u32[]{:S(2)}) collective-permute-start(f32[128,112]{1,0:T(8,128)S(1)} %first_coeffs.1.refs_0_), channel_id=1, source_target_pairs={{0,3},{1,2},{2,1},{3,0},{4,7},{5,6},{6,5},{7,4},{8,11},{9,10},{10,... | collective-permute-start | bytes 172040 | tf_op jit(solution)/shard_map/ppermute | solution.py:319
  13.0 0.7 %collective-permute-start.5 = (f32[128,112]{1,0:T(8,128)S(1)}, f32[128,112]{1,0:T(8,128)S(1)}, u32[]{:S(2)}, u32[]{:S(2)}) collective-permute-start(f32[128,112]{1,0:T(8,128)S(1)} %first_coeffs.1.refs_0_), channel_id=1, source_target_pairs={{0,2},{1,3},{2,0},{3,1},{4,6},{5,7},{6,4},{7,5},{8,10},{9,11},{10,... | collective-permute-start | bytes 172040 | tf_op jit(solution)/shard_map/ppermute | solution.py:319
  13.8 1.3 %collective-permute-start.4 = (f32[128,112]{1,0:T(8,128)S(1)}, f32[128,112]{1,0:T(8,128)S(1)}, u32[]{:S(2)}, u32[]{:S(2)}) collective-permute-start(f32[128,112]{1,0:T(8,128)S(1)} %first_coeffs.1.refs_0_), channel_id=1, source_target_pairs={{0,1},{1,0},{2,3},{3,2},{4,5},{5,4},{6,7},{7,6},{8,9},{9,8},{10,11... | collective-permute-start | bytes 172040 | tf_op jit(solution)/shard_map/ppermute | solution.py:319
  15.1 2.1 %collective-permute-done.6.refs_3_ = f32[128,112]{1,0:T(8,128)S(1)} collective-permute-done((f32[128,112]{1,0:T(8,128)S(1)}, f32[128,112]{1,0:T(8,128)S(1)}, u32[]{:S(2)}, u32[]{:S(2)}) %collective-permute-start.6) | collective-permute-done | bytes 57376 | tf_op jit(solution)/shard_map/ppermute | solution.py:319
  17.2 0.6 collective-permute-done.5.refs_2_
  17.7 0.3 collective-permute-done.4.refs_1_
  18.0 0.5 first_coarse.1
  18.5 0.1 collective-permute-start.7
  18.6 2.8 %collective-permute-start.8 = (f32[224,112]{1,0:T(8,128)S(1)}, f32[224,112]{1,0:T(8,128)S(1)}, u32[]{:S(2)}, u32[]{:S(2)}) collective-permute-start(f32[224,112]{1,0:T(8,128)S(1)} %get-tuple-element.51.refs_9_), channel_id=1, source_target_pairs={{0,1},{1,0},{2,3},{3,2},{4,5},{5,4},{6,7},{7,6},{8,9},{9,8},{10,11... | collective-permute-start | bytes 301064 | tf_op jit(solution)/shard_map/ppermute | solution.py:315
  21.4 0.0 collective-permute-start.9
  21.4 1.7 %collective-permute-start.10 = (f32[224,112]{1,0:T(8,128)S(1)}, f32[224,112]{1,0:T(8,128)S(1)}, u32[]{:S(2)}, u32[]{:S(2)}) collective-permute-start(f32[224,112]{1,0:T(8,128)S(1)} %get-tuple-element.53.refs_11_), channel_id=1, source_target_pairs={{0,4},{1,5},{2,6},{3,7},{4,0},{5,1},{6,2},{7,3},{8,12},{9,13},{10,... | collective-permute-start | bytes 301064 | tf_op jit(solution)/shard_map/ppermute | solution.py:315
  23.1 0.1 first_base.1
  23.2 2.2 %collective-permute-done.8.refs_5_ = f32[224,112]{1,0:T(8,128)S(1)} collective-permute-done((f32[224,112]{1,0:T(8,128)S(1)}, f32[224,112]{1,0:T(8,128)S(1)}, u32[]{:S(2)}, u32[]{:S(2)}) %collective-permute-start.8) | collective-permute-done | bytes 100384 | tf_op jit(solution)/shard_map/ppermute | solution.py:315
  25.4 0.8 %collective-permute-done.9.refs_6_ = f32[224,112]{1,0:T(8,128)S(1)} collective-permute-done((f32[224,112]{1,0:T(8,128)S(1)}, f32[224,112]{1,0:T(8,128)S(1)}, u32[]{:S(2)}, u32[]{:S(2)}) %collective-permute-start.9) | collective-permute-done | bytes 100384 | tf_op jit(solution)/shard_map/ppermute | solution.py:315
  26.2 0.8 %first.1 = (f32[224,112]{1,0:T(8,128)S(1)}, f32[224,112]{1,0:T(8,128)S(1)}, f32[224,112]{1,0:T(8,128)S(1)}, f32[224,112]{1,0:T(8,128)S(1)}, f32[232,112]{1,0:T(8...) custom-call(s32[4,112]{1,0:T(4,128)S(1)} %get-tuple-element.42.count, ...), custom_call_target="tpu_custom_call" | custom-call | bytes 2410240 | tf_op jit(solution)/shard_map/first/pallas_call | solution.py:289
  27.0 0.1 collective-permute-start.11
  27.0 2.7 %collective-permute-start.12 = (f32[232,112]{1,0:T(8,128)S(1)}, f32[232,112]{1,0:T(8,128)S(1)}, u32[]{:S(2)}, u32[]{:S(2)}) collective-permute-start(f32[232,112]{1,0:T(8,128)S(1)} %get-tuple-element.60.refs_1_.refs_9_), channel_id=1, source_target_pairs={{0,1},{1,0},{2,3},{3,2},{4,5},{5,4},{6,7},{7,6},{8,9},{9,8},{10,11... | collective-permute-start | bytes 311816 | tf_op jit(solution)/shard_map/ppermute | solution.py:315
  29.7 0.0 collective-permute-start.13
  29.8 0.4 collective-permute-start.14
  30.2 3.7 %collective-permute-done.12.refs_5_ = f32[232,112]{1,0:T(8,128)S(1)} collective-permute-done((f32[232,112]{1,0:T(8,128)S(1)}, f32[232,112]{1,0:T(8,128)S(1)}, u32[]{:S(2)}, u32[]{:S(2)}) %collective-permute-start.12) | collective-permute-done | bytes 103968 | tf_op jit(solution)/shard_map/ppermute | solution.py:315
  33.9 0.6 %collective-permute-done.13.refs_6_ = f32[232,112]{1,0:T(8,128)S(1)} collective-permute-done((f32[232,112]{1,0:T(8,128)S(1)}, f32[232,112]{1,0:T(8,128)S(1)}, u32[]{:S(2)}, u32[]{:S(2)}) %collective-permute-start.13) | collective-permute-done | bytes 103968 | tf_op jit(solution)/shard_map/ppermute | solution.py:315
  34.6 0.4 second_coeffs.1.refs_0_
  34.9 1.5 %collective-permute-start.17 = (f32[136,112]{1,0:T(8,128)S(1)}, f32[136,112]{1,0:T(8,128)S(1)}, u32[]{:S(2)}, u32[]{:S(2)}) collective-permute-start(f32[136,112]{1,0:T(8,128)S(1)} %second_coeffs.1.refs_0_), channel_id=1, source_target_pairs={{0,3},{1,2},{2,1},{3,0},{4,7},{5,6},{6,5},{7,4},{8,11},{9,10},{10,... | collective-permute-start | bytes 182792 | tf_op jit(solution)/shard_map/ppermute | solution.py:319
  36.4 1.3 %collective-permute-start.16 = (f32[136,112]{1,0:T(8,128)S(1)}, f32[136,112]{1,0:T(8,128)S(1)}, u32[]{:S(2)}, u32[]{:S(2)}) collective-permute-start(f32[136,112]{1,0:T(8,128)S(1)} %second_coeffs.1.refs_0_), channel_id=1, source_target_pairs={{0,2},{1,3},{2,0},{3,1},{4,6},{5,7},{6,4},{7,5},{8,10},{9,11},{10,... | collective-permute-start | bytes 182792 | tf_op jit(solution)/shard_map/ppermute | solution.py:319
  37.7 0.8 %collective-permute-start.15 = (f32[136,112]{1,0:T(8,128)S(1)}, f32[136,112]{1,0:T(8,128)S(1)}, u32[]{:S(2)}, u32[]{:S(2)}) collective-permute-start(f32[136,112]{1,0:T(8,128)S(1)} %second_coeffs.1.refs_0_), channel_id=1, source_target_pairs={{0,1},{1,0},{2,3},{3,2},{4,5},{5,4},{6,7},{7,6},{8,9},{9,8},{10,11... | collective-permute-start | bytes 182792 | tf_op jit(solution)/shard_map/ppermute | solution.py:319
  38.5 1.7 %collective-permute-done.17.refs_3_ = f32[136,112]{1,0:T(8,128)S(1)} collective-permute-done((f32[136,112]{1,0:T(8,128)S(1)}, f32[136,112]{1,0:T(8,128)S(1)}, u32[]{:S(2)}, u32[]{:S(2)}) %collective-permute-start.17) | collective-permute-done | bytes 60960 | tf_op jit(solution)/shard_map/ppermute | solution.py:319
  40.2 0.7 %collective-permute-done.16.refs_2_ = f32[136,112]{1,0:T(8,128)S(1)} collective-permute-done((f32[136,112]{1,0:T(8,128)S(1)}, f32[136,112]{1,0:T(8,128)S(1)}, u32[]{:S(2)}, u32[]{:S(2)}) %collective-permute-start.16) | collective-permute-done | bytes 60960 | tf_op jit(solution)/shard_map/ppermute | solution.py:319
  41.0 1.1 %collective-permute-done.15.refs_1_ = f32[136,112]{1,0:T(8,128)S(1)} collective-permute-done((f32[136,112]{1,0:T(8,128)S(1)}, f32[136,112]{1,0:T(8,128)S(1)}, u32[]{:S(2)}, u32[]{:S(2)}) %collective-permute-start.15) | collective-permute-done | bytes 60960 | tf_op jit(solution)/shard_map/ppermute | solution.py:319
  42.0 0.5 second_coarse.1
  42.6 0.1 collective-permute-start.18
  42.6 2.2 %collective-permute-start.19 = (f32[232,112]{1,0:T(8,128)S(1)}, f32[232,112]{1,0:T(8,128)S(1)}, u32[]{:S(2)}, u32[]{:S(2)}) collective-permute-start(f32[232,112]{1,0:T(8,128)S(1)} %get-tuple-element.64.refs_9_), channel_id=1, source_target_pairs={{0,1},{1,0},{2,3},{3,2},{4,5},{5,4},{6,7},{7,6},{8,9},{9,8},{10,11... | collective-permute-start | bytes 311816 | tf_op jit(solution)/shard_map/ppermute | solution.py:315
  44.8 0.0 collective-permute-start.20
  44.8 0.9 %collective-permute-start.21 = (f32[232,112]{1,0:T(8,128)S(1)}, f32[232,112]{1,0:T(8,128)S(1)}, u32[]{:S(2)}, u32[]{:S(2)}) collective-permute-start(f32[232,112]{1,0:T(8,128)S(1)} %get-tuple-element.66.refs_11_), channel_id=1, source_target_pairs={{0,4},{1,5},{2,6},{3,7},{4,0},{5,1},{6,2},{7,3},{8,12},{9,13},{10,... | collective-permute-start | bytes 311816 | tf_op jit(solution)/shard_map/ppermute | solution.py:315
  45.8 0.2 columns.1.refs_16_.first_ref
  46.0 0.1 second_base.1
  46.1 3.4 %collective-permute-done.19.refs_5_ = f32[232,112]{1,0:T(8,128)S(1)} collective-permute-done((f32[232,112]{1,0:T(8,128)S(1)}, f32[232,112]{1,0:T(8,128)S(1)}, u32[]{:S(2)}, u32[]{:S(2)}) %collective-permute-start.19) | collective-permute-done | bytes 103968 | tf_op jit(solution)/shard_map/ppermute | solution.py:315
  49.6 0.1 collective-permute-done.20.refs_6_
  49.7 0.8 %second.1 = (f32[4,112,224]{2,1,0:T(8,128)S(1)}, f32[32,8,112]{2,1,0:T(8,128)S(1)}) custom-call(s32[4,112]{1,0:T(4,128)S(1)} %get-tuple-element.42.counts_ref, bf16[896,896]{1,0:T(8,128)(2,1)S(1)} %get-tuple-element.43.operator_ref, f32[2,112]{1,0:T(2,128)S(1)} %get-tuple-element.58.sums_in_ref, f32[232,112]{1,0:T(8,128)S(1)} %get-tuple-element.67.refs_0_, ...), custom_call_target="tpu_custom_call" | custom-call | bytes 3658368 | tf_op jit(solution)/shard_map/second/pallas_call | solution.py:289
  50.4 11.1 %all_to_all.5.sums_ref = f32[32,8,112]{2,1,0:T(8,128)S(1)} all-to-all(f32[32,8,112]{2,1,0:T(8,128)S(1)} %get-tuple-element.75), channel_id=1, replica_groups=mesh['row'=8,'col'=4] {'col','row'}, dimensions={0} | all-to-all | bytes 229376 | tf_op jit(solution)/shard_map/all_to_all | solution.py:386
  61.5 1.2 %last.1 = f32[112,4,224]{2,1,0:T(4,128)} custom-call(f32[32,8,112]{2,1,0:T(8,128)S(1)} %all_to_all.5.sums_ref, f32[4,112,224]{2,1,0:T(8,128)S(1)} %columns.1.refs_16_.first_ref, f32[4,112,224]{2,1,0:T(8,128)S(1)} %get-tuple-element.76.second_ref), custom_call_target="tpu_custom_call" | custom-call | bytes 917504 | tf_op jit(solution)/shard_map/last/pallas_call | solution.py:289
  (9 shorter events, 0.0 us)
Async XLA Ops:
  1.4 7.9 %collective-permute-start = (f32[224,112]{1,0:T(8,128)S(1)}, f32[224,112]{1,0:T(8,128)S(1)}, u32[]{:S(2)}, u32[]{:S(2)}) collective-permute-start(f32[224,112]{1,0:T(8,128)S(1)} %get-tuple-element.44.refs_0_), channel_id=1, source_target_pairs={{0,4},{1,2},{2,1},{3,7},{4,0},{5,6},{6,5},{7,3},{8,12},{9,10},{10,... | collective-permute-start | bytes 301064 | tf_op jit(solution)/shard_map/ppermute | solution.py:315
  1.9 9.3 %collective-permute-start.1 = (f32[224,112]{1,0:T(8,128)S(1)}, f32[224,112]{1,0:T(8,128)S(1)}, u32[]{:S(2)}, u32[]{:S(2)}) collective-permute-start(f32[224,112]{1,0:T(8,128)S(1)} %get-tuple-element.45.refs_1_), channel_id=1, source_target_pairs={{0,1},{1,0},{2,3},{3,2},{4,5},{5,4},{6,7},{7,6},{8,9},{9,8},{10,11... | collective-permute-start | bytes 301064 | tf_op jit(solution)/shard_map/ppermute | solution.py:315
  5.9 5.3 %collective-permute-start.2 = (f32[224,112]{1,0:T(8,128)S(1)}, f32[224,112]{1,0:T(8,128)S(1)}, u32[]{:S(2)}, u32[]{:S(2)}) collective-permute-start(f32[224,112]{1,0:T(8,128)S(1)} %get-tuple-element.46.refs_2_), channel_id=1, source_target_pairs={{0,1},{1,3},{2,0},{3,2},{4,8},{5,9},{6,10},{7,11},{8,4},{9,5},{10,... | collective-permute-start | bytes 301064 | tf_op jit(solution)/shard_map/ppermute | solution.py:315
  5.9 5.3 %collective-permute-start.3 = (f32[224,112]{1,0:T(8,128)S(1)}, f32[224,112]{1,0:T(8,128)S(1)}, u32[]{:S(2)}, u32[]{:S(2)}) collective-permute-start(f32[224,112]{1,0:T(8,128)S(1)} %get-tuple-element.41.after_ref.refs_3_), channel_id=1, source_target_pairs={{0,4},{1,5},{2,6},{3,7},{4,0},{5,1},{6,2},{7,3},{8,12},{9,13},{10,... | collective-permute-start | bytes 301064 | tf_op jit(solution)/shard_map/ppermute | solution.py:315
  11.5 5.6 %collective-permute-start.6 = (f32[128,112]{1,0:T(8,128)S(1)}, f32[128,112]{1,0:T(8,128)S(1)}, u32[]{:S(2)}, u32[]{:S(2)}) collective-permute-start(f32[128,112]{1,0:T(8,128)S(1)} %first_coeffs.1.refs_0_), channel_id=1, source_target_pairs={{0,3},{1,2},{2,1},{3,0},{4,7},{5,6},{6,5},{7,4},{8,11},{9,10},{10,... | collective-permute-start | bytes 172040 | tf_op jit(solution)/shard_map/ppermute | solution.py:319
  13.0 4.7 %collective-permute-start.5 = (f32[128,112]{1,0:T(8,128)S(1)}, f32[128,112]{1,0:T(8,128)S(1)}, u32[]{:S(2)}, u32[]{:S(2)}) collective-permute-start(f32[128,112]{1,0:T(8,128)S(1)} %first_coeffs.1.refs_0_), channel_id=1, source_target_pairs={{0,2},{1,3},{2,0},{3,1},{4,6},{5,7},{6,4},{7,5},{8,10},{9,11},{10,... | collective-permute-start | bytes 172040 | tf_op jit(solution)/shard_map/ppermute | solution.py:319
  13.8 4.3 %collective-permute-start.4 = (f32[128,112]{1,0:T(8,128)S(1)}, f32[128,112]{1,0:T(8,128)S(1)}, u32[]{:S(2)}, u32[]{:S(2)}) collective-permute-start(f32[128,112]{1,0:T(8,128)S(1)} %first_coeffs.1.refs_0_), channel_id=1, source_target_pairs={{0,1},{1,0},{2,3},{3,2},{4,5},{5,4},{6,7},{7,6},{8,9},{9,8},{10,11... | collective-permute-start | bytes 172040 | tf_op jit(solution)/shard_map/ppermute | solution.py:319
  18.5 4.6 %collective-permute-start.7 = (f32[224,112]{1,0:T(8,128)S(1)}, f32[224,112]{1,0:T(8,128)S(1)}, u32[]{:S(2)}, u32[]{:S(2)}) collective-permute-start(f32[224,112]{1,0:T(8,128)S(1)} %get-tuple-element.50.refs_8_), channel_id=1, source_target_pairs={{0,4},{1,2},{2,1},{3,7},{4,0},{5,6},{6,5},{7,3},{8,12},{9,10},{10,... | collective-permute-start | bytes 301064 | tf_op jit(solution)/shard_map/ppermute | solution.py:315
  18.6 6.8 %collective-permute-start.8 = (f32[224,112]{1,0:T(8,128)S(1)}, f32[224,112]{1,0:T(8,128)S(1)}, u32[]{:S(2)}, u32[]{:S(2)}) collective-permute-start(f32[224,112]{1,0:T(8,128)S(1)} %get-tuple-element.51.refs_9_), channel_id=1, source_target_pairs={{0,1},{1,0},{2,3},{3,2},{4,5},{5,4},{6,7},{7,6},{8,9},{9,8},{10,11... | collective-permute-start | bytes 301064 | tf_op jit(solution)/shard_map/ppermute | solution.py:315
  21.4 4.8 %collective-permute-start.9 = (f32[224,112]{1,0:T(8,128)S(1)}, f32[224,112]{1,0:T(8,128)S(1)}, u32[]{:S(2)}, u32[]{:S(2)}) collective-permute-start(f32[224,112]{1,0:T(8,128)S(1)} %get-tuple-element.52.refs_10_), channel_id=1, source_target_pairs={{0,1},{1,3},{2,0},{3,2},{4,8},{5,9},{6,10},{7,11},{8,4},{9,5},{10,... | collective-permute-start | bytes 301064 | tf_op jit(solution)/shard_map/ppermute | solution.py:315
  21.4 4.8 %collective-permute-start.10 = (f32[224,112]{1,0:T(8,128)S(1)}, f32[224,112]{1,0:T(8,128)S(1)}, u32[]{:S(2)}, u32[]{:S(2)}) collective-permute-start(f32[224,112]{1,0:T(8,128)S(1)} %get-tuple-element.53.refs_11_), channel_id=1, source_target_pairs={{0,4},{1,5},{2,6},{3,7},{4,0},{5,1},{6,2},{7,3},{8,12},{9,13},{10,... | collective-permute-start | bytes 301064 | tf_op jit(solution)/shard_map/ppermute | solution.py:315
  27.0 3.3 %collective-permute-start.11 = (f32[232,112]{1,0:T(8,128)S(1)}, f32[232,112]{1,0:T(8,128)S(1)}, u32[]{:S(2)}, u32[]{:S(2)}) collective-permute-start(f32[232,112]{1,0:T(8,128)S(1)} %get-tuple-element.59.refs_0_.refs_8_), channel_id=1, source_target_pairs={{0,4},{1,2},{2,1},{3,7},{4,0},{5,6},{6,5},{7,3},{8,12},{9,10},{10,... | collective-permute-start | bytes 311816 | tf_op jit(solution)/shard_map/ppermute | solution.py:315
  27.0 6.9 %collective-permute-start.12 = (f32[232,112]{1,0:T(8,128)S(1)}, f32[232,112]{1,0:T(8,128)S(1)}, u32[]{:S(2)}, u32[]{:S(2)}) collective-permute-start(f32[232,112]{1,0:T(8,128)S(1)} %get-tuple-element.60.refs_1_.refs_9_), channel_id=1, source_target_pairs={{0,1},{1,0},{2,3},{3,2},{4,5},{5,4},{6,7},{7,6},{8,9},{9,8},{10,11... | collective-permute-start | bytes 311816 | tf_op jit(solution)/shard_map/ppermute | solution.py:315
  29.7 4.8 %collective-permute-start.13 = (f32[232,112]{1,0:T(8,128)S(1)}, f32[232,112]{1,0:T(8,128)S(1)}, u32[]{:S(2)}, u32[]{:S(2)}) collective-permute-start(f32[232,112]{1,0:T(8,128)S(1)} %get-tuple-element.61.refs_2_.refs_10_), channel_id=1, source_target_pairs={{0,1},{1,3},{2,0},{3,2},{4,8},{5,9},{6,10},{7,11},{8,4},{9,5},{10,... | collective-permute-start | bytes 311816 | tf_op jit(solution)/shard_map/ppermute | solution.py:315
  29.8 4.8 %collective-permute-start.14 = (f32[232,112]{1,0:T(8,128)S(1)}, f32[232,112]{1,0:T(8,128)S(1)}, u32[]{:S(2)}, u32[]{:S(2)}) collective-permute-start(f32[232,112]{1,0:T(8,128)S(1)} %get-tuple-element.62.refs_3_.refs_11_), channel_id=1, source_target_pairs={{0,4},{1,5},{2,6},{3,7},{4,0},{5,1},{6,2},{7,3},{8,12},{9,13},{10,... | collective-permute-start | bytes 311816 | tf_op jit(solution)/shard_map/ppermute | solution.py:315
  34.9 5.3 %collective-permute-start.17 = (f32[136,112]{1,0:T(8,128)S(1)}, f32[136,112]{1,0:T(8,128)S(1)}, u32[]{:S(2)}, u32[]{:S(2)}) collective-permute-start(f32[136,112]{1,0:T(8,128)S(1)} %second_coeffs.1.refs_0_), channel_id=1, source_target_pairs={{0,3},{1,2},{2,1},{3,0},{4,7},{5,6},{6,5},{7,4},{8,11},{9,10},{10,... | collective-permute-start | bytes 182792 | tf_op jit(solution)/shard_map/ppermute | solution.py:319
  36.4 4.5 %collective-permute-start.16 = (f32[136,112]{1,0:T(8,128)S(1)}, f32[136,112]{1,0:T(8,128)S(1)}, u32[]{:S(2)}, u32[]{:S(2)}) collective-permute-start(f32[136,112]{1,0:T(8,128)S(1)} %second_coeffs.1.refs_0_), channel_id=1, source_target_pairs={{0,2},{1,3},{2,0},{3,1},{4,6},{5,7},{6,4},{7,5},{8,10},{9,11},{10,... | collective-permute-start | bytes 182792 | tf_op jit(solution)/shard_map/ppermute | solution.py:319
  37.7 4.3 %collective-permute-start.15 = (f32[136,112]{1,0:T(8,128)S(1)}, f32[136,112]{1,0:T(8,128)S(1)}, u32[]{:S(2)}, u32[]{:S(2)}) collective-permute-start(f32[136,112]{1,0:T(8,128)S(1)} %second_coeffs.1.refs_0_), channel_id=1, source_target_pairs={{0,1},{1,0},{2,3},{3,2},{4,5},{5,4},{6,7},{7,6},{8,9},{9,8},{10,11... | collective-permute-start | bytes 182792 | tf_op jit(solution)/shard_map/ppermute | solution.py:319
  42.6 3.5 %collective-permute-start.18 = (f32[232,112]{1,0:T(8,128)S(1)}, f32[232,112]{1,0:T(8,128)S(1)}, u32[]{:S(2)}, u32[]{:S(2)}) collective-permute-start(f32[232,112]{1,0:T(8,128)S(1)} %get-tuple-element.63.refs_8_), channel_id=1, source_target_pairs={{0,4},{1,2},{2,1},{3,7},{4,0},{5,6},{6,5},{7,3},{8,12},{9,10},{10,... | collective-permute-start | bytes 311816 | tf_op jit(solution)/shard_map/ppermute | solution.py:315
  42.6 6.9 %collective-permute-start.19 = (f32[232,112]{1,0:T(8,128)S(1)}, f32[232,112]{1,0:T(8,128)S(1)}, u32[]{:S(2)}, u32[]{:S(2)}) collective-permute-start(f32[232,112]{1,0:T(8,128)S(1)} %get-tuple-element.64.refs_9_), channel_id=1, source_target_pairs={{0,1},{1,0},{2,3},{3,2},{4,5},{5,4},{6,7},{7,6},{8,9},{9,8},{10,11... | collective-permute-start | bytes 311816 | tf_op jit(solution)/shard_map/ppermute | solution.py:315
  44.8 4.8 %collective-permute-start.20 = (f32[232,112]{1,0:T(8,128)S(1)}, f32[232,112]{1,0:T(8,128)S(1)}, u32[]{:S(2)}, u32[]{:S(2)}) collective-permute-start(f32[232,112]{1,0:T(8,128)S(1)} %get-tuple-element.65.refs_10_), channel_id=1, source_target_pairs={{0,1},{1,3},{2,0},{3,2},{4,8},{5,9},{6,10},{7,11},{8,4},{9,5},{10,... | collective-permute-start | bytes 311816 | tf_op jit(solution)/shard_map/ppermute | solution.py:315
  44.8 4.8 %collective-permute-start.21 = (f32[232,112]{1,0:T(8,128)S(1)}, f32[232,112]{1,0:T(8,128)S(1)}, u32[]{:S(2)}, u32[]{:S(2)}) collective-permute-start(f32[232,112]{1,0:T(8,128)S(1)} %get-tuple-element.66.refs_11_), channel_id=1, source_target_pairs={{0,4},{1,5},{2,6},{3,7},{4,0},{5,1},{6,2},{7,3},{8,12},{9,13},{10,... | collective-permute-start | bytes 311816 | tf_op jit(solution)/shard_map/ppermute | solution.py:315

commit v7 on v6

--- a/solution.py
+++ b/solution.py
@@ -131,9 +131,8 @@
 
 def sum_of_pair(mine_ref, got_ref, depth, top):
     mine, got = mine_ref[:depth, :], got_ref[:depth, :]
-    if top is not None:
-        mine, got = mine * (scale_of(mine_ref) / top), got * (scale_of(got_ref) / top)
-    return mine + got
+    total = mine + got
+    return total if top is None else total * (1.0 / top)
 
 
 def coeffs_kernel(scaled, counts_ref, modes_ref, *refs):
@@ -206,9 +205,7 @@
         curvature += column_sum(vector_ref[...] * value)
         largest = jnp.maximum(largest, jnp.max(jnp.abs(value), axis=0, keepdims=True))
     largest = jnp.where(largest > 0.0, largest, 1.0)
-    inverse = 1.0 / largest
     for image_ref in image_refs:
-        image_ref[:depth, :] = image_ref[:depth, :] * inverse
         set_scale(image_ref, largest)
     sums_ref[0:1, :] = 0.5 * norm
     sums_ref[1:2, :] = curvature
@@ -225,6 +222,7 @@
     own_scale = scale_of(base_refs[0])
     top = widest(own_scale, got_part_refs, counts)
     own_factor = own_scale / top
+    inverse = 1.0 / scale_of(image_refs[0])
     mixed, square, reach, bend = 0.0, 0.0, 0.0, 0.0
     for face, base_ref, got_ref, vector_ref, count in zip(faces, base_refs, got_part_refs, vector_refs, counts):
         field = base_ref[:depth, :] * own_factor - masked(got_ref[:depth, :] * (scale_of(got_ref) / top), count)
@@ -235,7 +233,7 @@
         field = vector_ref[...]
         mixed += column_sum(first_ref[...] * field)
         square += column_sum(field * field)
-        reach += column_sum(field * image_ref[:depth, :])
+        reach += column_sum(field * (image_ref[:depth, :] * inverse))
         bend += column_sum(field * value)
         turned_ref[face] = field.T
     cross = (2.0 * scale_of(image_refs[0])) * reach

time: 62.9 us -> 62.8 us (level)
  no operation moved by 1% of the time
where the time goes in v7:
time: 62.8 us; the launch traced here: 62.6 us
  starting transfers between devices  24.3 us (39%)
  waiting for transfers between devices  19.4 us (31%)
  blocking collectives  11.1 us (18%)
  Pallas kernels  7.79 us (12%)
    ppermute x16, starting transfers between devices, swap(): lax.ppermute(field, ('row', 'col'), pairs)  17.2 us
    ppermute x16, waiting for transfers between devices, swap(): lax.ppermute(field, ('row', 'col'), pairs)  12.9 us
    all_to_all x1, blocking collectives, on_device(): every = lax.all_to_all(sums, ('col', 'row'), 0, 0)  11.1 us
    pallas_call x12, Pallas kernels, run(): pl.pallas_call(kernel, name=name, out_shape=outs, in_specs=in_specs, out_...  7.79 us
    ppermute x6, starting transfers between devices, gather(): return [block] + [lax.ppermute(block, 'col', pairs) for pairs in steps]  7.11 us
    ppermute x6, waiting for transfers between devices, gather(): return [block] + [lax.ppermute(block, 'col', pairs) for pairs in steps]  6.49 us
  transfers between devices with their start and end apart: 22, of which 13 were waited for; matrix products, arithmetic and copies ran while one was open for 0% of the time, Pallas kernels for 3%

profile of v7, /device:TPU:0, one launch (start us, length us, event | category | flops | bytes accessed | tf_op | source)
XLA Modules:
  0.0 62.6 jit_solution(9706473488199358279)
XLA Ops:
  0.0 1.4 %gap.1 = (f32[224,112]{1,0:T(8,128)S(1)}, f32[224,112]{1,0:T(8,128)S(1)}, f32[224,112]{1,0:T(8,128)S(1)}, f32[224,112]{1,0:T(8,128)S(1)}) custom-call(bf16[112,4,224]{2,1,0:T(4,128)(2,1)} %bitcast.8), custom_call_target="tpu_custom_call" | custom-call | bytes 200704 | tf_op jit(solution)/shard_map/gap/pallas_call | solution.py:287
  1.4 0.6 collective-permute-start
  1.9 4.0 %collective-permute-start.1 = (f32[224,112]{1,0:T(8,128)S(1)}, f32[224,112]{1,0:T(8,128)S(1)}, u32[]{:S(2)}, u32[]{:S(2)}) collective-permute-start(f32[224,112]{1,0:T(8,128)S(1)} %get-tuple-element.45.refs_1_), channel_id=1, source_target_pairs={{0,1},{1,0},{2,3},{3,2},{4,5},{5,4},{6,7},{7,6},{8,9},{9,8},{10,11... | collective-permute-start | bytes 301064 | tf_op jit(solution)/shard_map/ppermute | solution.py:313
  5.9 0.0 collective-permute-start.2
  5.9 1.7 %collective-permute-start.3 = (f32[224,112]{1,0:T(8,128)S(1)}, f32[224,112]{1,0:T(8,128)S(1)}, u32[]{:S(2)}, u32[]{:S(2)}) collective-permute-start(f32[224,112]{1,0:T(8,128)S(1)} %get-tuple-element.41.after_ref.refs_3_), channel_id=1, source_target_pairs={{0,4},{1,5},{2,6},{3,7},{4,0},{5,1},{6,2},{7,3},{8,12},{9,13},{10,... | collective-permute-start | bytes 301064 | tf_op jit(solution)/shard_map/ppermute | solution.py:313
  7.6 1.7 %prepare.1 = (s32[4,112]{1,0:T(4,128)S(1)}, bf16[128,896]{1,0:T(8,128)(2,1)S(1)}, bf16[896,896]{1,0:T(8,128)(2,1)S(1)}, bf16[896,128]{1,0:T(8,128)(2,1)S(1)}, bf16[128,1536]{1,0:T(8,128)(2,1)S(1)}) custom-call(s32[1,1,4]{2,1,0:T(1,128)} %rows_hbm.1, bf16[128,896]{1,0:T(8,128)(2,1)} %bitcast.7, f32[128,512]{1,0:T(8,128)} %bitcast.6, ...), custom_call_target="tpu_custom_call" | custom-call | bytes 2197520 | tf_op jit(solution)/shard_map/prepare/pallas_call | solution.py:287
  9.3 1.9 %collective-permute-done.1.refs_5_ = f32[224,112]{1,0:T(8,128)S(1)} collective-permute-done((f32[224,112]{1,0:T(8,128)S(1)}, f32[224,112]{1,0:T(8,128)S(1)}, u32[]{:S(2)}, u32[]{:S(2)}) %collective-permute-start.1) | collective-permute-done | bytes 100384 | tf_op jit(solution)/shard_map/ppermute | solution.py:313
  11.2 0.3 first_coeffs.1.refs_0_
  11.5 1.5 %collective-permute-start.6 = (f32[128,112]{1,0:T(8,128)S(1)}, f32[128,112]{1,0:T(8,128)S(1)}, u32[]{:S(2)}, u32[]{:S(2)}) collective-permute-start(f32[128,112]{1,0:T(8,128)S(1)} %first_coeffs.1.refs_0_), channel_id=1, source_target_pairs={{0,3},{1,2},{2,1},{3,0},{4,7},{5,6},{6,5},{7,4},{8,11},{9,10},{10,... | collective-permute-start | bytes 172040 | tf_op jit(solution)/shard_map/ppermute | solution.py:317
  13.0 0.7 %collective-permute-start.5 = (f32[128,112]{1,0:T(8,128)S(1)}, f32[128,112]{1,0:T(8,128)S(1)}, u32[]{:S(2)}, u32[]{:S(2)}) collective-permute-start(f32[128,112]{1,0:T(8,128)S(1)} %first_coeffs.1.refs_0_), channel_id=1, source_target_pairs={{0,2},{1,3},{2,0},{3,1},{4,6},{5,7},{6,4},{7,5},{8,10},{9,11},{10,... | collective-permute-start | bytes 172040 | tf_op jit(solution)/shard_map/ppermute | solution.py:317
  13.8 1.3 %collective-permute-start.4 = (f32[128,112]{1,0:T(8,128)S(1)}, f32[128,112]{1,0:T(8,128)S(1)}, u32[]{:S(2)}, u32[]{:S(2)}) collective-permute-start(f32[128,112]{1,0:T(8,128)S(1)} %first_coeffs.1.refs_0_), channel_id=1, source_target_pairs={{0,1},{1,0},{2,3},{3,2},{4,5},{5,4},{6,7},{7,6},{8,9},{9,8},{10,11... | collective-permute-start | bytes 172040 | tf_op jit(solution)/shard_map/ppermute | solution.py:317
  15.1 2.1 %collective-permute-done.6.refs_3_ = f32[128,112]{1,0:T(8,128)S(1)} collective-permute-done((f32[128,112]{1,0:T(8,128)S(1)}, f32[128,112]{1,0:T(8,128)S(1)}, u32[]{:S(2)}, u32[]{:S(2)}) %collective-permute-start.6) | collective-permute-done | bytes 57376 | tf_op jit(solution)/shard_map/ppermute | solution.py:317
  17.2 0.6 collective-permute-done.5.refs_2_
  17.7 0.3 collective-permute-done.4.refs_1_
  18.0 0.5 first_coarse.1
  18.5 0.1 collective-permute-start.7
  18.6 2.8 %collective-permute-start.8 = (f32[224,112]{1,0:T(8,128)S(1)}, f32[224,112]{1,0:T(8,128)S(1)}, u32[]{:S(2)}, u32[]{:S(2)}) collective-permute-start(f32[224,112]{1,0:T(8,128)S(1)} %get-tuple-element.51.refs_9_), channel_id=1, source_target_pairs={{0,1},{1,0},{2,3},{3,2},{4,5},{5,4},{6,7},{7,6},{8,9},{9,8},{10,11... | collective-permute-start | bytes 301064 | tf_op jit(solution)/shard_map/ppermute | solution.py:313
  21.4 0.0 collective-permute-start.9
  21.4 1.7 %collective-permute-start.10 = (f32[224,112]{1,0:T(8,128)S(1)}, f32[224,112]{1,0:T(8,128)S(1)}, u32[]{:S(2)}, u32[]{:S(2)}) collective-permute-start(f32[224,112]{1,0:T(8,128)S(1)} %get-tuple-element.53.refs_11_), channel_id=1, source_target_pairs={{0,4},{1,5},{2,6},{3,7},{4,0},{5,1},{6,2},{7,3},{8,12},{9,13},{10,... | collective-permute-start | bytes 301064 | tf_op jit(solution)/shard_map/ppermute | solution.py:313
  23.1 0.1 first_base.1
  23.2 2.2 %collective-permute-done.8.refs_5_ = f32[224,112]{1,0:T(8,128)S(1)} collective-permute-done((f32[224,112]{1,0:T(8,128)S(1)}, f32[224,112]{1,0:T(8,128)S(1)}, u32[]{:S(2)}, u32[]{:S(2)}) %collective-permute-start.8) | collective-permute-done | bytes 100384 | tf_op jit(solution)/shard_map/ppermute | solution.py:313
  25.4 0.8 %collective-permute-done.9.refs_6_ = f32[224,112]{1,0:T(8,128)S(1)} collective-permute-done((f32[224,112]{1,0:T(8,128)S(1)}, f32[224,112]{1,0:T(8,128)S(1)}, u32[]{:S(2)}, u32[]{:S(2)}) %collective-permute-start.9) | collective-permute-done | bytes 100384 | tf_op jit(solution)/shard_map/ppermute | solution.py:313
  26.2 0.7 %first.1 = (f32[224,112]{1,0:T(8,128)S(1)}, f32[224,112]{1,0:T(8,128)S(1)}, f32[224,112]{1,0:T(8,128)S(1)}, f32[224,112]{1,0:T(8,128)S(1)}, f32[232,112]{1,0:T(8...) custom-call(s32[4,112]{1,0:T(4,128)S(1)} %get-tuple-element.42.count, ...), custom_call_target="tpu_custom_call" | custom-call | bytes 2410240 | tf_op jit(solution)/shard_map/first/pallas_call | solution.py:287
  26.9 0.1 collective-permute-start.11
  27.0 2.7 %collective-permute-start.12 = (f32[232,112]{1,0:T(8,128)S(1)}, f32[232,112]{1,0:T(8,128)S(1)}, u32[]{:S(2)}, u32[]{:S(2)}) collective-permute-start(f32[232,112]{1,0:T(8,128)S(1)} %get-tuple-element.60.refs_1_.refs_9_), channel_id=1, source_target_pairs={{0,1},{1,0},{2,3},{3,2},{4,5},{5,4},{6,7},{7,6},{8,9},{9,8},{10,11... | collective-permute-start | bytes 311816 | tf_op jit(solution)/shard_map/ppermute | solution.py:313
  29.7 0.0 collective-permute-start.13
  29.7 0.4 collective-permute-start.14
  30.2 3.7 %collective-permute-done.12.refs_5_ = f32[232,112]{1,0:T(8,128)S(1)} collective-permute-done((f32[232,112]{1,0:T(8,128)S(1)}, f32[232,112]{1,0:T(8,128)S(1)}, u32[]{:S(2)}, u32[]{:S(2)}) %collective-permute-start.12) | collective-permute-done | bytes 103968 | tf_op jit(solution)/shard_map/ppermute | solution.py:313
  33.9 0.6 %collective-permute-done.13.refs_6_ = f32[232,112]{1,0:T(8,128)S(1)} collective-permute-done((f32[232,112]{1,0:T(8,128)S(1)}, f32[232,112]{1,0:T(8,128)S(1)}, u32[]{:S(2)}, u32[]{:S(2)}) %collective-permute-start.13) | collective-permute-done | bytes 103968 | tf_op jit(solution)/shard_map/ppermute | solution.py:313
  34.5 0.4 second_coeffs.1.refs_0_
  34.9 1.5 %collective-permute-start.17 = (f32[136,112]{1,0:T(8,128)S(1)}, f32[136,112]{1,0:T(8,128)S(1)}, u32[]{:S(2)}, u32[]{:S(2)}) collective-permute-start(f32[136,112]{1,0:T(8,128)S(1)} %second_coeffs.1.refs_0_), channel_id=1, source_target_pairs={{0,3},{1,2},{2,1},{3,0},{4,7},{5,6},{6,5},{7,4},{8,11},{9,10},{10,... | collective-permute-start | bytes 182792 | tf_op jit(solution)/shard_map/ppermute | solution.py:317
  36.4 1.3 %collective-permute-start.16 = (f32[136,112]{1,0:T(8,128)S(1)}, f32[136,112]{1,0:T(8,128)S(1)}, u32[]{:S(2)}, u32[]{:S(2)}) collective-permute-start(f32[136,112]{1,0:T(8,128)S(1)} %second_coeffs.1.refs_0_), channel_id=1, source_target_pairs={{0,2},{1,3},{2,0},{3,1},{4,6},{5,7},{6,4},{7,5},{8,10},{9,11},{10,... | collective-permute-start | bytes 182792 | tf_op jit(solution)/shard_map/ppermute | solution.py:317
  37.7 0.8 %collective-permute-start.15 = (f32[136,112]{1,0:T(8,128)S(1)}, f32[136,112]{1,0:T(8,128)S(1)}, u32[]{:S(2)}, u32[]{:S(2)}) collective-permute-start(f32[136,112]{1,0:T(8,128)S(1)} %second_coeffs.1.refs_0_), channel_id=1, source_target_pairs={{0,1},{1,0},{2,3},{3,2},{4,5},{5,4},{6,7},{7,6},{8,9},{9,8},{10,11... | collective-permute-start | bytes 182792 | tf_op jit(solution)/shard_map/ppermute | solution.py:317
  38.5 1.7 %collective-permute-done.17.refs_3_ = f32[136,112]{1,0:T(8,128)S(1)} collective-permute-done((f32[136,112]{1,0:T(8,128)S(1)}, f32[136,112]{1,0:T(8,128)S(1)}, u32[]{:S(2)}, u32[]{:S(2)}) %collective-permute-start.17) | collective-permute-done | bytes 60960 | tf_op jit(solution)/shard_map/ppermute | solution.py:317
  40.2 0.7 %collective-permute-done.16.refs_2_ = f32[136,112]{1,0:T(8,128)S(1)} collective-permute-done((f32[136,112]{1,0:T(8,128)S(1)}, f32[136,112]{1,0:T(8,128)S(1)}, u32[]{:S(2)}, u32[]{:S(2)}) %collective-permute-start.16) | collective-permute-done | bytes 60960 | tf_op jit(solution)/shard_map/ppermute | solution.py:317
  40.9 1.1 %collective-permute-done.15.refs_1_ = f32[136,112]{1,0:T(8,128)S(1)} collective-permute-done((f32[136,112]{1,0:T(8,128)S(1)}, f32[136,112]{1,0:T(8,128)S(1)}, u32[]{:S(2)}, u32[]{:S(2)}) %collective-permute-start.15) | collective-permute-done | bytes 60960 | tf_op jit(solution)/shard_map/ppermute | solution.py:317
  42.0 0.5 second_coarse.1
  42.5 0.1 collective-permute-start.18
  42.6 2.2 %collective-permute-start.19 = (f32[232,112]{1,0:T(8,128)S(1)}, f32[232,112]{1,0:T(8,128)S(1)}, u32[]{:S(2)}, u32[]{:S(2)}) collective-permute-start(f32[232,112]{1,0:T(8,128)S(1)} %get-tuple-element.64.refs_9_), channel_id=1, source_target_pairs={{0,1},{1,0},{2,3},{3,2},{4,5},{5,4},{6,7},{7,6},{8,9},{9,8},{10,11... | collective-permute-start | bytes 311816 | tf_op jit(solution)/shard_map/ppermute | solution.py:313
  44.8 0.0 collective-permute-start.20
  44.8 0.9 %collective-permute-start.21 = (f32[232,112]{1,0:T(8,128)S(1)}, f32[232,112]{1,0:T(8,128)S(1)}, u32[]{:S(2)}, u32[]{:S(2)}) collective-permute-start(f32[232,112]{1,0:T(8,128)S(1)} %get-tuple-element.66.refs_11_), channel_id=1, source_target_pairs={{0,4},{1,5},{2,6},{3,7},{4,0},{5,1},{6,2},{7,3},{8,12},{9,13},{10,... | collective-permute-start | bytes 311816 | tf_op jit(solution)/shard_map/ppermute | solution.py:313
  45.8 0.2 columns.1.refs_16_.first_ref
  45.9 0.1 second_base.1
  46.1 3.5 %collective-permute-done.19.refs_5_ = f32[232,112]{1,0:T(8,128)S(1)} collective-permute-done((f32[232,112]{1,0:T(8,128)S(1)}, f32[232,112]{1,0:T(8,128)S(1)}, u32[]{:S(2)}, u32[]{:S(2)}) %collective-permute-start.19) | collective-permute-done | bytes 103968 | tf_op jit(solution)/shard_map/ppermute | solution.py:313
  49.5 0.1 collective-permute-done.20.refs_6_
  49.6 0.8 %second.1 = (f32[4,112,224]{2,1,0:T(8,128)S(1)}, f32[32,8,112]{2,1,0:T(8,128)S(1)}) custom-call(s32[4,112]{1,0:T(4,128)S(1)} %get-tuple-element.42.counts_ref, bf16[896,896]{1,0:T(8,128)(2,1)S(1)} %get-tuple-element.43.operator_ref, f32[2,112]{1,0:T(2,128)S(1)} %get-tuple-element.58.sums_in_ref, f32[232,112]{1,0:T(8,128)S(1)} %get-tuple-element.67.refs_0_, ...), custom_call_target="tpu_custom_call" | custom-call | bytes 3658368 | tf_op jit(solution)/shard_map/second/pallas_call | solution.py:287
  50.4 11.1 %all_to_all.5.sums_ref = f32[32,8,112]{2,1,0:T(8,128)S(1)} all-to-all(f32[32,8,112]{2,1,0:T(8,128)S(1)} %get-tuple-element.75), channel_id=1, replica_groups=mesh['row'=8,'col'=4] {'col','row'}, dimensions={0} | all-to-all | bytes 229376 | tf_op jit(solution)/shard_map/all_to_all | solution.py:384
  61.5 1.2 %last.1 = f32[112,4,224]{2,1,0:T(4,128)} custom-call(f32[32,8,112]{2,1,0:T(8,128)S(1)} %all_to_all.5.sums_ref, f32[4,112,224]{2,1,0:T(8,128)S(1)} %columns.1.refs_16_.first_ref, f32[4,112,224]{2,1,0:T(8,128)S(1)} %get-tuple-element.76.second_ref), custom_call_target="tpu_custom_call" | custom-call | bytes 917504 | tf_op jit(solution)/shard_map/last/pallas_call | solution.py:287
  (9 shorter events, 0.0 us)
Async XLA Ops:
  1.4 7.9 %collective-permute-start = (f32[224,112]{1,0:T(8,128)S(1)}, f32[224,112]{1,0:T(8,128)S(1)}, u32[]{:S(2)}, u32[]{:S(2)}) collective-permute-start(f32[224,112]{1,0:T(8,128)S(1)} %get-tuple-element.44.refs_0_), channel_id=1, source_target_pairs={{0,4},{1,2},{2,1},{3,7},{4,0},{5,6},{6,5},{7,3},{8,12},{9,10},{10,... | collective-permute-start | bytes 301064 | tf_op jit(solution)/shard_map/ppermute | solution.py:313
  1.9 9.3 %collective-permute-start.1 = (f32[224,112]{1,0:T(8,128)S(1)}, f32[224,112]{1,0:T(8,128)S(1)}, u32[]{:S(2)}, u32[]{:S(2)}) collective-permute-start(f32[224,112]{1,0:T(8,128)S(1)} %get-tuple-element.45.refs_1_), channel_id=1, source_target_pairs={{0,1},{1,0},{2,3},{3,2},{4,5},{5,4},{6,7},{7,6},{8,9},{9,8},{10,11... | collective-permute-start | bytes 301064 | tf_op jit(solution)/shard_map/ppermute | solution.py:313
  5.9 5.3 %collective-permute-start.2 = (f32[224,112]{1,0:T(8,128)S(1)}, f32[224,112]{1,0:T(8,128)S(1)}, u32[]{:S(2)}, u32[]{:S(2)}) collective-permute-start(f32[224,112]{1,0:T(8,128)S(1)} %get-tuple-element.46.refs_2_), channel_id=1, source_target_pairs={{0,1},{1,3},{2,0},{3,2},{4,8},{5,9},{6,10},{7,11},{8,4},{9,5},{10,... | collective-permute-start | bytes 301064 | tf_op jit(solution)/shard_map/ppermute | solution.py:313
  5.9 5.3 %collective-permute-start.3 = (f32[224,112]{1,0:T(8,128)S(1)}, f32[224,112]{1,0:T(8,128)S(1)}, u32[]{:S(2)}, u32[]{:S(2)}) collective-permute-start(f32[224,112]{1,0:T(8,128)S(1)} %get-tuple-element.41.after_ref.refs_3_), channel_id=1, source_target_pairs={{0,4},{1,5},{2,6},{3,7},{4,0},{5,1},{6,2},{7,3},{8,12},{9,13},{10,... | collective-permute-start | bytes 301064 | tf_op jit(solution)/shard_map/ppermute | solution.py:313
  11.5 5.6 %collective-permute-start.6 = (f32[128,112]{1,0:T(8,128)S(1)}, f32[128,112]{1,0:T(8,128)S(1)}, u32[]{:S(2)}, u32[]{:S(2)}) collective-permute-start(f32[128,112]{1,0:T(8,128)S(1)} %first_coeffs.1.refs_0_), channel_id=1, source_target_pairs={{0,3},{1,2},{2,1},{3,0},{4,7},{5,6},{6,5},{7,4},{8,11},{9,10},{10,... | collective-permute-start | bytes 172040 | tf_op jit(solution)/shard_map/ppermute | solution.py:317
  13.0 4.7 %collective-permute-start.5 = (f32[128,112]{1,0:T(8,128)S(1)}, f32[128,112]{1,0:T(8,128)S(1)}, u32[]{:S(2)}, u32[]{:S(2)}) collective-permute-start(f32[128,112]{1,0:T(8,128)S(1)} %first_coeffs.1.refs_0_), channel_id=1, source_target_pairs={{0,2},{1,3},{2,0},{3,1},{4,6},{5,7},{6,4},{7,5},{8,10},{9,11},{10,... | collective-permute-start | bytes 172040 | tf_op jit(solution)/shard_map/ppermute | solution.py:317
  13.8 4.3 %collective-permute-start.4 = (f32[128,112]{1,0:T(8,128)S(1)}, f32[128,112]{1,0:T(8,128)S(1)}, u32[]{:S(2)}, u32[]{:S(2)}) collective-permute-start(f32[128,112]{1,0:T(8,128)S(1)} %first_coeffs.1.refs_0_), channel_id=1, source_target_pairs={{0,1},{1,0},{2,3},{3,2},{4,5},{5,4},{6,7},{7,6},{8,9},{9,8},{10,11... | collective-permute-start | bytes 172040 | tf_op jit(solution)/shard_map/ppermute | solution.py:317
  18.5 4.6 %collective-permute-start.7 = (f32[224,112]{1,0:T(8,128)S(1)}, f32[224,112]{1,0:T(8,128)S(1)}, u32[]{:S(2)}, u32[]{:S(2)}) collective-permute-start(f32[224,112]{1,0:T(8,128)S(1)} %get-tuple-element.50.refs_8_), channel_id=1, source_target_pairs={{0,4},{1,2},{2,1},{3,7},{4,0},{5,6},{6,5},{7,3},{8,12},{9,10},{10,... | collective-permute-start | bytes 301064 | tf_op jit(solution)/shard_map/ppermute | solution.py:313
  18.6 6.8 %collective-permute-start.8 = (f32[224,112]{1,0:T(8,128)S(1)}, f32[224,112]{1,0:T(8,128)S(1)}, u32[]{:S(2)}, u32[]{:S(2)}) collective-permute-start(f32[224,112]{1,0:T(8,128)S(1)} %get-tuple-element.51.refs_9_), channel_id=1, source_target_pairs={{0,1},{1,0},{2,3},{3,2},{4,5},{5,4},{6,7},{7,6},{8,9},{9,8},{10,11... | collective-permute-start | bytes 301064 | tf_op jit(solution)/shard_map/ppermute | solution.py:313
  21.4 4.8 %collective-permute-start.9 = (f32[224,112]{1,0:T(8,128)S(1)}, f32[224,112]{1,0:T(8,128)S(1)}, u32[]{:S(2)}, u32[]{:S(2)}) collective-permute-start(f32[224,112]{1,0:T(8,128)S(1)} %get-tuple-element.52.refs_10_), channel_id=1, source_target_pairs={{0,1},{1,3},{2,0},{3,2},{4,8},{5,9},{6,10},{7,11},{8,4},{9,5},{10,... | collective-permute-start | bytes 301064 | tf_op jit(solution)/shard_map/ppermute | solution.py:313
  21.4 4.8 %collective-permute-start.10 = (f32[224,112]{1,0:T(8,128)S(1)}, f32[224,112]{1,0:T(8,128)S(1)}, u32[]{:S(2)}, u32[]{:S(2)}) collective-permute-start(f32[224,112]{1,0:T(8,128)S(1)} %get-tuple-element.53.refs_11_), channel_id=1, source_target_pairs={{0,4},{1,5},{2,6},{3,7},{4,0},{5,1},{6,2},{7,3},{8,12},{9,13},{10,... | collective-permute-start | bytes 301064 | tf_op jit(solution)/shard_map/ppermute | solution.py:313
  26.9 3.3 %collective-permute-start.11 = (f32[232,112]{1,0:T(8,128)S(1)}, f32[232,112]{1,0:T(8,128)S(1)}, u32[]{:S(2)}, u32[]{:S(2)}) collective-permute-start(f32[232,112]{1,0:T(8,128)S(1)} %get-tuple-element.59.refs_0_.refs_8_), channel_id=1, source_target_pairs={{0,4},{1,2},{2,1},{3,7},{4,0},{5,6},{6,5},{7,3},{8,12},{9,10},{10,... | collective-permute-start | bytes 311816 | tf_op jit(solution)/shard_map/ppermute | solution.py:313
  27.0 6.9 %collective-permute-start.12 = (f32[232,112]{1,0:T(8,128)S(1)}, f32[232,112]{1,0:T(8,128)S(1)}, u32[]{:S(2)}, u32[]{:S(2)}) collective-permute-start(f32[232,112]{1,0:T(8,128)S(1)} %get-tuple-element.60.refs_1_.refs_9_), channel_id=1, source_target_pairs={{0,1},{1,0},{2,3},{3,2},{4,5},{5,4},{6,7},{7,6},{8,9},{9,8},{10,11... | collective-permute-start | bytes 311816 | tf_op jit(solution)/shard_map/ppermute | solution.py:313
  29.7 4.8 %collective-permute-start.13 = (f32[232,112]{1,0:T(8,128)S(1)}, f32[232,112]{1,0:T(8,128)S(1)}, u32[]{:S(2)}, u32[]{:S(2)}) collective-permute-start(f32[232,112]{1,0:T(8,128)S(1)} %get-tuple-element.61.refs_2_.refs_10_), channel_id=1, source_target_pairs={{0,1},{1,3},{2,0},{3,2},{4,8},{5,9},{6,10},{7,11},{8,4},{9,5},{10,... | collective-permute-start | bytes 311816 | tf_op jit(solution)/shard_map/ppermute | solution.py:313
  29.7 4.8 %collective-permute-start.14 = (f32[232,112]{1,0:T(8,128)S(1)}, f32[232,112]{1,0:T(8,128)S(1)}, u32[]{:S(2)}, u32[]{:S(2)}) collective-permute-start(f32[232,112]{1,0:T(8,128)S(1)} %get-tuple-element.62.refs_3_.refs_11_), channel_id=1, source_target_pairs={{0,4},{1,5},{2,6},{3,7},{4,0},{5,1},{6,2},{7,3},{8,12},{9,13},{10,... | collective-permute-start | bytes 311816 | tf_op jit(solution)/shard_map/ppermute | solution.py:313
  34.9 5.3 %collective-permute-start.17 = (f32[136,112]{1,0:T(8,128)S(1)}, f32[136,112]{1,0:T(8,128)S(1)}, u32[]{:S(2)}, u32[]{:S(2)}) collective-permute-start(f32[136,112]{1,0:T(8,128)S(1)} %second_coeffs.1.refs_0_), channel_id=1, source_target_pairs={{0,3},{1,2},{2,1},{3,0},{4,7},{5,6},{6,5},{7,4},{8,11},{9,10},{10,... | collective-permute-start | bytes 182792 | tf_op jit(solution)/shard_map/ppermute | solution.py:317
  36.4 4.5 %collective-permute-start.16 = (f32[136,112]{1,0:T(8,128)S(1)}, f32[136,112]{1,0:T(8,128)S(1)}, u32[]{:S(2)}, u32[]{:S(2)}) collective-permute-start(f32[136,112]{1,0:T(8,128)S(1)} %second_coeffs.1.refs_0_), channel_id=1, source_target_pairs={{0,2},{1,3},{2,0},{3,1},{4,6},{5,7},{6,4},{7,5},{8,10},{9,11},{10,... | collective-permute-start | bytes 182792 | tf_op jit(solution)/shard_map/ppermute | solution.py:317
  37.7 4.3 %collective-permute-start.15 = (f32[136,112]{1,0:T(8,128)S(1)}, f32[136,112]{1,0:T(8,128)S(1)}, u32[]{:S(2)}, u32[]{:S(2)}) collective-permute-start(f32[136,112]{1,0:T(8,128)S(1)} %second_coeffs.1.refs_0_), channel_id=1, source_target_pairs={{0,1},{1,0},{2,3},{3,2},{4,5},{5,4},{6,7},{7,6},{8,9},{9,8},{10,11... | collective-permute-start | bytes 182792 | tf_op jit(solution)/shard_map/ppermute | solution.py:317
  42.5 3.5 %collective-permute-start.18 = (f32[232,112]{1,0:T(8,128)S(1)}, f32[232,112]{1,0:T(8,128)S(1)}, u32[]{:S(2)}, u32[]{:S(2)}) collective-permute-start(f32[232,112]{1,0:T(8,128)S(1)} %get-tuple-element.63.refs_8_), channel_id=1, source_target_pairs={{0,4},{1,2},{2,1},{3,7},{4,0},{5,6},{6,5},{7,3},{8,12},{9,10},{10,... | collective-permute-start | bytes 311816 | tf_op jit(solution)/shard_map/ppermute | solution.py:313
  42.6 6.9 %collective-permute-start.19 = (f32[232,112]{1,0:T(8,128)S(1)}, f32[232,112]{1,0:T(8,128)S(1)}, u32[]{:S(2)}, u32[]{:S(2)}) collective-permute-start(f32[232,112]{1,0:T(8,128)S(1)} %get-tuple-element.64.refs_9_), channel_id=1, source_target_pairs={{0,1},{1,0},{2,3},{3,2},{4,5},{5,4},{6,7},{7,6},{8,9},{9,8},{10,11... | collective-permute-start | bytes 311816 | tf_op jit(solution)/shard_map/ppermute | solution.py:313
  44.8 4.8 %collective-permute-start.20 = (f32[232,112]{1,0:T(8,128)S(1)}, f32[232,112]{1,0:T(8,128)S(1)}, u32[]{:S(2)}, u32[]{:S(2)}) collective-permute-start(f32[232,112]{1,0:T(8,128)S(1)} %get-tuple-element.65.refs_10_), channel_id=1, source_target_pairs={{0,1},{1,3},{2,0},{3,2},{4,8},{5,9},{6,10},{7,11},{8,4},{9,5},{10,... | collective-permute-start | bytes 311816 | tf_op jit(solution)/shard_map/ppermute | solution.py:313
  44.8 4.8 %collective-permute-start.21 = (f32[232,112]{1,0:T(8,128)S(1)}, f32[232,112]{1,0:T(8,128)S(1)}, u32[]{:S(2)}, u32[]{:S(2)}) collective-permute-start(f32[232,112]{1,0:T(8,128)S(1)} %get-tuple-element.66.refs_11_), channel_id=1, source_target_pairs={{0,4},{1,5},{2,6},{3,7},{4,0},{5,1},{6,2},{7,3},{8,12},{9,13},{10,... | collective-permute-start | bytes 311816 | tf_op jit(solution)/shard_map/ppermute | solution.py:313

commit v8 on v7

--- a/solution.py
+++ b/solution.py
@@ -59,7 +59,11 @@
 
 
 def column_sum(value):
-    return jnp.sum(value, axis=0, keepdims=True)
+    return jnp.sum(value.reshape(-1, 8, value.shape[1]), axis=0)
+
+
+def column_total(partial_sums):
+    return jnp.sum(partial_sums, axis=0, keepdims=True)
 
 
 def gap_kernel(gap_hbm, *refs):
@@ -207,8 +211,8 @@
     largest = jnp.where(largest > 0.0, largest, 1.0)
     for image_ref in image_refs:
         set_scale(image_ref, largest)
-    sums_ref[0:1, :] = 0.5 * norm
-    sums_ref[1:2, :] = curvature
+    sums_ref[0:1, :] = 0.5 * column_total(norm)
+    sums_ref[1:2, :] = column_total(curvature)
 
 
 def second_kernel(counts_ref, operator_ref, sums_in_ref, *refs):
@@ -236,6 +240,7 @@
         reach += column_sum(field * (image_ref[:depth, :] * inverse))
         bend += column_sum(field * value)
         turned_ref[face] = field.T
+    mixed, square, reach, bend = map(column_total, (mixed, square, reach, bend))
     cross = (2.0 * scale_of(image_refs[0])) * reach
     rows = [sums_in_ref[0:1, :], sums_in_ref[1:2, :], 0.5 * mixed, 0.5 * square, cross, bend, top, top]
     table = jnp.concatenate(rows, axis=0)

time: 62.8 us -> 62.8 us (level)
  no operation moved by 1% of the time
where the time goes in v8:
time: 62.8 us; the launch traced here: 62.7 us
  starting transfers between devices  24.3 us (39%)
  waiting for transfers between devices  19.4 us (31%)
  blocking collectives  11.1 us (18%)
  Pallas kernels  7.8 us (12%)
    ppermute x16, starting transfers between devices, swap(): lax.ppermute(field, ('row', 'col'), pairs)  17.2 us
    ppermute x16, waiting for transfers between devices, swap(): lax.ppermute(field, ('row', 'col'), pairs)  12.9 us
    all_to_all x1, blocking collectives, on_device(): every = lax.all_to_all(sums, ('col', 'row'), 0, 0)  11.1 us
    pallas_call x12, Pallas kernels, run(): pl.pallas_call(kernel, name=name, out_shape=outs, in_specs=in_specs, out_...  7.8 us
    ppermute x6, starting transfers between devices, gather(): return [block] + [lax.ppermute(block, 'col', pairs) for pairs in steps]  7.11 us
    ppermute x6, waiting for transfers between devices, gather(): return [block] + [lax.ppermute(block, 'col', pairs) for pairs in steps]  6.49 us
  transfers between devices with their start and end apart: 22, of which 13 were waited for; matrix products, arithmetic and copies ran while one was open for 0% of the time, Pallas kernels for 3%

profile of v8, /device:TPU:0, one launch (start us, length us, event | category | flops | bytes accessed | tf_op | source)
XLA Modules:
  0.0 62.7 jit_solution(3160399820468986086)
XLA Ops:
  0.0 1.4 %gap.1 = (f32[224,112]{1,0:T(8,128)S(1)}, f32[224,112]{1,0:T(8,128)S(1)}, f32[224,112]{1,0:T(8,128)S(1)}, f32[224,112]{1,0:T(8,128)S(1)}) custom-call(bf16[112,4,224]{2,1,0:T(4,128)(2,1)} %bitcast.8), custom_call_target="tpu_custom_call" | custom-call | bytes 200704 | tf_op jit(solution)/shard_map/gap/pallas_call | solution.py:292
  1.4 0.6 collective-permute-start
  1.9 4.0 %collective-permute-start.1 = (f32[224,112]{1,0:T(8,128)S(1)}, f32[224,112]{1,0:T(8,128)S(1)}, u32[]{:S(2)}, u32[]{:S(2)}) collective-permute-start(f32[224,112]{1,0:T(8,128)S(1)} %get-tuple-element.45.refs_1_), channel_id=1, source_target_pairs={{0,1},{1,0},{2,3},{3,2},{4,5},{5,4},{6,7},{7,6},{8,9},{9,8},{10,11... | collective-permute-start | bytes 301064 | tf_op jit(solution)/shard_map/ppermute | solution.py:318
  5.9 0.0 collective-permute-start.2
  5.9 1.7 %collective-permute-start.3 = (f32[224,112]{1,0:T(8,128)S(1)}, f32[224,112]{1,0:T(8,128)S(1)}, u32[]{:S(2)}, u32[]{:S(2)}) collective-permute-start(f32[224,112]{1,0:T(8,128)S(1)} %get-tuple-element.41.after_ref.refs_3_), channel_id=1, source_target_pairs={{0,4},{1,5},{2,6},{3,7},{4,0},{5,1},{6,2},{7,3},{8,12},{9,13},{10,... | collective-permute-start | bytes 301064 | tf_op jit(solution)/shard_map/ppermute | solution.py:318
  7.6 1.7 %prepare.1 = (s32[4,112]{1,0:T(4,128)S(1)}, bf16[128,896]{1,0:T(8,128)(2,1)S(1)}, bf16[896,896]{1,0:T(8,128)(2,1)S(1)}, bf16[896,128]{1,0:T(8,128)(2,1)S(1)}, bf16[128,1536]{1,0:T(8,128)(2,1)S(1)}) custom-call(s32[1,1,4]{2,1,0:T(1,128)} %rows_hbm.1, bf16[128,896]{1,0:T(8,128)(2,1)} %bitcast.7, f32[128,512]{1,0:T(8,128)} %bitcast.6, ...), custom_call_target="tpu_custom_call" | custom-call | bytes 2197520 | tf_op jit(solution)/shard_map/prepare/pallas_call | solution.py:292
  9.3 1.9 %collective-permute-done.1.refs_5_ = f32[224,112]{1,0:T(8,128)S(1)} collective-permute-done((f32[224,112]{1,0:T(8,128)S(1)}, f32[224,112]{1,0:T(8,128)S(1)}, u32[]{:S(2)}, u32[]{:S(2)}) %collective-permute-start.1) | collective-permute-done | bytes 100384 | tf_op jit(solution)/shard_map/ppermute | solution.py:318
  11.2 0.3 first_coeffs.1.refs_0_
  11.5 1.5 %collective-permute-start.6 = (f32[128,112]{1,0:T(8,128)S(1)}, f32[128,112]{1,0:T(8,128)S(1)}, u32[]{:S(2)}, u32[]{:S(2)}) collective-permute-start(f32[128,112]{1,0:T(8,128)S(1)} %first_coeffs.1.refs_0_), channel_id=1, source_target_pairs={{0,3},{1,2},{2,1},{3,0},{4,7},{5,6},{6,5},{7,4},{8,11},{9,10},{10,... | collective-permute-start | bytes 172040 | tf_op jit(solution)/shard_map/ppermute | solution.py:322
  13.0 0.7 %collective-permute-start.5 = (f32[128,112]{1,0:T(8,128)S(1)}, f32[128,112]{1,0:T(8,128)S(1)}, u32[]{:S(2)}, u32[]{:S(2)}) collective-permute-start(f32[128,112]{1,0:T(8,128)S(1)} %first_coeffs.1.refs_0_), channel_id=1, source_target_pairs={{0,2},{1,3},{2,0},{3,1},{4,6},{5,7},{6,4},{7,5},{8,10},{9,11},{10,... | collective-permute-start | bytes 172040 | tf_op jit(solution)/shard_map/ppermute | solution.py:322
  13.8 1.3 %collective-permute-start.4 = (f32[128,112]{1,0:T(8,128)S(1)}, f32[128,112]{1,0:T(8,128)S(1)}, u32[]{:S(2)}, u32[]{:S(2)}) collective-permute-start(f32[128,112]{1,0:T(8,128)S(1)} %first_coeffs.1.refs_0_), channel_id=1, source_target_pairs={{0,1},{1,0},{2,3},{3,2},{4,5},{5,4},{6,7},{7,6},{8,9},{9,8},{10,11... | collective-permute-start | bytes 172040 | tf_op jit(solution)/shard_map/ppermute | solution.py:322
  15.1 2.1 %collective-permute-done.6.refs_3_ = f32[128,112]{1,0:T(8,128)S(1)} collective-permute-done((f32[128,112]{1,0:T(8,128)S(1)}, f32[128,112]{1,0:T(8,128)S(1)}, u32[]{:S(2)}, u32[]{:S(2)}) %collective-permute-start.6) | collective-permute-done | bytes 57376 | tf_op jit(solution)/shard_map/ppermute | solution.py:322
  17.2 0.6 collective-permute-done.5.refs_2_
  17.7 0.3 collective-permute-done.4.refs_1_
  18.0 0.5 first_coarse.1
  18.5 0.1 collective-permute-start.7
  18.6 2.8 %collective-permute-start.8 = (f32[224,112]{1,0:T(8,128)S(1)}, f32[224,112]{1,0:T(8,128)S(1)}, u32[]{:S(2)}, u32[]{:S(2)}) collective-permute-start(f32[224,112]{1,0:T(8,128)S(1)} %get-tuple-element.51.refs_9_), channel_id=1, source_target_pairs={{0,1},{1,0},{2,3},{3,2},{4,5},{5,4},{6,7},{7,6},{8,9},{9,8},{10,11... | collective-permute-start | bytes 301064 | tf_op jit(solution)/shard_map/ppermute | solution.py:318
  21.4 0.0 collective-permute-start.9
  21.4 1.7 %collective-permute-start.10 = (f32[224,112]{1,0:T(8,128)S(1)}, f32[224,112]{1,0:T(8,128)S(1)}, u32[]{:S(2)}, u32[]{:S(2)}) collective-permute-start(f32[224,112]{1,0:T(8,128)S(1)} %get-tuple-element.53.refs_11_), channel_id=1, source_target_pairs={{0,4},{1,5},{2,6},{3,7},{4,0},{5,1},{6,2},{7,3},{8,12},{9,13},{10,... | collective-permute-start | bytes 301064 | tf_op jit(solution)/shard_map/ppermute | solution.py:318
  23.1 0.1 first_base.1
  23.2 2.2 %collective-permute-done.8.refs_5_ = f32[224,112]{1,0:T(8,128)S(1)} collective-permute-done((f32[224,112]{1,0:T(8,128)S(1)}, f32[224,112]{1,0:T(8,128)S(1)}, u32[]{:S(2)}, u32[]{:S(2)}) %collective-permute-start.8) | collective-permute-done | bytes 100384 | tf_op jit(solution)/shard_map/ppermute | solution.py:318
  25.4 0.8 %collective-permute-done.9.refs_6_ = f32[224,112]{1,0:T(8,128)S(1)} collective-permute-done((f32[224,112]{1,0:T(8,128)S(1)}, f32[224,112]{1,0:T(8,128)S(1)}, u32[]{:S(2)}, u32[]{:S(2)}) %collective-permute-start.9) | collective-permute-done | bytes 100384 | tf_op jit(solution)/shard_map/ppermute | solution.py:318
  26.2 0.7 %first.1 = (f32[224,112]{1,0:T(8,128)S(1)}, f32[224,112]{1,0:T(8,128)S(1)}, f32[224,112]{1,0:T(8,128)S(1)}, f32[224,112]{1,0:T(8,128)S(1)}, f32[232,112]{1,0:T(8...) custom-call(s32[4,112]{1,0:T(4,128)S(1)} %get-tuple-element.42.count, ...), custom_call_target="tpu_custom_call" | custom-call | bytes 2410240 | tf_op jit(solution)/shard_map/first/pallas_call | solution.py:292
  26.9 0.1 collective-permute-start.11
  27.0 2.7 %collective-permute-start.12 = (f32[232,112]{1,0:T(8,128)S(1)}, f32[232,112]{1,0:T(8,128)S(1)}, u32[]{:S(2)}, u32[]{:S(2)}) collective-permute-start(f32[232,112]{1,0:T(8,128)S(1)} %get-tuple-element.60.refs_1_.refs_9_), channel_id=1, source_target_pairs={{0,1},{1,0},{2,3},{3,2},{4,5},{5,4},{6,7},{7,6},{8,9},{9,8},{10,11... | collective-permute-start | bytes 311816 | tf_op jit(solution)/shard_map/ppermute | solution.py:318
  29.7 0.0 collective-permute-start.13
  29.7 0.4 collective-permute-start.14
  30.2 3.7 %collective-permute-done.12.refs_5_ = f32[232,112]{1,0:T(8,128)S(1)} collective-permute-done((f32[232,112]{1,0:T(8,128)S(1)}, f32[232,112]{1,0:T(8,128)S(1)}, u32[]{:S(2)}, u32[]{:S(2)}) %collective-permute-start.12) | collective-permute-done | bytes 103968 | tf_op jit(solution)/shard_map/ppermute | solution.py:318
  33.9 0.6 %collective-permute-done.13.refs_6_ = f32[232,112]{1,0:T(8,128)S(1)} collective-permute-done((f32[232,112]{1,0:T(8,128)S(1)}, f32[232,112]{1,0:T(8,128)S(1)}, u32[]{:S(2)}, u32[]{:S(2)}) %collective-permute-start.13) | collective-permute-done | bytes 103968 | tf_op jit(solution)/shard_map/ppermute | solution.py:318
  34.5 0.4 second_coeffs.1.refs_0_
  34.9 1.5 %collective-permute-start.17 = (f32[136,112]{1,0:T(8,128)S(1)}, f32[136,112]{1,0:T(8,128)S(1)}, u32[]{:S(2)}, u32[]{:S(2)}) collective-permute-start(f32[136,112]{1,0:T(8,128)S(1)} %second_coeffs.1.refs_0_), channel_id=1, source_target_pairs={{0,3},{1,2},{2,1},{3,0},{4,7},{5,6},{6,5},{7,4},{8,11},{9,10},{10,... | collective-permute-start | bytes 182792 | tf_op jit(solution)/shard_map/ppermute | solution.py:322
  36.4 1.3 %collective-permute-start.16 = (f32[136,112]{1,0:T(8,128)S(1)}, f32[136,112]{1,0:T(8,128)S(1)}, u32[]{:S(2)}, u32[]{:S(2)}) collective-permute-start(f32[136,112]{1,0:T(8,128)S(1)} %second_coeffs.1.refs_0_), channel_id=1, source_target_pairs={{0,2},{1,3},{2,0},{3,1},{4,6},{5,7},{6,4},{7,5},{8,10},{9,11},{10,... | collective-permute-start | bytes 182792 | tf_op jit(solution)/shard_map/ppermute | solution.py:322
  37.7 0.8 %collective-permute-start.15 = (f32[136,112]{1,0:T(8,128)S(1)}, f32[136,112]{1,0:T(8,128)S(1)}, u32[]{:S(2)}, u32[]{:S(2)}) collective-permute-start(f32[136,112]{1,0:T(8,128)S(1)} %second_coeffs.1.refs_0_), channel_id=1, source_target_pairs={{0,1},{1,0},{2,3},{3,2},{4,5},{5,4},{6,7},{7,6},{8,9},{9,8},{10,11... | collective-permute-start | bytes 182792 | tf_op jit(solution)/shard_map/ppermute | solution.py:322
  38.5 1.7 %collective-permute-done.17.refs_3_ = f32[136,112]{1,0:T(8,128)S(1)} collective-permute-done((f32[136,112]{1,0:T(8,128)S(1)}, f32[136,112]{1,0:T(8,128)S(1)}, u32[]{:S(2)}, u32[]{:S(2)}) %collective-permute-start.17) | collective-permute-done | bytes 60960 | tf_op jit(solution)/shard_map/ppermute | solution.py:322
  40.2 0.7 %collective-permute-done.16.refs_2_ = f32[136,112]{1,0:T(8,128)S(1)} collective-permute-done((f32[136,112]{1,0:T(8,128)S(1)}, f32[136,112]{1,0:T(8,128)S(1)}, u32[]{:S(2)}, u32[]{:S(2)}) %collective-permute-start.16) | collective-permute-done | bytes 60960 | tf_op jit(solution)/shard_map/ppermute | solution.py:322
  40.9 1.1 %collective-permute-done.15.refs_1_ = f32[136,112]{1,0:T(8,128)S(1)} collective-permute-done((f32[136,112]{1,0:T(8,128)S(1)}, f32[136,112]{1,0:T(8,128)S(1)}, u32[]{:S(2)}, u32[]{:S(2)}) %collective-permute-start.15) | collective-permute-done | bytes 60960 | tf_op jit(solution)/shard_map/ppermute | solution.py:322
  42.0 0.5 second_coarse.1
  42.5 0.1 collective-permute-start.18
  42.6 2.2 %collective-permute-start.19 = (f32[232,112]{1,0:T(8,128)S(1)}, f32[232,112]{1,0:T(8,128)S(1)}, u32[]{:S(2)}, u32[]{:S(2)}) collective-permute-start(f32[232,112]{1,0:T(8,128)S(1)} %get-tuple-element.64.refs_9_), channel_id=1, source_target_pairs={{0,1},{1,0},{2,3},{3,2},{4,5},{5,4},{6,7},{7,6},{8,9},{9,8},{10,11... | collective-permute-start | bytes 311816 | tf_op jit(solution)/shard_map/ppermute | solution.py:318
  44.8 0.0 collective-permute-start.20
  44.8 0.9 %collective-permute-start.21 = (f32[232,112]{1,0:T(8,128)S(1)}, f32[232,112]{1,0:T(8,128)S(1)}, u32[]{:S(2)}, u32[]{:S(2)}) collective-permute-start(f32[232,112]{1,0:T(8,128)S(1)} %get-tuple-element.66.refs_11_), channel_id=1, source_target_pairs={{0,4},{1,5},{2,6},{3,7},{4,0},{5,1},{6,2},{7,3},{8,12},{9,13},{10,... | collective-permute-start | bytes 311816 | tf_op jit(solution)/shard_map/ppermute | solution.py:318
  45.7 0.2 columns.1.refs_16_.first_ref
  45.9 0.1 second_base.1
  46.1 3.5 %collective-permute-done.19.refs_5_ = f32[232,112]{1,0:T(8,128)S(1)} collective-permute-done((f32[232,112]{1,0:T(8,128)S(1)}, f32[232,112]{1,0:T(8,128)S(1)}, u32[]{:S(2)}, u32[]{:S(2)}) %collective-permute-start.19) | collective-permute-done | bytes 103968 | tf_op jit(solution)/shard_map/ppermute | solution.py:318
  49.5 0.1 collective-permute-done.20.refs_6_
  49.6 0.8 %second.1 = (f32[4,112,224]{2,1,0:T(8,128)S(1)}, f32[32,8,112]{2,1,0:T(8,128)S(1)}) custom-call(s32[4,112]{1,0:T(4,128)S(1)} %get-tuple-element.42.counts_ref, bf16[896,896]{1,0:T(8,128)(2,1)S(1)} %get-tuple-element.43.operator_ref, f32[2,112]{1,0:T(2,128)S(1)} %get-tuple-element.58.sums_in_ref, f32[232,112]{1,0:T(8,128)S(1)} %get-tuple-element.67.refs_0_, ...), custom_call_target="tpu_custom_call" | custom-call | bytes 3658368 | tf_op jit(solution)/shard_map/second/pallas_call | solution.py:292
  50.4 11.1 %all_to_all.5.sums_ref = f32[32,8,112]{2,1,0:T(8,128)S(1)} all-to-all(f32[32,8,112]{2,1,0:T(8,128)S(1)} %get-tuple-element.75), channel_id=1, replica_groups=mesh['row'=8,'col'=4] {'col','row'}, dimensions={0} | all-to-all | bytes 229376 | tf_op jit(solution)/shard_map/all_to_all | solution.py:389
  61.5 1.2 %last.1 = f32[112,4,224]{2,1,0:T(4,128)} custom-call(f32[32,8,112]{2,1,0:T(8,128)S(1)} %all_to_all.5.sums_ref, f32[4,112,224]{2,1,0:T(8,128)S(1)} %columns.1.refs_16_.first_ref, f32[4,112,224]{2,1,0:T(8,128)S(1)} %get-tuple-element.76.second_ref), custom_call_target="tpu_custom_call" | custom-call | bytes 917504 | tf_op jit(solution)/shard_map/last/pallas_call | solution.py:292
  (9 shorter events, 0.0 us)
Async XLA Ops:
  1.4 7.9 %collective-permute-start = (f32[224,112]{1,0:T(8,128)S(1)}, f32[224,112]{1,0:T(8,128)S(1)}, u32[]{:S(2)}, u32[]{:S(2)}) collective-permute-start(f32[224,112]{1,0:T(8,128)S(1)} %get-tuple-element.44.refs_0_), channel_id=1, source_target_pairs={{0,4},{1,2},{2,1},{3,7},{4,0},{5,6},{6,5},{7,3},{8,12},{9,10},{10,... | collective-permute-start | bytes 301064 | tf_op jit(solution)/shard_map/ppermute | solution.py:318
  1.9 9.3 %collective-permute-start.1 = (f32[224,112]{1,0:T(8,128)S(1)}, f32[224,112]{1,0:T(8,128)S(1)}, u32[]{:S(2)}, u32[]{:S(2)}) collective-permute-start(f32[224,112]{1,0:T(8,128)S(1)} %get-tuple-element.45.refs_1_), channel_id=1, source_target_pairs={{0,1},{1,0},{2,3},{3,2},{4,5},{5,4},{6,7},{7,6},{8,9},{9,8},{10,11... | collective-permute-start | bytes 301064 | tf_op jit(solution)/shard_map/ppermute | solution.py:318
  5.9 5.3 %collective-permute-start.2 = (f32[224,112]{1,0:T(8,128)S(1)}, f32[224,112]{1,0:T(8,128)S(1)}, u32[]{:S(2)}, u32[]{:S(2)}) collective-permute-start(f32[224,112]{1,0:T(8,128)S(1)} %get-tuple-element.46.refs_2_), channel_id=1, source_target_pairs={{0,1},{1,3},{2,0},{3,2},{4,8},{5,9},{6,10},{7,11},{8,4},{9,5},{10,... | collective-permute-start | bytes 301064 | tf_op jit(solution)/shard_map/ppermute | solution.py:318
  5.9 5.3 %collective-permute-start.3 = (f32[224,112]{1,0:T(8,128)S(1)}, f32[224,112]{1,0:T(8,128)S(1)}, u32[]{:S(2)}, u32[]{:S(2)}) collective-permute-start(f32[224,112]{1,0:T(8,128)S(1)} %get-tuple-element.41.after_ref.refs_3_), channel_id=1, source_target_pairs={{0,4},{1,5},{2,6},{3,7},{4,0},{5,1},{6,2},{7,3},{8,12},{9,13},{10,... | collective-permute-start | bytes 301064 | tf_op jit(solution)/shard_map/ppermute | solution.py:318
  11.5 5.6 %collective-permute-start.6 = (f32[128,112]{1,0:T(8,128)S(1)}, f32[128,112]{1,0:T(8,128)S(1)}, u32[]{:S(2)}, u32[]{:S(2)}) collective-permute-start(f32[128,112]{1,0:T(8,128)S(1)} %first_coeffs.1.refs_0_), channel_id=1, source_target_pairs={{0,3},{1,2},{2,1},{3,0},{4,7},{5,6},{6,5},{7,4},{8,11},{9,10},{10,... | collective-permute-start | bytes 172040 | tf_op jit(solution)/shard_map/ppermute | solution.py:322
  13.0 4.7 %collective-permute-start.5 = (f32[128,112]{1,0:T(8,128)S(1)}, f32[128,112]{1,0:T(8,128)S(1)}, u32[]{:S(2)}, u32[]{:S(2)}) collective-permute-start(f32[128,112]{1,0:T(8,128)S(1)} %first_coeffs.1.refs_0_), channel_id=1, source_target_pairs={{0,2},{1,3},{2,0},{3,1},{4,6},{5,7},{6,4},{7,5},{8,10},{9,11},{10,... | collective-permute-start | bytes 172040 | tf_op jit(solution)/shard_map/ppermute | solution.py:322
  13.8 4.3 %collective-permute-start.4 = (f32[128,112]{1,0:T(8,128)S(1)}, f32[128,112]{1,0:T(8,128)S(1)}, u32[]{:S(2)}, u32[]{:S(2)}) collective-permute-start(f32[128,112]{1,0:T(8,128)S(1)} %first_coeffs.1.refs_0_), channel_id=1, source_target_pairs={{0,1},{1,0},{2,3},{3,2},{4,5},{5,4},{6,7},{7,6},{8,9},{9,8},{10,11... | collective-permute-start | bytes 172040 | tf_op jit(solution)/shard_map/ppermute | solution.py:322
  18.5 4.6 %collective-permute-start.7 = (f32[224,112]{1,0:T(8,128)S(1)}, f32[224,112]{1,0:T(8,128)S(1)}, u32[]{:S(2)}, u32[]{:S(2)}) collective-permute-start(f32[224,112]{1,0:T(8,128)S(1)} %get-tuple-element.50.refs_8_), channel_id=1, source_target_pairs={{0,4},{1,2},{2,1},{3,7},{4,0},{5,6},{6,5},{7,3},{8,12},{9,10},{10,... | collective-permute-start | bytes 301064 | tf_op jit(solution)/shard_map/ppermute | solution.py:318
  18.6 6.8 %collective-permute-start.8 = (f32[224,112]{1,0:T(8,128)S(1)}, f32[224,112]{1,0:T(8,128)S(1)}, u32[]{:S(2)}, u32[]{:S(2)}) collective-permute-start(f32[224,112]{1,0:T(8,128)S(1)} %get-tuple-element.51.refs_9_), channel_id=1, source_target_pairs={{0,1},{1,0},{2,3},{3,2},{4,5},{5,4},{6,7},{7,6},{8,9},{9,8},{10,11... | collective-permute-start | bytes 301064 | tf_op jit(solution)/shard_map/ppermute | solution.py:318
  21.4 4.8 %collective-permute-start.9 = (f32[224,112]{1,0:T(8,128)S(1)}, f32[224,112]{1,0:T(8,128)S(1)}, u32[]{:S(2)}, u32[]{:S(2)}) collective-permute-start(f32[224,112]{1,0:T(8,128)S(1)} %get-tuple-element.52.refs_10_), channel_id=1, source_target_pairs={{0,1},{1,3},{2,0},{3,2},{4,8},{5,9},{6,10},{7,11},{8,4},{9,5},{10,... | collective-permute-start | bytes 301064 | tf_op jit(solution)/shard_map/ppermute | solution.py:318
  21.4 4.8 %collective-permute-start.10 = (f32[224,112]{1,0:T(8,128)S(1)}, f32[224,112]{1,0:T(8,128)S(1)}, u32[]{:S(2)}, u32[]{:S(2)}) collective-permute-start(f32[224,112]{1,0:T(8,128)S(1)} %get-tuple-element.53.refs_11_), channel_id=1, source_target_pairs={{0,4},{1,5},{2,6},{3,7},{4,0},{5,1},{6,2},{7,3},{8,12},{9,13},{10,... | collective-permute-start | bytes 301064 | tf_op jit(solution)/shard_map/ppermute | solution.py:318
  26.9 3.2 %collective-permute-start.11 = (f32[232,112]{1,0:T(8,128)S(1)}, f32[232,112]{1,0:T(8,128)S(1)}, u32[]{:S(2)}, u32[]{:S(2)}) collective-permute-start(f32[232,112]{1,0:T(8,128)S(1)} %get-tuple-element.59.refs_0_.refs_8_), channel_id=1, source_target_pairs={{0,4},{1,2},{2,1},{3,7},{4,0},{5,6},{6,5},{7,3},{8,12},{9,10},{10,... | collective-permute-start | bytes 311816 | tf_op jit(solution)/shard_map/ppermute | solution.py:318
  27.0 6.9 %collective-permute-start.12 = (f32[232,112]{1,0:T(8,128)S(1)}, f32[232,112]{1,0:T(8,128)S(1)}, u32[]{:S(2)}, u32[]{:S(2)}) collective-permute-start(f32[232,112]{1,0:T(8,128)S(1)} %get-tuple-element.60.refs_1_.refs_9_), channel_id=1, source_target_pairs={{0,1},{1,0},{2,3},{3,2},{4,5},{5,4},{6,7},{7,6},{8,9},{9,8},{10,11... | collective-permute-start | bytes 311816 | tf_op jit(solution)/shard_map/ppermute | solution.py:318
  29.7 4.8 %collective-permute-start.13 = (f32[232,112]{1,0:T(8,128)S(1)}, f32[232,112]{1,0:T(8,128)S(1)}, u32[]{:S(2)}, u32[]{:S(2)}) collective-permute-start(f32[232,112]{1,0:T(8,128)S(1)} %get-tuple-element.61.refs_2_.refs_10_), channel_id=1, source_target_pairs={{0,1},{1,3},{2,0},{3,2},{4,8},{5,9},{6,10},{7,11},{8,4},{9,5},{10,... | collective-permute-start | bytes 311816 | tf_op jit(solution)/shard_map/ppermute | solution.py:318
  29.7 4.8 %collective-permute-start.14 = (f32[232,112]{1,0:T(8,128)S(1)}, f32[232,112]{1,0:T(8,128)S(1)}, u32[]{:S(2)}, u32[]{:S(2)}) collective-permute-start(f32[232,112]{1,0:T(8,128)S(1)} %get-tuple-element.62.refs_3_.refs_11_), channel_id=1, source_target_pairs={{0,4},{1,5},{2,6},{3,7},{4,0},{5,1},{6,2},{7,3},{8,12},{9,13},{10,... | collective-permute-start | bytes 311816 | tf_op jit(solution)/shard_map/ppermute | solution.py:318
  34.9 5.3 %collective-permute-start.17 = (f32[136,112]{1,0:T(8,128)S(1)}, f32[136,112]{1,0:T(8,128)S(1)}, u32[]{:S(2)}, u32[]{:S(2)}) collective-permute-start(f32[136,112]{1,0:T(8,128)S(1)} %second_coeffs.1.refs_0_), channel_id=1, source_target_pairs={{0,3},{1,2},{2,1},{3,0},{4,7},{5,6},{6,5},{7,4},{8,11},{9,10},{10,... | collective-permute-start | bytes 182792 | tf_op jit(solution)/shard_map/ppermute | solution.py:322
  36.4 4.5 %collective-permute-start.16 = (f32[136,112]{1,0:T(8,128)S(1)}, f32[136,112]{1,0:T(8,128)S(1)}, u32[]{:S(2)}, u32[]{:S(2)}) collective-permute-start(f32[136,112]{1,0:T(8,128)S(1)} %second_coeffs.1.refs_0_), channel_id=1, source_target_pairs={{0,2},{1,3},{2,0},{3,1},{4,6},{5,7},{6,4},{7,5},{8,10},{9,11},{10,... | collective-permute-start | bytes 182792 | tf_op jit(solution)/shard_map/ppermute | solution.py:322
  37.7 4.3 %collective-permute-start.15 = (f32[136,112]{1,0:T(8,128)S(1)}, f32[136,112]{1,0:T(8,128)S(1)}, u32[]{:S(2)}, u32[]{:S(2)}) collective-permute-start(f32[136,112]{1,0:T(8,128)S(1)} %second_coeffs.1.refs_0_), channel_id=1, source_target_pairs={{0,1},{1,0},{2,3},{3,2},{4,5},{5,4},{6,7},{7,6},{8,9},{9,8},{10,11... | collective-permute-start | bytes 182792 | tf_op jit(solution)/shard_map/ppermute | solution.py:322
  42.5 3.5 %collective-permute-start.18 = (f32[232,112]{1,0:T(8,128)S(1)}, f32[232,112]{1,0:T(8,128)S(1)}, u32[]{:S(2)}, u32[]{:S(2)}) collective-permute-start(f32[232,112]{1,0:T(8,128)S(1)} %get-tuple-element.63.refs_8_), channel_id=1, source_target_pairs={{0,4},{1,2},{2,1},{3,7},{4,0},{5,6},{6,5},{7,3},{8,12},{9,10},{10,... | collective-permute-start | bytes 311816 | tf_op jit(solution)/shard_map/ppermute | solution.py:318
  42.6 6.9 %collective-permute-start.19 = (f32[232,112]{1,0:T(8,128)S(1)}, f32[232,112]{1,0:T(8,128)S(1)}, u32[]{:S(2)}, u32[]{:S(2)}) collective-permute-start(f32[232,112]{1,0:T(8,128)S(1)} %get-tuple-element.64.refs_9_), channel_id=1, source_target_pairs={{0,1},{1,0},{2,3},{3,2},{4,5},{5,4},{6,7},{7,6},{8,9},{9,8},{10,11... | collective-permute-start | bytes 311816 | tf_op jit(solution)/shard_map/ppermute | solution.py:318
  44.8 4.8 %collective-permute-start.20 = (f32[232,112]{1,0:T(8,128)S(1)}, f32[232,112]{1,0:T(8,128)S(1)}, u32[]{:S(2)}, u32[]{:S(2)}) collective-permute-start(f32[232,112]{1,0:T(8,128)S(1)} %get-tuple-element.65.refs_10_), channel_id=1, source_target_pairs={{0,1},{1,3},{2,0},{3,2},{4,8},{5,9},{6,10},{7,11},{8,4},{9,5},{10,... | collective-permute-start | bytes 311816 | tf_op jit(solution)/shard_map/ppermute | solution.py:318
  44.8 4.8 %collective-permute-start.21 = (f32[232,112]{1,0:T(8,128)S(1)}, f32[232,112]{1,0:T(8,128)S(1)}, u32[]{:S(2)}, u32[]{:S(2)}) collective-permute-start(f32[232,112]{1,0:T(8,128)S(1)} %get-tuple-element.66.refs_11_), channel_id=1, source_target_pairs={{0,4},{1,5},{2,6},{3,7},{4,0},{5,1},{6,2},{7,3},{8,12},{9,13},{10,... | collective-permute-start | bytes 311816 | tf_op jit(solution)/shard_map/ppermute | solution.py:318
